TPU v7x, 128 devices: a whole 4x4x4 slice. The times are simulated.
128 devices in a mesh: dp: 16 (over x_lo, z, core), seq: 8 (over x_hi, y).
Axes of the slice: x: 4 (x_hi: 2, x_lo: 2; x = x_hi * 2 + x_lo), y: 4, z: 4, core: 2. Of those that a mesh axis runs over, the one named last changes fastest.
Arguments:
- video: bfloat16 [16, 8, 256, 1152], P('dp', 'seq'), may hold values from -6 to 6
- out_grad: bfloat16 [16, 8, 256, 1152], P('dp', 'seq'), may hold values from -6 to 6
- gain_spatial: float32 [1152], replicated, may hold values from 0.1 to 1.9
- gain_temporal: float32 [1152], replicated, may hold values from 0.1 to 1.9
- w_spatial_qkv: bfloat16 [1152, 3456], replicated, may hold values from -4 to 4
- w_spatial_out: bfloat16 [1152, 1152], replicated, may hold values from -0.1875 to 0.1875
- w_temporal_qkv: bfloat16 [1152, 3456], replicated, may hold values from -4 to 4
- w_temporal_out: bfloat16 [1152, 1152], replicated, may hold values from -0.1875 to 0.1875
Outputs:
- video_grad: bfloat16 [16, 8, 256, 1152], P('dp', 'seq')
- w_grad: float32 [1152, 1152], P(('dp', 'seq'))
All inputs are finite; a program needn't handle non-finite values.
Results may differ from a plain program's by a relative error of at most 0.018.
Values may be sent and summed in bfloat16 or wider, within the bound.
No kernel may reach another device: no remote copies, remote signals or barrier semaphores. Data moves between devices by JAX's collectives and lax.ppermute only.
A program may use at most 128 MiB of HBM per device.

v0:
```python
import math

import jax
import jax.numpy as jnp
from jax import lax
from jax.sharding import PartitionSpec as P

HEADS = 16


epsilon = 1e-06


def layer_norm(stream, gain_vec):
    center = jnp.mean(stream, axis=-1, keepdims=True)
    centered = stream - center
    spread = jnp.mean(centered * centered, axis=-1, keepdims=True)
    return (centered * lax.rsqrt(spread + epsilon) * gain_vec).astype(jnp.bfloat16)


def project(hidden, weight):
    return jnp.dot(hidden, weight, preferred_element_type=jnp.float32)


def split_heads(block):
    shape = block.shape[:-1] + (HEADS, block.shape[-1] // HEADS)
    return block.reshape(shape).astype(jnp.float32)


def spatial_mix(qkv):
    width = qkv.shape[-1] // 3
    query_part = split_heads(qkv[..., :width])
    key_part = split_heads(qkv[..., width : 2 * width])
    value_part = split_heads(qkv[..., 2 * width :])
    scale = 1.0 / math.sqrt(width // HEADS)
    scores = (
        jnp.einsum("bfqhd,bfkhd->bfhqk", query_part, key_part, precision=lax.Precision.HIGHEST)
        * scale
    )
    weights = jax.nn.softmax(scores, axis=-1)
    mixed = jnp.einsum("bfhqk,bfkhd->bfqhd", weights, value_part, precision=lax.Precision.HIGHEST)
    return mixed.reshape(qkv.shape[:-1] + (width,)).astype(jnp.bfloat16)


def temporal_mix(qkv):
    width = qkv.shape[-1] // 3
    query_part = split_heads(qkv[..., :width])
    key_part = split_heads(qkv[..., width : 2 * width])
    value_part = split_heads(qkv[..., 2 * width :])
    scale = 1.0 / math.sqrt(width // HEADS)
    scores = (
        jnp.einsum("bqphd,bkphd->bphqk", query_part, key_part, precision=lax.Precision.HIGHEST)
        * scale
    )
    weights = jax.nn.softmax(scores, axis=-1)
    mixed = jnp.einsum("bphqk,bkphd->bqphd", weights, value_part, precision=lax.Precision.HIGHEST)
    return mixed.reshape(qkv.shape[:-1] + (width,)).astype(jnp.bfloat16)


def spatial_section(clip, gain_vec, w_qkv, w_out):
    hidden = layer_norm(clip.astype(jnp.float32), gain_vec)
    qkv = project(hidden, w_qkv).astype(jnp.bfloat16)
    return clip.astype(jnp.float32) + project(spatial_mix(qkv), w_out)


def token_outer(mixed, grad_rows):
    width = mixed.shape[-1]
    return lax.dot_general(
        mixed.reshape(-1, width),
        grad_rows.reshape(-1, width),
        (((0,), (0,)), ((), ())),
        preferred_element_type=jnp.float32,
    )


def per_device(
    video,
    out_grad,
    gain_spatial,
    gain_temporal,
    w_spatial_qkv,
    w_spatial_out,
    w_temporal_qkv,
    w_temporal_out,
):
    token_total = (
        lax.axis_size("dp")
        * lax.axis_size("seq")
        * video.shape[0]
        * video.shape[1]
        * video.shape[2]
    )
    stream, spatial_back = jax.vjp(
        lambda clip_in: spatial_section(clip_in, gain_spatial, w_spatial_qkv, w_spatial_out), video
    )
    grad_float = out_grad.astype(jnp.float32)
    qkv, pre_back = jax.vjp(
        lambda stream_in: project(layer_norm(stream_in, gain_temporal), w_temporal_qkv).astype(
            jnp.bfloat16
        ),
        stream,
    )
    moved_qkv = lax.all_to_all(qkv, "seq", split_axis=2, concat_axis=1, tiled=True)
    mixed_pos, mix_back = jax.vjp(temporal_mix, moved_qkv)
    mixed = lax.all_to_all(mixed_pos, "seq", split_axis=1, concat_axis=2, tiled=True)
    local_sum = token_outer(mixed, out_grad)
    unused, out_back = jax.vjp(lambda mixed_in: project(mixed_in, w_temporal_out), mixed)
    mixed_grad = out_back(grad_float)[0]
    mixed_grad_pos = lax.all_to_all(mixed_grad, "seq", split_axis=2, concat_axis=1, tiled=True)
    qkv_grad_pos = mix_back(mixed_grad_pos)[0]
    qkv_grad = lax.all_to_all(qkv_grad_pos, "seq", split_axis=1, concat_axis=2, tiled=True)
    stream_grad = grad_float + pre_back(qkv_grad)[0]
    video_grad = spatial_back(stream_grad)[0]
    local_sum = local_sum / math.sqrt(float(token_total))
    w_grad = lax.psum_scatter(local_sum, ("dp", "seq"), scatter_dimension=0, tiled=True)
    return (video_grad, w_grad)


def solution(mesh):
    return jax.shard_map(
        per_device,
        mesh=mesh,
        in_specs=(
            P("dp", "seq", None, None),
            P("dp", "seq", None, None),
            P(),
            P(),
            P(),
            P(),
            P(),
            P(),
        ),
        out_specs=(P("dp", "seq", None, None), P(("dp", "seq"), None)),
        check_vma=False,
    )
```

profile of v0, /device:TPU:1, one launch (start us, length us, event | category | flops | bytes accessed | tf_op | source)
XLA Modules:
  0.0 361.7 jit_solution(15675530483380894013)
XLA Ops:
  7.2 3.1 fusion.7
  12.8 6.0 %reduce.23 = bf16[256,1152]{1,0:T(8,128)(2,1)} reduce(bf16[256,1,1,1152]{3,2,1,0:T(2,128)(2,1)} %bitcast.153, bf16[]{:T(256)} %broadcast.212), dimensions={1,2}, to_apply=%bitcast.145.reduce_sub_computation | reduce | bytes 1179650
  21.4 7.7 %all-to-all-start = ((bf16[8,2,18432]{2,1,0:T(2,128)(2,1)}), bf16[8,2,18432]{2,1,0:T(2,128)(2,1)}, u32[]{:S(2)}, u32[]{:S(2)}) async-start(bf16[8,2,18432]{2,1,0:T(2,128)(2,1)} %reshape.406), calls=%async_computation | async-start | bytes 1179648 | tf_op jit(solution)/shard_map/all_to_all | solution.py:109
  29.7 5.9 %fusion = bf16[1,1,256,3456]{3,2,1,0:T(8,128)(2,1)S(1)} fusion(bf16[1152,3456]{1,0:T(8,128)(2,1)} %param.12, bf16[1,1,256,1152]{3,2,1,0:T(8,128)(2,1)S(1)} %copy-done.4, f32[1152]{0:T(1024)S(1)} %copy-done.26, f32[256]{0:T(256)S(1)} %fusion.57, f32[256]{0:T(256)S(1)} %broadcast_multiply_fusion.1), kind=kOutput, calls=%fused_computation.3 | convolution fusion | flops 2040791040 | bytes 10328576 | tf_op jit(solution)/shard_map/jvp()/dot_general | solution.py:22
  54.7 5.0 %copy.131 = bf16[1,1,256,3456]{3,1,0,2:T(2,128)(2,1)} copy(bf16[1,1,256,3456]{3,2,1,0:T(8,128)(2,1)S(1)} %fusion.1) | data formatting | bytes 3538944 | tf_op jit(solution)/shard_map/jvp()/convert_element_type | solution.py:98
  59.7 13.1 %reduce.22 = bf16[256,3456]{1,0:T(8,128)(2,1)} reduce(bf16[256,1,1,3456]{3,2,1,0:T(2,128)(2,1)} %bitcast.146, bf16[]{:T(256)} %broadcast.212), dimensions={1,2}, to_apply=%bitcast.144.reduce_sub_computation | reduce | bytes 3538946
  72.8 5.7 %reshape.404 = bf16[8,2,55296]{2,1,0:T(2,128)(2,1)} reshape(bf16[256,3456]{1,0:T(8,128)(2,1)} %reduce.22) | data formatting | bytes 3538944
  78.5 6.6 %all-to-all-start.1 = ((bf16[8,2,55296]{2,1,0:T(2,128)(2,1)}), bf16[8,2,55296]{2,1,0:T(2,128)(2,1)}, u32[]{:S(2)}, u32[]{:S(2)}) async-start(bf16[8,2,55296]{2,1,0:T(2,128)(2,1)} %reshape.404), calls=%async_computation.1 | async-start | bytes 3538944 | tf_op jit(solution)/shard_map/all_to_all | solution.py:103
  85.2 3.5 reshape.407
  88.7 5.5 %bitcast_reduce_fusion = bf16[256,1152]{1,0:T(8,128)(2,1)} fusion(bf16[256,1,1,1152]{3,2,1,0:T(2,128)(2,1)} %reshape.407), kind=kLoop, calls=%fused_computation.115 | loop fusion | bytes 1179648 | tf_op jit(solution)/shard_map/all_to_all | solution.py:109
  94.2 3.7 %reshape.381 = bf16[1,8,32,16,72]{4,3,2,1,0:T(8,128)(2,1)} reshape(bf16[256,1152]{1,0:T(8,128)(2,1)} %bitcast_reduce_fusion) | data formatting | bytes 1179648 | tf_op jit(solution)/shard_map/transpose(jvp())/reshape | solution.py:57
  97.9 9.9 %all-to-all-done.1 = bf16[8,2,55296]{2,1,0:T(2,128)(2,1)} async-done(((bf16[8,2,55296]{2,1,0:T(2,128)(2,1)}), bf16[8,2,55296]{2,1,0:T(2,128)(2,1)}, u32[]{:S(2)}, u32[]{:S(2)}) %all-to-all-start.1) | async-done | bytes 1769504 | tf_op jit(solution)/shard_map/all_to_all | solution.py:103
  107.9 6.5 %reshape.405 = bf16[256,1,1,3456]{3,2,1,0:T(2,128)(2,1)} reshape(bf16[8,2,55296]{2,1,0:T(2,128)(2,1)} %all-to-all-done.1) | data formatting | bytes 3538944
  117.9 3.7 %reshape.388 = bf16[8,32,16,72]{3,2,1,0:T(8,128)(2,1)} reshape(bf16[1,8,32,1152]{3,2,1,0:T(8,128)(2,1)} %get-tuple-element.4) | data formatting | bytes 1179648 | tf_op jit(solution)/shard_map/reshape.54
  121.6 3.7 %reshape.391 = bf16[8,32,16,72]{3,2,1,0:T(8,128)(2,1)} reshape(bf16[1,8,32,1152]{3,2,1,0:T(8,128)(2,1)} %get-tuple-element.5) | data formatting | bytes 1179648 | tf_op jit(solution)/shard_map/reshape.63
  125.3 3.9 %reshape.389 = bf16[8,32,16,72]{3,2,1,0:T(8,128)(2,1)} reshape(bf16[1,8,32,1152]{3,2,1,0:T(8,128)(2,1)} %get-tuple-element.6) | data formatting | bytes 1179648 | tf_op jit(solution)/shard_map/reshape.55
  129.2 3.2 multiply_reduce_fusion.3
  139.6 4.1 %fusion.21 = bf16[1,8,32,16,72]{4,1,3,2,0:T(8,128)(2,1)} fusion(bf16[8,32,16,72]{3,2,1,0:T(8,128)(2,1)S(1)} %copy-done.13, f32[32,16,8,8]{2,3,1,0:T(8,128)S(1)} %get-tuple-element.17, f32[32,16,8]{2,1,0:T(8,128)S(1)} %neg.20, f32[32,16,8]{2,1,0:T(8,128)S(1)} %fusion.56, f32[32,16,8]{2,1,0:T(8,128)S(1)} %get-tuple-element.14, ...), kind=kOutput, calls=%fused_computation.47 | convolution fusion | flops 28803072 | bytes 1490944 | tf_op jit(solution)/shard_map/transpose(jvp(bqphd,bkphd->bphqk))/dot_general | solution.py:52
  143.7 3.8 %fusion.20 = bf16[1,8,32,16,72]{4,1,3,2,0:T(8,128)(2,1)} fusion(bf16[8,32,16,72]{3,2,1,0:T(8,128)(2,1)S(1)} %copy-done.12, f32[32,16,8,8]{2,3,1,0:T(8,128)S(1)} %get-tuple-element.17, f32[32,16,8]{2,1,0:T(8,128)S(1)} %neg.20, f32[32,16,8]{2,1,0:T(8,128)S(1)} %fusion.56, f32[32,16,8]{2,1,0:T(8,128)S(1)} %get-tuple-element.14, ...), kind=kOutput, calls=%fused_computation.46 | convolution fusion | flops 28803072 | bytes 1490944 | tf_op jit(solution)/shard_map/transpose(jvp(bqphd,bkphd->bphqk))/dot_general | solution.py:52
  148.6 2.9 convert_element_type.198
  151.6 5.6 %all-to-all-start.3 = ((bf16[1,8,32,1152]{3,2,0,1:T(8,128)(2,1)}), bf16[1,8,32,1152]{3,2,0,1:T(8,128)(2,1)}, u32[]{:S(2)}, u32[]{:S(2)}) async-start(bf16[1,8,32,1152]{3,2,0,1:T(8,128)(2,1)} %bitcast.158), calls=%async_computation.3 | async-start | bytes 1179648 | tf_op jit(solution)/shard_map/all_to_all | solution.py:105
  157.1 4.6 %fusion.19 = bf16[1,8,32,16,72]{4,1,3,2,0:T(8,128)(2,1)S(1)} fusion(bf16[1,8,32,16,72]{4,3,2,1,0:T(8,128)(2,1)} %reshape.381, f32[32,16,8]{2,1,0:T(8,128)} %copy-done.19, f32[32,16,8,8]{2,3,1,0:T(8,128)} %copy-done.3, f32[32,16,8]{2,1,0:T(8,128)S(1)} %get-tuple-element.14), kind=kOutput, calls=%fused_computation.45 | convolution fusion | flops 28704768 | bytes 1343488 | tf_op jit(solution)/shard_map/transpose(jvp(bphqk,bkphd->bqphd))/dot_general | solution.py:56
  162.9 2.9 reshape.390
  168.1 2.9 reshape.392
  173.4 2.9 reshape.393
  179.1 6.6 %all-to-all-start.2 = ((bf16[1,8,32,3456]{3,2,0,1:T(8,128)(2,1)}), bf16[1,8,32,3456]{3,2,0,1:T(8,128)(2,1)}, u32[]{:S(2)}, u32[]{:S(2)}) async-start(bf16[1,8,32,3456]{3,2,0,1:T(8,128)(2,1)} %add_bitcast_fusion), calls=%async_computation.2 | async-start | bytes 3538944 | tf_op jit(solution)/shard_map/all_to_all | solution.py:111
  186.2 4.6 %convolution_multiply_fusion = f32[1152,1152]{1,0:T(8,128)} fusion(bf16[256,1152]{1,0:T(8,128)(2,1)} %bitcast.47, bf16[1,1,256,1152]{3,2,1,0:T(8,128)(2,1)} %param.9), kind=kOutput, calls=%fused_computation | convolution fusion | flops 680804352 | bytes 6488064 | tf_op jit(solution)/shard_map/dot_general | solution.py:68
  190.8 18.2 %all-to-all-done.2 = bf16[1,8,32,3456]{3,2,0,1:T(8,128)(2,1)} async-done(((bf16[1,8,32,3456]{3,2,0,1:T(8,128)(2,1)}), bf16[1,8,32,3456]{3,2,0,1:T(8,128)(2,1)}, u32[]{:S(2)}, u32[]{:S(2)}) %all-to-all-start.2) | async-done | bytes 1769504 | tf_op jit(solution)/shard_map/all_to_all | solution.py:111
  209.1 6.8 %fusion.28 = (f32[256]{0:T(256)S(1)}, f32[256,1152]{1,0:T(8,128)S(1)}) fusion(f32[1,1,256,1152]{3,2,1,0:T(8,128)} %copy-done.7, f32[256]{0:T(256)S(1)} %copy-done.21, f32[1152]{0:T(1024)S(1)} %copy-done.25, bf16[256,3456]{1,0:T(8,128)(2,1)} %bitcast.23, bf16[1152,3456]{1,0:T(8,128)(2,1)} %param.14), kind=kOutput, calls=%fused_computation.59 | convolution fusion | flops 2040200960 | bytes 12098048 | tf_op jit(solution)/shard_map/transpose(jvp())/dot_general | solution.py:22
  221.4 4.1 %multiply_reduce_fusion = (f32[16,256]{1,0:T(8,128)S(1)}, f32[16,256,256]{1,2,0:T(8,128)S(1)}) fusion(f32[16,256]{1,0:T(8,128)S(1)} %multiply_divide_fusion.1, f32[16,256]{1,0:T(8,128)S(1)} %get-tuple-element.10, f32[16,256,256]{1,2,0:T(8,128)} %copy-done.1, bf16[16,72,256]{2,1,0:T(8,128)(2,1)} %bitcast.156, bf16[256,16,72]{0,2,1:T(8,128)(2,1)} %bitcast.154), kind=kOutput, calls=%fused_computation.6 | convolution fusion | flops 156233728 | bytes 9617408 | tf_op jit(solution)/shard_map/transpose(jvp(bfhqk,bfkhd->bfqhd))/dot_general | solution.py:41
  230.8 3.1 convolution_convert_fusion.12
  239.5 113.6 %all-reduce.9.cloned.1.call-done = f32[1152,1152]{1,0:T(8,128)} async-done(((f32[1152,1152]{1,0:T(8,128)}), f32[1152,1152]{1,0:T(8,128)}) %all-reduce.9.cloned.1.call-update) | async-done | bytes 5308432
  (117 shorter events, 63.3 us)
Async XLA Ops:
  7.2 42.6 %copy-start = (bf16[1152,1152]{1,0:T(8,128)(2,1)S(1)}, bf16[1152,1152]{1,0:T(8,128)(2,1)}, u32[]{:S(2)}) copy-start(bf16[1152,1152]{1,0:T(8,128)(2,1)} %param.13) | copy-start | bytes 7962628
  12.2 17.0 %copy-start.4 = (bf16[1,1,256,1152]{3,2,1,0:T(8,128)(2,1)S(1)}, bf16[1,1,256,1152]{3,2,1,0:T(8,128)(2,1)}, u32[]{:S(2)}) copy-start(bf16[1,1,256,1152]{3,2,1,0:T(8,128)(2,1)} %param.8) | copy-start | bytes 1769476
  18.9 10.8 %copy-start.26 = (f32[1152]{0:T(1024)S(1)}, f32[1152]{0:T(1024)}, u32[]{:S(2)}) copy-start(f32[1152]{0:T(1024)} %param.10) | copy-start | bytes 13828
  21.4 57.1 %all-to-all-start = ((bf16[8,2,18432]{2,1,0:T(2,128)(2,1)}), bf16[8,2,18432]{2,1,0:T(2,128)(2,1)}, u32[]{:S(2)}, u32[]{:S(2)}) async-start(bf16[8,2,18432]{2,1,0:T(2,128)(2,1)} %reshape.406), calls=%async_computation | async-start | bytes 1179648 | tf_op jit(solution)/shard_map/all_to_all | solution.py:109
  45.3 2.1 copy-start.1
  45.3 2.1 copy-start.15
  45.3 6.7 %slice-start = ((s8[7962624]{0:T(1024)(128)(4,1)}), s8[4194304]{0:T(1024)(128)(4,1)S(1)}, s32[]{:S(2)}) async-start(s8[7962624]{0:T(1024)(128)(4,1)} %bitcast.161), calls=%async_computation.5 | async-start | bytes 8388608
  47.4 4.6 %slice-start.1 = ((s8[7962624]{0:T(1024)(128)(4,1)}), s8[3768320]{0:T(1024)(128)(4,1)S(1)}, s32[]{:S(2)}) async-start(s8[7962624]{0:T(1024)(128)(4,1)} %bitcast.161), calls=%async_computation.6 | async-start | bytes 7536640
  49.8 2.2 copy-start.24
  51.0 3.7 %copy-start.20 = (f32[256]{0:T(256)}, f32[256]{0:T(256)S(1)}, u32[]{:S(2)}) copy-start(f32[256]{0:T(256)S(1)} %broadcast_multiply_fusion) | copy-start | bytes 3076
  52.0 2.7 copy-start.22
  78.5 29.3 %all-to-all-start.1 = ((bf16[8,2,55296]{2,1,0:T(2,128)(2,1)}), bf16[8,2,55296]{2,1,0:T(2,128)(2,1)}, u32[]{:S(2)}, u32[]{:S(2)}) async-start(bf16[8,2,55296]{2,1,0:T(2,128)(2,1)} %reshape.404), calls=%async_computation.1 | async-start | bytes 3538944 | tf_op jit(solution)/shard_map/all_to_all | solution.py:103
  132.4 11.3 %copy-start.3 = (f32[32,16,8,8]{2,3,1,0:T(8,128)}, f32[32,16,8,8]{2,3,1,0:T(8,128)S(1)}, u32[]{:S(2)}) copy-start(f32[32,16,8,8]{2,3,1,0:T(8,128)S(1)} %get-tuple-element.15) | copy-start | bytes 393220
  132.4 2.0 copy-start.14
  133.4 10.3 %copy-start.19 = (f32[32,16,8]{2,1,0:T(8,128)}, f32[32,16,8]{2,1,0:T(8,128)S(1)}, u32[]{:S(2)}) copy-start(f32[32,16,8]{2,1,0:T(8,128)S(1)} %fusion.56) | copy-start | bytes 49156
  134.4 2.8 copy-start.11
  137.2 2.3 copy-start.13
  139.6 4.1 %copy-start.12 = (bf16[8,32,16,72]{3,2,1,0:T(8,128)(2,1)S(1)}, bf16[8,32,16,72]{3,2,1,0:T(8,128)(2,1)}, u32[]{:S(2)}) copy-start(bf16[8,32,16,72]{3,2,1,0:T(8,128)(2,1)} %reshape.388) | copy-start | bytes 1769476
  151.6 27.5 %all-to-all-start.3 = ((bf16[1,8,32,1152]{3,2,0,1:T(8,128)(2,1)}), bf16[1,8,32,1152]{3,2,0,1:T(8,128)(2,1)}, u32[]{:S(2)}, u32[]{:S(2)}) async-start(bf16[1,8,32,1152]{3,2,0,1:T(8,128)(2,1)} %bitcast.158), calls=%async_computation.3 | async-start | bytes 1179648 | tf_op jit(solution)/shard_map/all_to_all | solution.py:105
  179.1 30.0 %all-to-all-start.2 = ((bf16[1,8,32,3456]{3,2,0,1:T(8,128)(2,1)}), bf16[1,8,32,3456]{3,2,0,1:T(8,128)(2,1)}, u32[]{:S(2)}, u32[]{:S(2)}) async-start(bf16[1,8,32,3456]{3,2,0,1:T(8,128)(2,1)} %add_bitcast_fusion), calls=%async_computation.2 | async-start | bytes 3538944 | tf_op jit(solution)/shard_map/all_to_all | solution.py:111
  185.7 167.4 %all-reduce.9.cloned.1.call-start = ((), (), s32[]{:S(2)}) async-start(), calls=%async_computation.4 | async-start | bytes 10616832
  190.8 18.3 %copy-start.21 = (f32[256]{0:T(256)S(1)}, f32[256]{0:T(256)}, u32[]{:S(2)}) copy-start(f32[256]{0:T(256)} %copy-done.20) | copy-start | bytes 3076
  190.8 18.3 %copy-start.25 = (f32[1152]{0:T(1024)S(1)}, f32[1152]{0:T(1024)}, u32[]{:S(2)}) copy-start(f32[1152]{0:T(1024)} %param.11) | copy-start | bytes 13828
  209.0 6.8 %copy-start.8 = (f32[1,1,256,1152]{3,2,1,0:T(8,128)S(1)}, f32[1,1,256,1152]{3,2,1,0:T(8,128)}, u32[]{:S(2)}) copy-start(f32[1,1,256,1152]{3,2,1,0:T(8,128)} %copy-done.7) | copy-start | bytes 3538948
  209.0 6.8 %copy-start.23 = (f32[256]{0:T(256)S(1)}, f32[256]{0:T(256)}, u32[]{:S(2)}) copy-start(f32[256]{0:T(256)} %copy-done.22) | copy-start | bytes 3076
  215.8 1.5 copy-start.17
  221.4 4.1 %copy-start.2 = (f32[16,256,256]{1,2,0:T(8,128)S(1)}, f32[16,256,256]{1,2,0:T(8,128)}, u32[]{:S(2)}) copy-start(f32[16,256,256]{1,2,0:T(8,128)} %copy-done.1) | copy-start | bytes 12582916
  226.7 1.8 copy-start.6
  228.5 2.3 copy-start.16
  228.5 5.4 %slice-start.2 = ((s8[7962624]{0:T(1024)(128)(4,1)}), s8[3768320]{0:T(1024)(128)(4,1)S(1)}, s32[]{:S(2)}) async-start(s8[7962624]{0:T(1024)(128)(4,1)} %bitcast.163), calls=%async_computation.7 | async-start | bytes 7536640
  230.8 3.1 slice-start.3
  230.8 3.1 copy-start.27
  (5 other events, 6.0 us)
Sparse Core Ops, SparseCore 0:
  191.5 161.5 all-reduce.8
where the time goes:
time: 368 us; the launch traced here: 362 us
  waiting for transfers between devices  142 us (39%)
  local copies, waits for them, and re-layouts  84.9 us (23%)
  matrix products  65.4 us (18%)
  other arithmetic  27.8 us (8%)
  starting transfers between devices  27.1 us (7%)
  between operations  14.7 us (4%)
    unnamed x2, waiting for transfers between devices  114 us
    unnamed x71, local copies, waits for them, and re-layouts  27.9 us
    dot_general x7, matrix products, project(): return jnp.dot(hidden, weight, preferred_element_type=jnp.float32)  24.4 us
    unnamed x4, other arithmetic  19.1 us
    all_to_all x1, waiting for transfers between devices, per_device(): lax.all_to_all(qkv_grad_pos, 'seq', split_axis=1, concat_axis=2, tiled=True)  18.2 us
    another operation x3, local copies, waits for them, and re-layouts  11.3 us
    dot_general x3, matrix products, temporal_mix(): jnp.einsum('bqphd,bkphd->bphqk', query_part, key_part, precision=lax.Prec...  11.1 us
    all_to_all x1, waiting for transfers between devices, per_device(): lax.all_to_all(qkv, 'seq', split_axis=2, concat_axis=1, tiled=True)  9.94 us
  transfers between devices with their start and end apart: 5, of which 3 were waited for; matrix products, arithmetic and copies ran while one was open for 32% of the time, Pallas kernels for 0%

commit v1 on v0

v1 whole, which is shorter than its diff:
```python
import math

import jax
import jax.numpy as jnp
from jax import lax
from jax.experimental import pallas as pl
from jax.experimental.pallas import tpu as pltpu
from jax.sharding import PartitionSpec as P

HEADS = 16
D = 1152
HD = D // HEADS
T = 256
SEQ = 8
POS = T // SEQ
DP = 16
EPS = 1e-06
SCALE = 1.0 / math.sqrt(HD)
BF = jnp.bfloat16
F32 = jnp.float32
ROWS = 32
WIN = 256
CHUNK = 88
OWN = D // (DP * SEQ)
LANES = 128
TILES = D // LANES

VMEM = pltpu.VMEM
ANY = pl.ANY


def nn(a, b):
    return lax.dot_general(a, b, (((1,), (0,)), ((), ())), preferred_element_type=F32)


def nt(a, b):
    return lax.dot_general(a, b, (((1,), (1,)), ((), ())), preferred_element_type=F32)


def tn(a, b):
    return lax.dot_general(a, b, (((0,), (0,)), ((), ())), preferred_element_type=F32)


def row_stats(x):
    center = jnp.mean(x, axis=-1, keepdims=True)
    centered = x - center
    spread = jnp.mean(centered * centered, axis=-1, keepdims=True)
    return centered, lax.rsqrt(spread + EPS)


def row_blocks(fn):
    def body(i, carry):
        fn(pl.ds(pl.multiple_of(i * ROWS, ROWS), ROWS))
        return carry

    lax.fori_loop(0, T // ROWS, body, 0)


def norm_back(x, g, dy):
    centered, inv = row_stats(x)
    xhat = centered * inv
    dxhat = dy * g
    mean_d = jnp.mean(dxhat, axis=-1, keepdims=True)
    mean_dx = jnp.mean(dxhat * xhat, axis=-1, keepdims=True)
    return inv * (dxhat - mean_d - xhat * mean_dx)


def window(h):
    tile = jnp.minimum(lax.div(h * HD, LANES), TILES - 2)
    low = pl.multiple_of(tile * LANES, LANES)
    start = h * HD - low
    lane = lax.broadcasted_iota(jnp.int32, (1, WIN), 1)
    inside = jnp.where((lane >= start) & (lane < start + HD), 1.0, 0.0)
    return low, inside.astype(BF)


def softmax_keys(scores):
    top = jnp.max(scores, axis=0, keepdims=True)
    e = jnp.exp((scores - top) * SCALE)
    return e * (1.0 / jnp.sum(e, axis=0, keepdims=True))


def score_grad(prob, prob_grad):
    t = prob * prob_grad
    delta = jnp.sum(t, axis=0, keepdims=True)
    return ((t - prob * delta) * SCALE).astype(BF)


def heads_loop(fn, unroll=2):
    def body(i, carry):
        for u in range(unroll):
            fn(i * unroll + u)
        return carry

    lax.fori_loop(0, HEADS // unroll, body, 0)


def fetch(src, dst, sem):
    copy = pltpu.make_async_copy(src, dst, sem)
    copy.start()
    return copy


def fetch_columns(src, dst, sems):
    out = []
    for c in range(3):
        cols = slice(c * D, (c + 1) * D)
        out.append(fetch(src.at[:, cols], dst.at[:, cols], sems.at[c]))
    return out


def spatial_forward(video, gs, gt, wq_hbm, wo_hbm, hid_out, stream_out, qkv, prob,
                    wq, wo, hid, mix, sems):
    wq_copies = fetch_columns(wq_hbm, wq, sems)
    wo_copy = fetch(wo_hbm, wo, sems.at[3])

    def first_norm(rows):
        centered, inv = row_stats(video[rows, :].astype(F32))
        hid[rows, :] = (centered * inv * gs[...]).astype(BF)

    row_blocks(first_norm)
    for c in range(3):
        cols = slice(c * D, (c + 1) * D)
        wq_copies[c].wait()
        qkv[:, cols] = nn(hid[...], wq[:, cols]).astype(BF)
    mix[...] = jnp.zeros_like(mix)

    def head(h):
        low, inside = window(h)
        q = qkv[:, pl.ds(low, WIN)] * inside
        k = qkv[:, pl.ds(D + low, WIN)]
        v = qkv[:, pl.ds(2 * D + low, WIN)] * inside
        p = softmax_keys(nt(k, q)).astype(BF)
        prob[h] = p
        mix[:, pl.ds(low, WIN)] += tn(p, v).astype(BF)

    heads_loop(head)
    wo_copy.wait()
    stream_out[...] = video[...].astype(F32) + nn(mix[...], wo[...])

    def second_norm(rows):
        centered, inv = row_stats(stream_out[rows, :])
        hid_out[rows, :] = (centered * inv * gt[...]).astype(BF)

    row_blocks(second_norm)


HALF = POS // 2
BLK = SEQ * HALF


def temporal(hid_in, dmix_in, wq_hbm, mixed_out, dhid_out,
             wq, hid, dmix, qkv, mix, dqkv, sems):
    wq_copies = fetch_columns(wq_hbm, wq, sems)
    for b in range(2):
        part = slice(b * HALF, (b + 1) * HALF)
        rows = slice(b * BLK, (b + 1) * BLK)
        hid[rows, :] = hid_in[:, part, :].reshape(BLK, D)
        dmix[rows, :] = dmix_in[:, part, :].reshape(BLK, D)
    mix[...] = jnp.zeros_like(mix)
    dqkv[...] = jnp.zeros_like(dqkv)
    for c in range(3):
        cols = slice(c * D, (c + 1) * D)
        wq_copies[c].wait()
        qkv[:, cols] = nn(hid[...], wq[:, cols]).astype(BF)

    key_pos = lax.rem(lax.broadcasted_iota(jnp.int32, (BLK, BLK), 0), HALF)
    query_pos = lax.rem(lax.broadcasted_iota(jnp.int32, (BLK, BLK), 1), HALF)
    same = key_pos == query_pos

    def head(h):
        low, inside = window(h)
        for b in range(2):
            rows = slice(b * BLK, (b + 1) * BLK)
            qs, ks, vs = pl.ds(low, WIN), pl.ds(D + low, WIN), pl.ds(2 * D + low, WIN)
            q = qkv[rows, qs] * inside
            k = qkv[rows, ks] * inside
            v = qkv[rows, vs] * inside
            do = dmix[rows, qs] * inside
            p = softmax_keys(jnp.where(same, nt(k, q), -1e30))
            pb = p.astype(BF)
            mix[rows, qs] += tn(pb, v).astype(BF)
            ds = score_grad(p, nt(v, do))
            dqkv[rows, vs] += nn(pb, do).astype(BF)
            dqkv[rows, ks] += nn(ds, q).astype(BF)
            dqkv[rows, qs] += tn(ds, k).astype(BF)

    heads_loop(head)
    dh = nt(dqkv[...], wq[...]).astype(BF)
    for b in range(2):
        part = slice(b * HALF, (b + 1) * HALF)
        rows = slice(b * BLK, (b + 1) * BLK)
        mixed_out[:, part, :] = mix[rows, :].reshape(SEQ, HALF, D)
        dhid_out[:, part, :] = dh[rows, :].reshape(SEQ, HALF, D)


def spatial_backward(dhid, stream, gt, og, qkv, prob, video, gs, wo_hbm, wq_hbm, out,
                     wo, wq, sg, sgb, dmix, dqkv, dh, sems):
    wo_copy = fetch(wo_hbm, wo, sems.at[3])
    wq_copies = fetch_columns(wq_hbm, wq, sems)

    def stream_grad(rows):
        dx = norm_back(stream[rows, :], gt[...], dhid[rows, :].astype(F32))
        total = og[rows, :].astype(F32) + dx
        sg[rows, :] = total
        sgb[rows, :] = total.astype(BF)

    row_blocks(stream_grad)
    dqkv[...] = jnp.zeros_like(dqkv)
    wo_copy.wait()
    dmix[...] = nt(sgb[...], wo[...]).astype(BF)

    def head(h):
        low, inside = window(h)
        qs, ks, vs = pl.ds(low, WIN), pl.ds(D + low, WIN), pl.ds(2 * D + low, WIN)
        q = qkv[:, qs] * inside
        k = qkv[:, ks] * inside
        v = qkv[:, vs]
        do = dmix[:, qs] * inside
        pb = prob[h]
        ds = score_grad(pb.astype(F32), nt(v, do))
        dqkv[:, vs] += nn(pb, do).astype(BF)
        dqkv[:, ks] += nn(ds, q).astype(BF)
        dqkv[:, qs] += tn(ds, k).astype(BF)

    heads_loop(head)
    for copy in wq_copies:
        copy.wait()
    dh[...] = nt(dqkv[...], wq[...]).astype(BF)

    def video_grad(rows):
        dx = norm_back(video[rows, :].astype(F32), gs[...], dh[rows, :].astype(F32))
        out[rows, :] = (sg[rows, :] + dx).astype(BF)

    row_blocks(video_grad)


GROUPS = DP // 2
PER_CORE = GROUPS * HD


def outer_product(core, mixed, og, keep, send, full):
    step = 3 * LANES
    for c in range(D // step):
        full[c * step : (c + 1) * step, :] = tn(mixed[:, c * step : (c + 1) * step], og[...])
    first = core[0] == 0
    for g in range(0, GROUPS, 2):
        even, odd = (
            jnp.concatenate(
                [full[(2 * (g + i) + c) * HD : (2 * (g + i) + c + 1) * HD, :] for i in range(2)]
            )
            for c in range(2)
        )
        rows = slice(g * HD, (g + 2) * HD)
        keep[rows, :] = jnp.where(first, even, odd)
        send[rows, :] = jnp.where(first, odd, even).astype(BF)


def add_and_cut(keep, got, out, block, cut):
    cut[...] = jnp.zeros_like(cut)

    def body(g, carry):
        rows = pl.ds(pl.multiple_of(g * HD, HD), HD)
        block[...] = keep[rows, :] + got[rows, :].astype(F32)
        for j in range(SEQ):
            for t in range(TILES):
                cut[j, t * OWN : (t + 1) * OWN, :] = block[
                    j * OWN : (j + 1) * OWN, t * LANES : (t + 1) * LANES
                ]
            out[g * SEQ + j] = cut[j].astype(BF)
        return carry

    lax.fori_loop(0, GROUPS, body, 0)


def sum_chunks(got, out, total, *, scale):
    total[...] = jnp.sum(got[...].astype(F32), axis=0) * scale
    for t in range(TILES):
        out[:, t * LANES : (t + 1) * LANES] = total[t * OWN : (t + 1) * OWN, :]


def call(fn, outs, args, scratch, flops, name, specs=None):
    if specs is None:
        specs = [VMEM] * len(args)
    moved = sum(a.size * a.dtype.itemsize for a in args)
    moved += sum(math.prod(s) * jnp.dtype(d).itemsize for s, d in outs)
    return pl.pallas_call(
        fn,
        out_shape=[jax.ShapeDtypeStruct(s, d) for s, d in outs],
        in_specs=[pl.BlockSpec(memory_space=s) for s in specs],
        out_specs=[pl.BlockSpec(memory_space=VMEM)] * len(outs),
        scratch_shapes=scratch,
        cost_estimate=pl.CostEstimate(flops=flops, bytes_accessed=moved, transcendentals=0),
        name=name,
    )(*args)


def per_device(
    video,
    out_grad,
    gain_spatial,
    gain_temporal,
    w_spatial_qkv,
    w_spatial_out,
    w_temporal_qkv,
    w_temporal_out,
):
    videos = lax.axis_size("dp") * video.shape[0]
    tokens = videos * SEQ * T
    shape = video.shape
    clip = video.reshape(T, D)
    og = out_grad.reshape(T, D)
    gs = gain_spatial.reshape(1, D)
    gt = gain_temporal.reshape(1, D)
    dma = pltpu.SemaphoreType.DMA((4,))
    wide, square = VMEM((D, 3 * D), BF), VMEM((D, D), BF)
    tok, tok3 = VMEM((T, D), BF), VMEM((T, 3 * D), BF)
    unit = 2 * T * D * D

    def exchange(x):
        return lax.all_to_all(x.reshape(SEQ, POS, D), "seq", 0, 0, tiled=True)

    og_pos = exchange(og)
    hid, stream, qkv, prob = call(
        spatial_forward,
        [((T, D), BF), ((T, D), F32), ((T, 3 * D), BF), ((HEADS, T, T), BF)],
        (clip, gs, gt, w_spatial_qkv, w_spatial_out),
        [wide, square, tok, tok, dma],
        5 * unit,
        "spatial_forward",
        [VMEM, VMEM, VMEM, ANY, ANY],
    )
    hid_pos = exchange(hid)
    dmix = nt(og_pos.reshape(T, D), w_temporal_out).astype(BF).reshape(SEQ, POS, D)
    mixed_pos, dhid_pos = call(
        temporal,
        [((SEQ, POS, D), BF), ((SEQ, POS, D), BF)],
        (hid_pos, dmix, w_temporal_qkv),
        [wide, tok, tok, tok3, tok, tok3, dma],
        8 * unit,
        "temporal",
        [VMEM, VMEM, ANY],
    )
    dhid = exchange(dhid_pos).reshape(T, D)

    core = lax.rem(lax.axis_index("dp"), 2).reshape(1)
    keep, send = call(
        outer_product,
        [((PER_CORE, D), F32), ((PER_CORE, D), BF)],
        (core, mixed_pos.reshape(T, D), og_pos.reshape(T, D)),
        [VMEM((D, D), F32)],
        unit,
        "outer_product",
        [pltpu.SMEM, VMEM, VMEM],
    )
    got = lax.ppermute(send, "dp", [(i, i ^ 1) for i in range(DP)])
    chunks = call(
        add_and_cut,
        [((GROUPS * SEQ, CHUNK, LANES), BF)],
        (keep, got),
        [VMEM((HD, D), F32), VMEM((SEQ, CHUNK, LANES), F32)],
        unit,
        "add_and_cut",
    )[0]
    chunks, dhid = lax.optimization_barrier((chunks, dhid))
    owners = [
        [(g * 2 + c) * SEQ + s for g in range(GROUPS) for s in range(SEQ)] for c in range(2)
    ]
    parts = lax.all_to_all(
        chunks, ("dp", "seq"), 0, 0, axis_index_groups=owners, tiled=True
    )
    video_grad = call(
        spatial_backward,
        [((T, D), BF)],
        (dhid, stream, gt, og, qkv, prob, clip, gs, w_spatial_out, w_spatial_qkv),
        [square, wide, VMEM((T, D), F32), tok, tok, tok3, tok, dma],
        7 * unit,
        "spatial_backward",
        [VMEM] * 8 + [ANY] * 2,
    )[0]

    def finish(got_ref, out_ref, total_ref):
        sum_chunks(got_ref, out_ref, total_ref, scale=1.0 / math.sqrt(float(tokens)))

    w_grad = call(
        finish,
        [((OWN, D), F32)],
        (parts,),
        [VMEM((CHUNK, LANES), F32)],
        1000,
        "sum_chunks",
    )[0]
    return (video_grad.reshape(shape), w_grad)


def solution(mesh):
    return jax.shard_map(
        per_device,
        mesh=mesh,
        in_specs=(
            P("dp", "seq", None, None),
            P("dp", "seq", None, None),
            P(),
            P(),
            P(),
            P(),
            P(),
            P(),
        ),
        out_specs=(P("dp", "seq", None, None), P(("dp", "seq"), None)),
        check_vma=False,
    )
```

time: 368 us -> 122 us (0.33); the launches traced: 362 us -> 121 us
  waiting for transfers between devices: 142 us -> 15.8 us
  local copies, waits for them, and re-layouts: 84.9 us -> 2.6 us
  Pallas kernels: 0 us -> 69.1 us
  matrix products: 65.4 us -> 1.87 us
  other arithmetic: 27.8 us -> 0 us
  between operations: 14.7 us -> 0.72 us
  starting transfers between devices: 27.1 us -> 30.8 us
    unnamed x2 -> x0, waiting for transfers between devices: 114 us -> none
    pallas_call x0 -> x6, Pallas kernels: none -> 69.1 us  [call(): pl.pallas_call(fn, out_shape=[jax.ShapeDtypeStruct(s, d) for s, d in outs...]
    dot_general x20 -> x1, matrix products: 65.4 us -> 1.87 us  [nt(): lax.dot_general(a, b, (((1,), (1,)), ((), ())), preferred_element_type=F32)]
    unnamed x71 -> x6, local copies, waits for them, and re-layouts: 27.9 us -> 0.02 us
    unnamed x4 -> x0, other arithmetic: 19.1 us -> none
    convert_element_type x8 -> x0, local copies, waits for them, and re-layouts: 19 us -> none  [the longest x3 5.81 us: split_heads(): return block.reshape(shape).astype(jnp.float32)]
    all_to_all x4, waiting for transfers between devices: 28.2 us -> 15.8 us  [the longest x3 13.9 us: exchange(): return lax.all_to_all(x.reshape(SEQ, POS, D), 'seq', 0, 0, tiled=True)]
    another operation x3 -> x0, local copies, waits for them, and re-layouts: 11.3 us -> none
  transfers between devices with their start and end apart: 5 -> 5, of which waited for: 3 -> 3; matrix products, arithmetic and copies ran while one was open for 32% -> 4% of each run, Pallas kernels for 0% -> 34%
where the time goes in v1:
time: 122 us; the launch traced here: 121 us
  Pallas kernels  69.1 us (57%)
  starting transfers between devices  30.8 us (25%)
  waiting for transfers between devices  15.8 us (13%)
  local copies, waits for them, and re-layouts  2.6 us (2%)
  matrix products  1.87 us (2%)
    pallas_call x6, Pallas kernels, call(): pl.pallas_call(fn, out_shape=[jax.ShapeDtypeStruct(s, d) for s, d in outs...  69.1 us
    all_to_all x3, starting transfers between devices, exchange(): return lax.all_to_all(x.reshape(SEQ, POS, D), 'seq', 0, 0, tiled=True)  17.9 us
    all_to_all x3, waiting for transfers between devices, exchange(): return lax.all_to_all(x.reshape(SEQ, POS, D), 'seq', 0, 0, tiled=True)  13.9 us
    all_to_all x1, starting transfers between devices, per_device(): lax.all_to_all(chunks, ('dp', 'seq'), 0, 0, axis_index_groups=owners, til...  9.13 us
    ppermute x1, starting transfers between devices, per_device(): got = lax.ppermute(send, 'dp', [(i, i ^ 1) for i in range(DP)])  3.76 us
  transfers between devices with their start and end apart: 5, of which 3 were waited for; matrix products, arithmetic and copies ran while one was open for 4% of the time, Pallas kernels for 34%

profile of v1, /device:TPU:1, one launch (start us, length us, event | category | flops | bytes accessed | tf_op | source)
XLA Modules:
  0.0 120.9 jit_solution(288694389392366575)
XLA Ops:
  0.6 0.0 copy-start
  0.6 7.7 %all-to-all-start.1 = ((bf16[8,32,1152]{2,1,0:T(8,128)(2,1)}), bf16[8,32,1152]{2,1,0:T(8,128)(2,1)S(1)}, u32[]{:S(2)}, u32[]{:S(2)}) async-start(bf16[8,32,1152]{2,1,0:T(8,128)(2,1)} %bitcast.12), calls=%async_computation.1 | async-start | bytes 1179648 | tf_op jit(solution)/shard_map/all_to_all | solution.py:321
  8.4 1.3 %reshape.40.gs = f32[1,1152]{1,0:T(1,128)} reshape(f32[1152]{0:T(1024)} %param.10) | data formatting | bytes 9216 | tf_op jit(solution)/shard_map/reshape | solution.py:313
  9.7 1.3 %reshape.41.gt = f32[1,1152]{1,0:T(1,128)} reshape(f32[1152]{0:T(1024)} %param.11) | data formatting | bytes 9216 | tf_op jit(solution)/shard_map/reshape | solution.py:314
  11.0 18.1 %spatial_forward.1 = (bf16[256,1152]{1,0:T(8,128)(2,1)}, f32[256,1152]{1,0:T(8,128)}, bf16[256,3456]{1,0:T(8,128)(2,1)}, bf16[16,256,256]{2,1,0:T(8,128)(2,1)}) custom-call(bf16[256,1152]{1,0:T(8,128)(2,1)} %bitcast.15, f32[1,1152]{1,0:T(1,128)} %reshape.40.gs, f32[1,1152]{1,0:T(1,128)} %reshape.41.gt, bf16[1152,3456]{1,0:T(8,128)(2,1)} %wq_hbm.5, ...), custom_call_target="tpu_custom_call" | custom-call | flops 3397386240 | bytes 16851968 | tf_op jit(solution)/shard_map/spatial_forward/pallas_call | solution.py:287
  29.1 0.0 all-to-all-done.1
  29.1 0.0 copy-start.2
  29.1 6.7 %all-to-all-start = ((bf16[8,32,1152]{2,1,0:T(8,128)(2,1)}), bf16[8,32,1152]{2,1,0:T(8,128)(2,1)}, u32[]{:S(2)}, u32[]{:S(2)}) async-start(bf16[8,32,1152]{2,1,0:T(8,128)(2,1)} %bitcast.20), calls=%async_computation | async-start | bytes 1179648 | tf_op jit(solution)/shard_map/all_to_all | solution.py:321
  35.8 0.0 copy-done
  35.8 1.9 %convolution_convert_fusion = bf16[256,1152]{1,0:T(8,128)(2,1)} fusion(bf16[256,1152]{1,0:T(8,128)(2,1)S(1)} %bitcast.18, bf16[1152,1152]{1,0:T(8,128)(2,1)S(1)} %copy-done), kind=kOutput, calls=%fused_computation | convolution fusion | flops 679772160 | bytes 3833856 | tf_op jit(solution)/shard_map/dot_general | solution.py:37
  37.7 0.0 copy-done.2
  37.7 7.2 %all-to-all-done.hid_in = bf16[8,32,1152]{2,1,0:T(8,128)(2,1)} async-done(((bf16[8,32,1152]{2,1,0:T(8,128)(2,1)}), bf16[8,32,1152]{2,1,0:T(8,128)(2,1)}, u32[]{:S(2)}, u32[]{:S(2)}) %all-to-all-start) | async-done | bytes 589856 | tf_op jit(solution)/shard_map/all_to_all | solution.py:321
  44.9 21.7 %temporal.1 = (bf16[8,32,1152]{2,1,0:T(8,128)(2,1)}, bf16[8,32,1152]{2,1,0:T(8,128)(2,1)}) custom-call(bf16[8,32,1152]{2,1,0:T(8,128)(2,1)} %all-to-all-done.hid_in, bf16[8,32,1152]{2,1,0:T(8,128)(2,1)} %bitcast.21, bf16[1152,3456]{1,0:T(8,128)(2,1)} %wq_hbm.4), custom_call_target="tpu_custom_call" | custom-call | flops 5435817984 | bytes 10321920 | tf_op jit(solution)/shard_map/temporal/pallas_call | solution.py:287
  66.6 4.2 %outer_product.1 = (f32[576,1152]{1,0:T(8,128)}, bf16[576,1152]{1,0:T(8,128)(2,1)}) custom-call(s32[1]{0:T(128)} %bitcast.core, bf16[256,1152]{1,0:T(8,128)(2,1)} %bitcast.22, bf16[256,1152]{1,0:T(8,128)(2,1)} %bitcast.19), custom_call_target="tpu_custom_call" | custom-call | flops 679477248 | bytes 5160964 | tf_op jit(solution)/shard_map/outer_product/pallas_call | solution.py:287
  70.8 3.8 %collective-permute-start = (bf16[576,1152]{1,0:T(8,128)(2,1)}, bf16[576,1152]{1,0:T(8,128)(2,1)}, u32[]{:S(2)}, u32[]{:S(2)}) collective-permute-start(bf16[576,1152]{1,0:T(8,128)(2,1)} %get-tuple-element.15), channel_id=1, source_target_pairs={{0,8},{8,0},{16,24},{24,16},{32,40},{40,32},{48,56},{56,48},{64,72... | collective-permute-start | bytes 3981320 | tf_op jit(solution)/shard_map/ppermute | solution.py:356
  74.5 3.5 %all-to-all-start.2 = ((bf16[8,32,1152]{2,1,0:T(8,128)(2,1)}), bf16[8,32,1152]{2,1,0:T(8,128)(2,1)S(1)}, u32[]{:S(2)}, u32[]{:S(2)}) async-start(bf16[8,32,1152]{2,1,0:T(8,128)(2,1)} %get-tuple-element.16), calls=%async_computation.2 | async-start | bytes 1179648 | tf_op jit(solution)/shard_map/all_to_all | solution.py:321
  78.1 0.0 collective-permute-done.got
  78.1 4.1 %add_and_cut.1 = bf16[64,88,128]{2,1,0:T(8,128)(2,1)} custom-call(f32[576,1152]{1,0:T(8,128)} %get-tuple-element.14.keep, bf16[576,1152]{1,0:T(8,128)(2,1)} %collective-permute-done.got), custom_call_target="tpu_custom_call" | custom-call | flops 679477248 | bytes 5423104 | tf_op jit(solution)/shard_map/add_and_cut/pallas_call | solution.py:287
  82.2 6.6 %all-to-all-done.2 = bf16[8,32,1152]{2,1,0:T(8,128)(2,1)S(1)} async-done(((bf16[8,32,1152]{2,1,0:T(8,128)(2,1)}), bf16[8,32,1152]{2,1,0:T(8,128)(2,1)S(1)}, u32[]{:S(2)}, u32[]{:S(2)}) %all-to-all-start.2) | async-done | bytes 589856 | tf_op jit(solution)/shard_map/all_to_all | solution.py:321
  88.8 0.0 copy-start.1
  88.8 9.1 %all-to-all-start.3 = ((bf16[64,88,128]{2,1,0:T(8,128)(2,1)}), bf16[64,88,128]{2,1,0:T(8,128)(2,1)}, u32[]{:S(2)}, u32[]{:S(2)}) async-start(bf16[64,88,128]{2,1,0:T(8,128)(2,1)} %add_and_cut.1), calls=%async_computation.3 | async-start | bytes 2883584 | tf_op jit(solution)/shard_map/all_to_all | solution.py:369
  97.9 0.0 copy-done.1
  98.0 18.7 %spatial_backward.1 = bf16[256,1152]{1,0:T(8,128)(2,1)} custom-call(bf16[256,1152]{1,0:T(8,128)(2,1)} %bitcast.14, f32[256,1152]{1,0:T(8,128)} %get-tuple-element.18.stream, f32[1,1152]{1,0:T(1,128)} %reshape.41.gt, bf16[256,1152]{1,0:T(8,128)(2,1)} %bitcast.13, bf16[256,3456]{1,0:T(8,128)(2,1)} %get-tuple-element.19.qkv, ...), custom_call_target="tpu_custom_call" | custom-call | flops 4756340736 | bytes 18031616 | tf_op jit(solution)/shard_map/spatial_backward/pallas_call | solution.py:287
  116.7 2.0 %all-to-all-done.3.got_ref = bf16[64,88,128]{2,1,0:T(8,128)(2,1)} async-done(((bf16[64,88,128]{2,1,0:T(8,128)(2,1)}), bf16[64,88,128]{2,1,0:T(8,128)(2,1)}, u32[]{:S(2)}, u32[]{:S(2)}) %all-to-all-start.3) | async-done | bytes 1441824 | tf_op jit(solution)/shard_map/all_to_all | solution.py:369
  118.7 2.3 %sum_chunks.1 = f32[9,1152]{1,0:T(8,128)} custom-call(bf16[64,88,128]{2,1,0:T(8,128)(2,1)} %all-to-all-done.3.got_ref), custom_call_target="tpu_custom_call" | custom-call | flops 1000 | bytes 1483264 | tf_op jit(solution)/shard_map/sum_chunks/pallas_call | solution.py:287
Async XLA Ops:
  0.6 35.2 %copy-start = (bf16[1152,1152]{1,0:T(8,128)(2,1)S(1)}, bf16[1152,1152]{1,0:T(8,128)(2,1)}, u32[]{:S(2)}) copy-start(bf16[1152,1152]{1,0:T(8,128)(2,1)} %param.15) | copy-start | bytes 7962628
  0.6 28.5 %all-to-all-start.1 = ((bf16[8,32,1152]{2,1,0:T(8,128)(2,1)}), bf16[8,32,1152]{2,1,0:T(8,128)(2,1)S(1)}, u32[]{:S(2)}, u32[]{:S(2)}) async-start(bf16[8,32,1152]{2,1,0:T(8,128)(2,1)} %bitcast.12), calls=%async_computation.1 | async-start | bytes 1179648 | tf_op jit(solution)/shard_map/all_to_all | solution.py:321
  29.1 8.6 %copy-start.2 = (bf16[8,32,1152]{2,1,0:T(8,128)(2,1)}, bf16[8,32,1152]{2,1,0:T(8,128)(2,1)S(1)}, u32[]{:S(2)}) copy-start(bf16[8,32,1152]{2,1,0:T(8,128)(2,1)S(1)} %all-to-all-done.1) | copy-start | bytes 1769476
  29.1 15.8 %all-to-all-start = ((bf16[8,32,1152]{2,1,0:T(8,128)(2,1)}), bf16[8,32,1152]{2,1,0:T(8,128)(2,1)}, u32[]{:S(2)}, u32[]{:S(2)}) async-start(bf16[8,32,1152]{2,1,0:T(8,128)(2,1)} %bitcast.20), calls=%async_computation | async-start | bytes 1179648 | tf_op jit(solution)/shard_map/all_to_all | solution.py:321
  70.8 7.3 %collective-permute-start = (bf16[576,1152]{1,0:T(8,128)(2,1)}, bf16[576,1152]{1,0:T(8,128)(2,1)}, u32[]{:S(2)}, u32[]{:S(2)}) collective-permute-start(bf16[576,1152]{1,0:T(8,128)(2,1)} %get-tuple-element.15), channel_id=1, source_target_pairs={{0,8},{8,0},{16,24},{24,16},{32,40},{40,32},{48,56},{56,48},{64,72... | collective-permute-start | bytes 3981320 | tf_op jit(solution)/shard_map/ppermute | solution.py:356
  74.5 14.3 %all-to-all-start.2 = ((bf16[8,32,1152]{2,1,0:T(8,128)(2,1)}), bf16[8,32,1152]{2,1,0:T(8,128)(2,1)S(1)}, u32[]{:S(2)}, u32[]{:S(2)}) async-start(bf16[8,32,1152]{2,1,0:T(8,128)(2,1)} %get-tuple-element.16), calls=%async_computation.2 | async-start | bytes 1179648 | tf_op jit(solution)/shard_map/all_to_all | solution.py:321
  88.8 9.1 %copy-start.1 = (bf16[8,32,1152]{2,1,0:T(8,128)(2,1)}, bf16[8,32,1152]{2,1,0:T(8,128)(2,1)S(1)}, u32[]{:S(2)}) copy-start(bf16[8,32,1152]{2,1,0:T(8,128)(2,1)S(1)} %all-to-all-done.2) | copy-start | bytes 1769476
  88.8 29.9 %all-to-all-start.3 = ((bf16[64,88,128]{2,1,0:T(8,128)(2,1)}), bf16[64,88,128]{2,1,0:T(8,128)(2,1)}, u32[]{:S(2)}, u32[]{:S(2)}) async-start(bf16[64,88,128]{2,1,0:T(8,128)(2,1)} %add_and_cut.1), calls=%async_computation.3 | async-start | bytes 2883584 | tf_op jit(solution)/shard_map/all_to_all | solution.py:369

commit v2 on v1

v2 whole, which is shorter than its diff:
```python
import math

import jax
import jax.numpy as jnp
from jax import lax
from jax.experimental import pallas as pl
from jax.experimental.pallas import tpu as pltpu
from jax.sharding import PartitionSpec as P


HEADS = 16
D = 1152
HD = D // HEADS
T = 256
SEQ = 8
POS = T // SEQ
DP = 16
EPS = 1e-06
LOG2E = 1.0 / math.log(2.0)
SCALE = 1.0 / math.sqrt(HD)
BF = jnp.bfloat16
F32 = jnp.float32
ROWS = 32
WIN = 256
CHUNK = 88
OWN = D // (DP * SEQ)
LANES = 128
TILES = D // LANES

VMEM = pltpu.VMEM
ANY = pl.ANY


def nn(a, b):
    return lax.dot_general(a, b, (((1,), (0,)), ((), ())), preferred_element_type=F32)


def nt(a, b):
    return lax.dot_general(a, b, (((1,), (1,)), ((), ())), preferred_element_type=F32)


def tn(a, b):
    return lax.dot_general(a, b, (((0,), (0,)), ((), ())), preferred_element_type=F32)


def row_stats(x):
    center = jnp.mean(x, axis=-1, keepdims=True)
    centered = x - center
    spread = jnp.mean(centered * centered, axis=-1, keepdims=True)
    return centered, lax.rsqrt(spread + EPS)


def row_blocks(fn):
    def body(i, carry):
        fn(pl.ds(pl.multiple_of(i * ROWS, ROWS), ROWS))
        return carry

    lax.fori_loop(0, T // ROWS, body, 0)


def norm_back(x, g, dy):
    centered, inv = row_stats(x)
    xhat = centered * inv
    dxhat = dy * g
    mean_d = jnp.mean(dxhat, axis=-1, keepdims=True)
    mean_dx = jnp.mean(dxhat * xhat, axis=-1, keepdims=True)
    return inv * (dxhat - mean_d - xhat * mean_dx)


def window(h):
    tile = jnp.minimum(lax.div(h * HD, LANES), TILES - 2)
    low = pl.multiple_of(tile * LANES, LANES)
    start = h * HD - low
    lane = lax.broadcasted_iota(jnp.int32, (1, WIN), 1)
    inside = jnp.where((lane >= start) & (lane < start + HD), 1.0, 0.0)
    return low, inside.astype(BF)


def softmax_keys(scores):
    top = jnp.max(scores, axis=0, keepdims=True)
    e = jnp.exp2((scores - top) * (SCALE * LOG2E))
    return e * (1.0 / jnp.sum(e, axis=0, keepdims=True))


def score_grad(prob, prob_grad):
    t = prob * prob_grad
    delta = jnp.sum(t, axis=0, keepdims=True)
    return ((t - prob * delta) * SCALE).astype(BF)


def heads_loop(first, second, unroll=8, ahead=1):
    def body(i, carry):
        waiting = []
        for u in range(unroll):
            h = i * unroll + u
            waiting.append((h, first(h)))
            if len(waiting) > ahead:
                h, values = waiting.pop(0)
                second(h, *values)
        for h, values in waiting:
            second(h, *values)
        return carry

    lax.fori_loop(0, HEADS // unroll, body, 0)


def merge(slots, dst, base=0):
    for t in range(TILES):
        total = None
        for h in range(HEADS):
            first = min(h * HD // LANES, TILES - 2)
            if h * HD < (t + 1) * LANES and (h + 1) * HD > t * LANES:
                at = (t - first) * LANES
                piece = slots[h, :, at : at + LANES]
                total = piece if total is None else total + piece
        dst[:, base + t * LANES : base + (t + 1) * LANES] = total


def fetch(src, dst, sem):
    copy = pltpu.make_async_copy(src, dst, sem)
    copy.start()
    return copy


CUTS = (0, 512, 1536, 2560, 3456)
PIECES = [slice(a, b) for a, b in zip(CUTS, CUTS[1:])]


def fetch_columns(src, dst, sems):
    return [fetch(src.at[:, p], dst.at[:, p], sems.at[i]) for i, p in enumerate(PIECES)]


def spatial_forward(video, gs, gt, wq_hbm, wo_hbm, hid_out, stream_hbm, qkv_hbm, prob_hbm,
                    wq, wo, hid, mix, stream, qkv, prob, slots, sems, out_sems):
    wq_copies = fetch_columns(wq_hbm, wq, sems)
    wo_copy = fetch(wo_hbm, wo, sems.at[4])

    def first_norm(rows):
        centered, inv = row_stats(video[rows, :].astype(F32))
        hid[rows, :] = (centered * inv * gs[...].reshape(1, D)).astype(BF)

    row_blocks(first_norm)
    for copy, p in zip(wq_copies, PIECES):
        copy.wait()
        qkv[:, p] = nn(hid[...], wq[:, p]).astype(BF)
    qkv_copy = fetch(qkv, qkv_hbm, out_sems.at[0])

    def head(h):
        low, inside = window(h)
        q = qkv[:, pl.ds(low, WIN)] * inside
        k = qkv[:, pl.ds(D + low, WIN)]
        v = qkv[:, pl.ds(2 * D + low, WIN)] * inside
        return nt(k, q), v

    def rest(h, scores, v):
        p = softmax_keys(scores).astype(BF)
        prob[h] = p
        slots[h] = tn(p, v).astype(BF)

    heads_loop(head, rest)
    prob_copy = fetch(prob, prob_hbm, out_sems.at[1])
    merge(slots, mix)
    wo_copy.wait()
    stream[...] = video[...].astype(F32) + nn(mix[...], wo[...])
    stream_copy = fetch(stream, stream_hbm, out_sems.at[2])

    def second_norm(rows):
        centered, inv = row_stats(stream[rows, :])
        hid_out[rows, :] = (centered * inv * gt[...].reshape(1, D)).astype(BF)

    row_blocks(second_norm)
    for copy in (qkv_copy, prob_copy, stream_copy):
        copy.wait()


HALF = POS // 2
BLK = SEQ * HALF


def temporal(hid_in, dmix_in, wq_hbm, mixed_out, dhid_out,
             wq, hid, dmix, qkv, mix, dqkv, o_slots, q_slots, k_slots, v_slots, sems):
    wq_copies = fetch_columns(wq_hbm, wq, sems)
    for b in range(2):
        part = slice(b * HALF, (b + 1) * HALF)
        rows = slice(b * BLK, (b + 1) * BLK)
        hid[rows, :] = hid_in[:, part, :].reshape(BLK, D)
        dmix[rows, :] = dmix_in[:, part, :].reshape(BLK, D)
    for copy, p in zip(wq_copies, PIECES):
        copy.wait()
        qkv[:, p] = nn(hid[...], wq[:, p]).astype(BF)

    key_pos = lax.rem(lax.broadcasted_iota(jnp.int32, (BLK, BLK), 0), HALF)
    query_pos = lax.rem(lax.broadcasted_iota(jnp.int32, (BLK, BLK), 1), HALF)
    same = key_pos == query_pos

    def head(h):
        low, inside = window(h)
        values = []
        for b in range(2):
            rows = slice(b * BLK, (b + 1) * BLK)
            qs, ks, vs = pl.ds(low, WIN), pl.ds(D + low, WIN), pl.ds(2 * D + low, WIN)
            q = qkv[rows, qs] * inside
            k = qkv[rows, ks] * inside
            v = qkv[rows, vs] * inside
            do = dmix[rows, qs] * inside
            values.append((nt(k, q), nt(v, do), q, k, v, do))
        return values

    def rest(h, *values):
        for b, (scores, prob_grad, q, k, v, do) in enumerate(values):
            rows = slice(b * BLK, (b + 1) * BLK)
            p = softmax_keys(jnp.where(same, scores, -1e30))
            pb = p.astype(BF)
            ds = score_grad(p, prob_grad)
            o_slots[h, rows, :] = tn(pb, v).astype(BF)
            v_slots[h, rows, :] = nn(pb, do).astype(BF)
            k_slots[h, rows, :] = nn(ds, q).astype(BF)
            q_slots[h, rows, :] = tn(ds, k).astype(BF)

    heads_loop(head, rest)
    merge(o_slots, mix)
    for i, slots in enumerate((q_slots, k_slots, v_slots)):
        merge(slots, dqkv, i * D)
    dh = nt(dqkv[...], wq[...]).astype(BF)
    for b in range(2):
        part = slice(b * HALF, (b + 1) * HALF)
        rows = slice(b * BLK, (b + 1) * BLK)
        mixed_out[:, part, :] = mix[rows, :].reshape(SEQ, HALF, D)
        dhid_out[:, part, :] = dh[rows, :].reshape(SEQ, HALF, D)


def spatial_backward(dhid_hbm, stream_hbm, gt, og_hbm, qkv_hbm, prob_hbm, video_hbm, gs,
                     wo_hbm, wq_hbm, out, dhid, stream, og, qkv, prob, video, wo, wq,
                     sg, sgb, dmix, dqkv, dh, q_slots, k_slots, v_slots, sems):
    pairs = (
        (dhid_hbm, dhid), (stream_hbm, stream), (og_hbm, og), (wo_hbm, wo), (qkv_hbm, qkv),
        (prob_hbm, prob), (wq_hbm, wq), (video_hbm, video),
    )
    copies = [fetch(src, dst, sems.at[i]) for i, (src, dst) in enumerate(pairs)]
    for copy in copies[:3]:
        copy.wait()

    def stream_grad(rows):
        dx = norm_back(stream[rows, :], gt[...].reshape(1, D), dhid[rows, :].astype(F32))
        total = og[rows, :].astype(F32) + dx
        sg[rows, :] = total
        sgb[rows, :] = total.astype(BF)

    row_blocks(stream_grad)
    copies[3].wait()
    dmix[...] = nt(sgb[...], wo[...]).astype(BF)
    copies[4].wait()
    copies[5].wait()

    def head(h):
        low, inside = window(h)
        qs, ks, vs = pl.ds(low, WIN), pl.ds(D + low, WIN), pl.ds(2 * D + low, WIN)
        q = qkv[:, qs] * inside
        k = qkv[:, ks] * inside
        v = qkv[:, vs]
        do = dmix[:, qs] * inside
        return nt(v, do), q, k, do

    def rest(h, prob_grad, q, k, do):
        pb = prob[h]
        ds = score_grad(pb.astype(F32), prob_grad)
        v_slots[h] = nn(pb, do).astype(BF)
        k_slots[h] = nn(ds, q).astype(BF)
        q_slots[h] = tn(ds, k).astype(BF)

    heads_loop(head, rest)
    for i, slots in enumerate((q_slots, k_slots, v_slots)):
        merge(slots, dqkv, i * D)
    copies[6].wait()
    dh[...] = nt(dqkv[...], wq[...]).astype(BF)
    copies[7].wait()

    def video_grad(rows):
        dx = norm_back(video[rows, :].astype(F32), gs[...].reshape(1, D), dh[rows, :].astype(F32))
        out[rows, :] = (sg[rows, :] + dx).astype(BF)

    row_blocks(video_grad)


GROUPS = DP // 2
PER_CORE = GROUPS * HD


def outer_product(core, mixed, og, keep, send, full):
    step = 3 * LANES
    for c in range(D // step):
        full[c * step : (c + 1) * step, :] = tn(mixed[:, c * step : (c + 1) * step], og[...])
    first = core[0] == 0
    for g in range(0, GROUPS, 2):
        even, odd = (
            jnp.concatenate(
                [full[(2 * (g + i) + c) * HD : (2 * (g + i) + c + 1) * HD, :] for i in range(2)]
            )
            for c in range(2)
        )
        rows = slice(g * HD, (g + 2) * HD)
        keep[rows, :] = jnp.where(first, even, odd).astype(BF)
        send[rows, :] = jnp.where(first, odd, even).astype(BF)


SUB = 8


def add_and_cut(keep, got, out, block):
    place = lax.broadcasted_iota(jnp.int32, (SUB, 1), 0)

    def body(g, carry):
        rows = pl.ds(pl.multiple_of(g * 2 * HD, 2 * HD), 2 * HD)
        block[...] = keep[rows, :].astype(F32) + got[rows, :].astype(F32)
        for i in range(2):
            for j in range(SEQ):
                at = i * HD + j * SUB
                upper, lower = block[at : at + SUB, :], block[at + SUB : at + 2 * SUB, :]
                eight = jnp.where(place >= j, upper, lower)
                ninth = lower[j : j + 1, :]
                parts = [eight[:, t * LANES : (t + 1) * LANES] for t in range(TILES)]
                for first in (0, SUB):
                    rest = jnp.zeros((SUB, LANES), F32)
                    for t in range(first, min(first + SUB, TILES)):
                        rest = jnp.where(
                            place == t - first, ninth[:, t * LANES : (t + 1) * LANES], rest
                        )
                    parts.append(rest)
                out[(g * 2 + i) * SEQ + j] = jnp.concatenate(parts).astype(BF)
        return carry

    lax.fori_loop(0, GROUPS // 2, body, 0)


def sum_chunks(owner, got, out, total, *, scale):
    total[...] = jnp.sum(got[...].astype(F32), axis=0) * scale
    back = lax.rem(SUB - owner[0], SUB)
    for t in range(TILES):
        lanes = slice(t * LANES, (t + 1) * LANES)
        out[:SUB, lanes] = pltpu.roll(total[t * SUB : (t + 1) * SUB, :], back, 0)
        out[SUB:, lanes] = total[TILES * SUB + t : TILES * SUB + t + 1, :]


def call(fn, outs, args, scratch, flops, specs=None, out_specs=None):
    if specs is None:
        specs = [VMEM] * len(args)
    if out_specs is None:
        out_specs = [VMEM] * len(outs)
    moved = sum(a.size * a.dtype.itemsize for a in args)
    moved += sum(math.prod(s) * jnp.dtype(d).itemsize for s, d in outs)
    return pl.pallas_call(
        fn,
        out_shape=[jax.ShapeDtypeStruct(s, d) for s, d in outs],
        in_specs=[pl.BlockSpec(memory_space=s) for s in specs],
        out_specs=[pl.BlockSpec(memory_space=s) for s in out_specs],
        scratch_shapes=scratch,
        cost_estimate=pl.CostEstimate(flops=flops, bytes_accessed=moved, transcendentals=0),
    )(*args)


UNIT = 2 * T * D * D
WIDE, SQUARE = VMEM((D, 3 * D), BF), VMEM((D, D), BF)
TOK, TOK3, TOKF = VMEM((T, D), BF), VMEM((T, 3 * D), BF), VMEM((T, D), F32)
PROB, SLOTS = VMEM((HEADS, T, T), BF), VMEM((HEADS, T, WIN), BF)
DMA = pltpu.SemaphoreType.DMA


def run_spatial_forward(clip, gs, gt, wq, wo):
    return call(
        spatial_forward,
        [((T, D), BF), ((T, D), F32), ((T, 3 * D), BF), ((HEADS, T, T), BF)],
        (clip, gs, gt, wq, wo),
        [WIDE, SQUARE, TOK, TOK, TOKF, TOK3, PROB, SLOTS, DMA((5,)), DMA((3,))],
        5 * UNIT,
        [VMEM, VMEM, VMEM, ANY, ANY],
        [VMEM, ANY, ANY, ANY],
    )


def run_temporal(hid, dmix, wq):
    return call(
        temporal,
        [((SEQ, POS, D), BF), ((SEQ, POS, D), BF)],
        (hid, dmix, wq),
        [WIDE, TOK, TOK, TOK3, TOK, TOK3, SLOTS, SLOTS, SLOTS, SLOTS, DMA((4,))],
        8 * UNIT,
        [VMEM, VMEM, ANY],
    )


def run_spatial_backward(dhid, stream, gt, og, qkv, prob, clip, gs, wo, wq):
    return call(
        spatial_backward,
        [((T, D), BF)],
        (dhid, stream, gt, og, qkv, prob, clip, gs, wo, wq),
        [TOK, TOKF, TOK, TOK3, PROB, TOK, SQUARE, WIDE, TOKF, TOK, TOK, TOK3, TOK,
         SLOTS, SLOTS, SLOTS, DMA((8,))],
        7 * UNIT,
        [ANY, ANY, VMEM, ANY, ANY, ANY, ANY, VMEM, ANY, ANY],
    )[0]


def run_outer_product(core, mixed, og):
    return call(
        outer_product,
        [((PER_CORE, D), BF), ((PER_CORE, D), BF)],
        (core, mixed, og),
        [VMEM((D, D), F32)],
        UNIT,
        [pltpu.SMEM, VMEM, VMEM],
    )


def run_add_and_cut(keep, got):
    return call(
        add_and_cut,
        [((GROUPS * SEQ, CHUNK, LANES), BF)],
        (keep, got),
        [VMEM((2 * HD, D), F32)],
        UNIT // 4,
    )[0]


def run_sum_chunks(owner, parts, scale):
    def finish(owner_ref, got_ref, out_ref, total_ref):
        sum_chunks(owner_ref, got_ref, out_ref, total_ref, scale=scale)

    return call(
        finish,
        [((OWN, D), F32)],
        (owner, parts),
        [VMEM((CHUNK, LANES), F32)],
        1000,
        [pltpu.SMEM, VMEM],
    )[0]


def per_device(
    video,
    out_grad,
    gain_spatial,
    gain_temporal,
    w_spatial_qkv,
    w_spatial_out,
    w_temporal_qkv,
    w_temporal_out,
):
    tokens = lax.axis_size("dp") * video.shape[0] * SEQ * T
    shape = video.shape
    clip = video.reshape(T, D)
    og = out_grad.reshape(T, D)

    def exchange(x):
        return lax.all_to_all(x.reshape(SEQ, POS, D), "seq", 0, 0, tiled=True)

    og_pos = exchange(og)
    hid, stream, qkv, prob = run_spatial_forward(
        clip, gain_spatial, gain_temporal, w_spatial_qkv, w_spatial_out
    )
    hid_pos = exchange(hid)
    dmix = nt(og_pos.reshape(T, D), w_temporal_out).astype(BF).reshape(SEQ, POS, D)
    mixed_pos, dhid_pos = run_temporal(hid_pos, dmix, w_temporal_qkv)
    dhid = exchange(dhid_pos).reshape(T, D)

    core = lax.rem(lax.axis_index("dp"), 2).reshape(1)
    keep, send = run_outer_product(core, mixed_pos.reshape(T, D), og_pos.reshape(T, D))
    got = lax.ppermute(send, "dp", [(i, i ^ 1) for i in range(DP)])
    chunks = run_add_and_cut(keep, got)
    chunks, dhid = lax.optimization_barrier((chunks, dhid))
    owners = [
        [(g * 2 + c) * SEQ + s for g in range(GROUPS) for s in range(SEQ)] for c in range(2)
    ]
    parts = lax.all_to_all(
        chunks, ("dp", "seq"), 0, 0, axis_index_groups=owners, tiled=True
    )
    video_grad = run_spatial_backward(
        dhid, stream, gain_temporal, og, qkv, prob, clip, gain_spatial,
        w_spatial_out, w_spatial_qkv,
    )
    owner = lax.axis_index("seq").reshape(1)
    w_grad = run_sum_chunks(owner, parts, 1.0 / math.sqrt(float(tokens)))
    return (video_grad.reshape(shape), w_grad)


def solution(mesh):
    return jax.shard_map(
        per_device,
        mesh=mesh,
        in_specs=(
            P("dp", "seq", None, None),
            P("dp", "seq", None, None),
            P(),
            P(),
            P(),
            P(),
            P(),
            P(),
        ),
        out_specs=(P("dp", "seq", None, None), P(("dp", "seq"), None)),
        check_vma=False,
    )
```

time: 122 us -> 105 us (0.86)
  Pallas kernels: 69.1 us -> 50.8 us
  waiting for transfers between devices: 15.8 us -> 19.7 us
  local copies, waits for them, and re-layouts: 2.6 us -> 0.02 us
    pallas_call x6, Pallas kernels: 69.1 us -> 50.8 us  [call(): pl.pallas_call(fn, out_shape=[jax.ShapeDtypeStruct(s, d) for s, d in outs...]
    all_to_all x1, waiting for transfers between devices: 1.97 us -> 5.14 us  [per_device(): lax.all_to_all(chunks, ('dp', 'seq'), 0, 0, axis_index_groups=owners, til...]
    reshape x2 -> x0, local copies, waits for them, and re-layouts: 2.59 us -> none  [the longest x1 1.29 us: per_device(): gt = gain_temporal.reshape(1, D)]
  transfers between devices with their start and end apart: 5 -> 5, of which waited for: 3 -> 3; matrix products, arithmetic and copies ran while one was open for 4% -> 2% of each run, Pallas kernels for 34% -> 29%
where the time goes in v2:
time: 105 us; the launch traced here: 104 us
  Pallas kernels  50.8 us (48%)
  starting transfers between devices  31 us (30%)
  waiting for transfers between devices  19.7 us (19%)
  matrix products  1.86 us (2%)
    pallas_call x6, Pallas kernels, call(): pl.pallas_call(fn, out_shape=[jax.ShapeDtypeStruct(s, d) for s, d in outs...  50.8 us
    all_to_all x3, starting transfers between devices, exchange(): return lax.all_to_all(x.reshape(SEQ, POS, D), 'seq', 0, 0, tiled=True)  17.9 us
    all_to_all x3, waiting for transfers between devices, exchange(): return lax.all_to_all(x.reshape(SEQ, POS, D), 'seq', 0, 0, tiled=True)  14.6 us
    all_to_all x1, starting transfers between devices, per_device(): lax.all_to_all(chunks, ('dp', 'seq'), 0, 0, axis_index_groups=owners, til...  9.35 us
    all_to_all x1, waiting for transfers between devices, per_device(): lax.all_to_all(chunks, ('dp', 'seq'), 0, 0, axis_index_groups=owners, til...  5.14 us
    ppermute x1, starting transfers between devices, per_device(): got = lax.ppermute(send, 'dp', [(i, i ^ 1) for i in range(DP)])  3.75 us
  transfers between devices with their start and end apart: 5, of which 3 were waited for; matrix products, arithmetic and copies ran while one was open for 2% of the time, Pallas kernels for 29%

profile of v2, /device:TPU:1, one launch (start us, length us, event | category | flops | bytes accessed | tf_op | source)
XLA Modules:
  0.0 104.2 jit_solution(9188445222058924883)
XLA Ops:
  0.6 0.0 copy-start
  0.6 7.7 %all-to-all-start.1 = ((bf16[8,32,1152]{2,1,0:T(8,128)(2,1)}), bf16[8,32,1152]{2,1,0:T(8,128)(2,1)S(1)}, u32[]{:S(2)}, u32[]{:S(2)}) async-start(bf16[8,32,1152]{2,1,0:T(8,128)(2,1)} %bitcast.13), calls=%async_computation.1 | async-start | bytes 1179648 | tf_op jit(solution)/shard_map/all_to_all | solution.py:454
  8.4 12.0 %shard_map.95 = (bf16[256,1152]{1,0:T(8,128)(2,1)}, f32[256,1152]{1,0:T(8,128)}, bf16[256,3456]{1,0:T(8,128)(2,1)}, bf16[16,256,256]{2,1,0:T(8,128)(2,1)}) custom-call(bf16[256,1152]{1,0:T(8,128)(2,1)} %bitcast.16, f32[1152]{0:T(1024)} %gs.3, f32[1152]{0:T(1024)} %gt.3, bf16[1152,3456]{1,0:T(8,128)(2,1)} %wq_hbm.5, bf16[1152,1152]{1,0:T(8,128)(2,1)} %wo_hbm.3), custom_call_target="tpu_custom_call" | custom-call | flops 3397386240 | bytes 16851968 | tf_op jit(solution)/shard_map/pallas_call | solution.py:351
  20.4 0.0 all-to-all-done.1
  20.4 0.0 copy-start.2
  20.4 6.7 %all-to-all-start = ((bf16[8,32,1152]{2,1,0:T(8,128)(2,1)}), bf16[8,32,1152]{2,1,0:T(8,128)(2,1)}, u32[]{:S(2)}, u32[]{:S(2)}) async-start(bf16[8,32,1152]{2,1,0:T(8,128)(2,1)} %bitcast.21), calls=%async_computation | async-start | bytes 1179648 | tf_op jit(solution)/shard_map/all_to_all | solution.py:454
  27.0 0.0 copy-done
  27.1 1.9 %convolution_convert_fusion = bf16[256,1152]{1,0:T(8,128)(2,1)} fusion(bf16[256,1152]{1,0:T(8,128)(2,1)S(1)} %bitcast.19, bf16[1152,1152]{1,0:T(8,128)(2,1)S(1)} %copy-done), kind=kOutput, calls=%fused_computation | convolution fusion | flops 679772160 | bytes 3833856 | tf_op jit(solution)/shard_map/dot_general | solution.py:39
  28.9 0.0 copy-done.2
  28.9 7.2 %all-to-all-done.hid_in = bf16[8,32,1152]{2,1,0:T(8,128)(2,1)} async-done(((bf16[8,32,1152]{2,1,0:T(8,128)(2,1)}), bf16[8,32,1152]{2,1,0:T(8,128)(2,1)}, u32[]{:S(2)}, u32[]{:S(2)}) %all-to-all-start) | async-done | bytes 589856 | tf_op jit(solution)/shard_map/all_to_all | solution.py:454
  36.2 14.1 %shard_map.96 = (bf16[8,32,1152]{2,1,0:T(8,128)(2,1)}, bf16[8,32,1152]{2,1,0:T(8,128)(2,1)}) custom-call(bf16[8,32,1152]{2,1,0:T(8,128)(2,1)} %all-to-all-done.hid_in, bf16[8,32,1152]{2,1,0:T(8,128)(2,1)} %bitcast.22, bf16[1152,3456]{1,0:T(8,128)(2,1)} %wq_hbm.4), custom_call_target="tpu_custom_call" | custom-call | flops 5435817984 | bytes 10321920 | tf_op jit(solution)/shard_map/pallas_call | solution.py:351
  50.3 3.7 %shard_map.97 = (bf16[576,1152]{1,0:T(8,128)(2,1)}, bf16[576,1152]{1,0:T(8,128)(2,1)}) custom-call(s32[1]{0:T(128)} %bitcast.core, bf16[256,1152]{1,0:T(8,128)(2,1)} %bitcast.23, bf16[256,1152]{1,0:T(8,128)(2,1)} %bitcast.20), custom_call_target="tpu_custom_call" | custom-call | flops 679477248 | bytes 3833860 | tf_op jit(solution)/shard_map/pallas_call | solution.py:351
  54.0 3.7 %collective-permute-start = (bf16[576,1152]{1,0:T(8,128)(2,1)}, bf16[576,1152]{1,0:T(8,128)(2,1)}, u32[]{:S(2)}, u32[]{:S(2)}) collective-permute-start(bf16[576,1152]{1,0:T(8,128)(2,1)} %get-tuple-element.15), channel_id=1, source_target_pairs={{0,8},{8,0},{16,24},{24,16},{32,40},{40,32},{48,56},{56,48},{64,72... | collective-permute-start | bytes 3981320 | tf_op jit(solution)/shard_map/ppermute | solution.py:467
  57.7 3.5 %all-to-all-start.2 = ((bf16[8,32,1152]{2,1,0:T(8,128)(2,1)}), bf16[8,32,1152]{2,1,0:T(8,128)(2,1)S(1)}, u32[]{:S(2)}, u32[]{:S(2)}) async-start(bf16[8,32,1152]{2,1,0:T(8,128)(2,1)} %get-tuple-element.16), calls=%async_computation.2 | async-start | bytes 1179648 | tf_op jit(solution)/shard_map/all_to_all | solution.py:454
  61.3 0.0 collective-permute-done.got
  61.3 3.4 %shard_map.98 = bf16[64,88,128]{2,1,0:T(8,128)(2,1)} custom-call(bf16[576,1152]{1,0:T(8,128)(2,1)} %get-tuple-element.14.keep, bf16[576,1152]{1,0:T(8,128)(2,1)} %collective-permute-done.got), custom_call_target="tpu_custom_call" | custom-call | flops 169869312 | bytes 4096000 | tf_op jit(solution)/shard_map/pallas_call | solution.py:351
  64.7 7.4 %all-to-all-done.2 = bf16[8,32,1152]{2,1,0:T(8,128)(2,1)S(1)} async-done(((bf16[8,32,1152]{2,1,0:T(8,128)(2,1)}), bf16[8,32,1152]{2,1,0:T(8,128)(2,1)S(1)}, u32[]{:S(2)}, u32[]{:S(2)}) %all-to-all-start.2) | async-done | bytes 589856 | tf_op jit(solution)/shard_map/all_to_all | solution.py:454
  72.0 0.0 copy-start.1
  72.0 9.4 %all-to-all-start.3 = ((bf16[64,88,128]{2,1,0:T(8,128)(2,1)}), bf16[64,88,128]{2,1,0:T(8,128)(2,1)}, u32[]{:S(2)}, u32[]{:S(2)}) async-start(bf16[64,88,128]{2,1,0:T(8,128)(2,1)} %shard_map.98), calls=%async_computation.3 | async-start | bytes 2883584 | tf_op jit(solution)/shard_map/all_to_all | solution.py:473
  81.4 0.0 copy-done.1
  81.4 15.3 %shard_map.99 = bf16[256,1152]{1,0:T(8,128)(2,1)} custom-call(bf16[256,1152]{1,0:T(8,128)(2,1)} %bitcast.15, f32[256,1152]{1,0:T(8,128)} %get-tuple-element.18.stream_hbm, f32[1152]{0:T(1024)} %gt.3, bf16[256,1152]{1,0:T(8,128)(2,1)} %bitcast.14, bf16[256,3456]{1,0:T(8,128)(2,1)} %get-tuple-element.19.qkv_hbm, ...), custom_call_target="tpu_custom_call" | custom-call | flops 4756340736 | bytes 18031616 | tf_op jit(solution)/shard_map/pallas_call | solution.py:351
  96.8 5.1 %all-to-all-done.3.got_ref = bf16[64,88,128]{2,1,0:T(8,128)(2,1)} async-done(((bf16[64,88,128]{2,1,0:T(8,128)(2,1)}), bf16[64,88,128]{2,1,0:T(8,128)(2,1)}, u32[]{:S(2)}, u32[]{:S(2)}) %all-to-all-start.3) | async-done | bytes 1441824 | tf_op jit(solution)/shard_map/all_to_all | solution.py:473
  101.9 2.3 %shard_map.100 = f32[9,1152]{1,0:T(8,128)} custom-call(s32[1]{0:T(128)} %bitcast.10.owner_ref, bf16[64,88,128]{2,1,0:T(8,128)(2,1)} %all-to-all-done.3.got_ref), custom_call_target="tpu_custom_call" | custom-call | flops 1000 | bytes 1483268 | tf_op jit(solution)/shard_map/pallas_call | solution.py:351
Async XLA Ops:
  0.6 26.4 %copy-start = (bf16[1152,1152]{1,0:T(8,128)(2,1)S(1)}, bf16[1152,1152]{1,0:T(8,128)(2,1)}, u32[]{:S(2)}) copy-start(bf16[1152,1152]{1,0:T(8,128)(2,1)} %param.15) | copy-start | bytes 7962628
  0.6 19.7 %all-to-all-start.1 = ((bf16[8,32,1152]{2,1,0:T(8,128)(2,1)}), bf16[8,32,1152]{2,1,0:T(8,128)(2,1)S(1)}, u32[]{:S(2)}, u32[]{:S(2)}) async-start(bf16[8,32,1152]{2,1,0:T(8,128)(2,1)} %bitcast.13), calls=%async_computation.1 | async-start | bytes 1179648 | tf_op jit(solution)/shard_map/all_to_all | solution.py:454
  20.4 8.5 %copy-start.2 = (bf16[8,32,1152]{2,1,0:T(8,128)(2,1)}, bf16[8,32,1152]{2,1,0:T(8,128)(2,1)S(1)}, u32[]{:S(2)}) copy-start(bf16[8,32,1152]{2,1,0:T(8,128)(2,1)S(1)} %all-to-all-done.1) | copy-start | bytes 1769476
  20.4 15.8 %all-to-all-start = ((bf16[8,32,1152]{2,1,0:T(8,128)(2,1)}), bf16[8,32,1152]{2,1,0:T(8,128)(2,1)}, u32[]{:S(2)}, u32[]{:S(2)}) async-start(bf16[8,32,1152]{2,1,0:T(8,128)(2,1)} %bitcast.21), calls=%async_computation | async-start | bytes 1179648 | tf_op jit(solution)/shard_map/all_to_all | solution.py:454
  54.0 7.3 %collective-permute-start = (bf16[576,1152]{1,0:T(8,128)(2,1)}, bf16[576,1152]{1,0:T(8,128)(2,1)}, u32[]{:S(2)}, u32[]{:S(2)}) collective-permute-start(bf16[576,1152]{1,0:T(8,128)(2,1)} %get-tuple-element.15), channel_id=1, source_target_pairs={{0,8},{8,0},{16,24},{24,16},{32,40},{40,32},{48,56},{56,48},{64,72... | collective-permute-start | bytes 3981320 | tf_op jit(solution)/shard_map/ppermute | solution.py:467
  57.7 14.3 %all-to-all-start.2 = ((bf16[8,32,1152]{2,1,0:T(8,128)(2,1)}), bf16[8,32,1152]{2,1,0:T(8,128)(2,1)S(1)}, u32[]{:S(2)}, u32[]{:S(2)}) async-start(bf16[8,32,1152]{2,1,0:T(8,128)(2,1)} %get-tuple-element.16), calls=%async_computation.2 | async-start | bytes 1179648 | tf_op jit(solution)/shard_map/all_to_all | solution.py:454
  72.0 9.4 %copy-start.1 = (bf16[8,32,1152]{2,1,0:T(8,128)(2,1)}, bf16[8,32,1152]{2,1,0:T(8,128)(2,1)S(1)}, u32[]{:S(2)}) copy-start(bf16[8,32,1152]{2,1,0:T(8,128)(2,1)S(1)} %all-to-all-done.2) | copy-start | bytes 1769476
  72.0 29.9 %all-to-all-start.3 = ((bf16[64,88,128]{2,1,0:T(8,128)(2,1)}), bf16[64,88,128]{2,1,0:T(8,128)(2,1)}, u32[]{:S(2)}, u32[]{:S(2)}) async-start(bf16[64,88,128]{2,1,0:T(8,128)(2,1)} %shard_map.98), calls=%async_computation.3 | async-start | bytes 2883584 | tf_op jit(solution)/shard_map/all_to_all | solution.py:473

commit v3 on v2

--- a/solution.py
+++ b/solution.py
@@ -283,53 +283,45 @@
 
 
 GROUPS = DP // 2
-PER_CORE = GROUPS * HD
-
-
-def outer_product(core, mixed, og, keep, send, full):
+
+
+SUB = 8
+
+
+def outer_product(core, mixed, other_mixed, og, other_og, out, m, g, full, sems):
+    copies = [
+        fetch(mixed, m.at[:T, :], sems.at[0]),
+        fetch(og, g.at[:T, :], sems.at[1]),
+        fetch(other_mixed, m.at[T:, :], sems.at[2]),
+        fetch(other_og, g.at[T:, :], sems.at[3]),
+    ]
+    for copy in copies:
+        copy.wait()
     step = 3 * LANES
     for c in range(D // step):
-        full[c * step : (c + 1) * step, :] = tn(mixed[:, c * step : (c + 1) * step], og[...])
-    first = core[0] == 0
-    for g in range(0, GROUPS, 2):
-        even, odd = (
-            jnp.concatenate(
-                [full[(2 * (g + i) + c) * HD : (2 * (g + i) + c + 1) * HD, :] for i in range(2)]
-            )
-            for c in range(2)
-        )
-        rows = slice(g * HD, (g + 2) * HD)
-        keep[rows, :] = jnp.where(first, even, odd).astype(BF)
-        send[rows, :] = jnp.where(first, odd, even).astype(BF)
-
-
-SUB = 8
-
-
-def add_and_cut(keep, got, out, block):
+        full[c * step : (c + 1) * step, :] = tn(m[:, c * step : (c + 1) * step], g[...])
     place = lax.broadcasted_iota(jnp.int32, (SUB, 1), 0)
 
-    def body(g, carry):
-        rows = pl.ds(pl.multiple_of(g * 2 * HD, 2 * HD), 2 * HD)
-        block[...] = keep[rows, :].astype(F32) + got[rows, :].astype(F32)
-        for i in range(2):
-            for j in range(SEQ):
-                at = i * HD + j * SUB
-                upper, lower = block[at : at + SUB, :], block[at + SUB : at + 2 * SUB, :]
-                eight = jnp.where(place >= j, upper, lower)
-                ninth = lower[j : j + 1, :]
-                parts = [eight[:, t * LANES : (t + 1) * LANES] for t in range(TILES)]
-                for first in (0, SUB):
-                    rest = jnp.zeros((SUB, LANES), F32)
-                    for t in range(first, min(first + SUB, TILES)):
-                        rest = jnp.where(
-                            place == t - first, ninth[:, t * LANES : (t + 1) * LANES], rest
-                        )
-                    parts.append(rest)
-                out[(g * 2 + i) * SEQ + j] = jnp.concatenate(parts).astype(BF)
+    def body(i, carry):
+        base = (2 * i + core[0]) * HD
+        for j in range(SEQ):
+            at = base + j * SUB
+            upper = full[pl.ds(pl.multiple_of(at, SUB), SUB), :]
+            lower = full[pl.ds(pl.multiple_of(at + SUB, SUB), SUB), :]
+            eight = jnp.where(place >= j, upper, lower)
+            ninth = lower[j : j + 1, :]
+            parts = [eight[:, t * LANES : (t + 1) * LANES] for t in range(TILES)]
+            for first in (0, SUB):
+                rest = jnp.zeros((SUB, LANES), F32)
+                for t in range(first, min(first + SUB, TILES)):
+                    rest = jnp.where(
+                        place == t - first, ninth[:, t * LANES : (t + 1) * LANES], rest
+                    )
+                parts.append(rest)
+            out[i * SEQ + j] = jnp.concatenate(parts).astype(BF)
         return carry
 
-    lax.fori_loop(0, GROUPS // 2, body, 0)
+    lax.fori_loop(0, GROUPS, body, 0)
 
 
 def sum_chunks(owner, got, out, total, *, scale):
@@ -400,24 +392,15 @@
     )[0]
 
 
-def run_outer_product(core, mixed, og):
+def run_outer_product(core, mixed, other_mixed, og, other_og):
+    pair = VMEM((2 * T, D), BF)
     return call(
         outer_product,
-        [((PER_CORE, D), BF), ((PER_CORE, D), BF)],
-        (core, mixed, og),
-        [VMEM((D, D), F32)],
-        UNIT,
-        [pltpu.SMEM, VMEM, VMEM],
-    )
-
-
-def run_add_and_cut(keep, got):
-    return call(
-        add_and_cut,
         [((GROUPS * SEQ, CHUNK, LANES), BF)],
-        (keep, got),
-        [VMEM((2 * HD, D), F32)],
-        UNIT // 4,
+        (core, mixed, other_mixed, og, other_og),
+        [pair, pair, VMEM((D, D), F32), DMA((4,))],
+        2 * UNIT,
+        [pltpu.SMEM, ANY, ANY, ANY, ANY],
     )[0]
 
 
@@ -453,7 +436,11 @@
     def exchange(x):
         return lax.all_to_all(x.reshape(SEQ, POS, D), "seq", 0, 0, tiled=True)
 
+    def swap(x):
+        return lax.ppermute(x, "dp", [(i, i ^ 1) for i in range(DP)])
+
     og_pos = exchange(og)
+    other_og = swap(og_pos)
     hid, stream, qkv, prob = run_spatial_forward(
         clip, gain_spatial, gain_temporal, w_spatial_qkv, w_spatial_out
     )
@@ -463,9 +450,10 @@
     dhid = exchange(dhid_pos).reshape(T, D)
 
     core = lax.rem(lax.axis_index("dp"), 2).reshape(1)
-    keep, send = run_outer_product(core, mixed_pos.reshape(T, D), og_pos.reshape(T, D))
-    got = lax.ppermute(send, "dp", [(i, i ^ 1) for i in range(DP)])
-    chunks = run_add_and_cut(keep, got)
+    other_mixed = swap(mixed_pos)
+    chunks = run_outer_product(
+        core, *(x.reshape(T, D) for x in (mixed_pos, other_mixed, og_pos, other_og))
+    )
     chunks, dhid = lax.optimization_barrier((chunks, dhid))
     owners = [
         [(g * 2 + c) * SEQ + s for g in range(GROUPS) for s in range(SEQ)] for c in range(2)

time: 105 us -> 102 us (0.971)
  waiting for transfers between devices: 19.7 us -> 15.6 us
  Pallas kernels: 50.8 us -> 48.6 us
  starting transfers between devices: 31 us -> 32.7 us
  matrix products: 1.86 us -> 2.92 us
    all_to_all x3, waiting for transfers between devices: 14.6 us -> 10.4 us  [exchange(): return lax.all_to_all(x.reshape(SEQ, POS, D), 'seq', 0, 0, tiled=True)]
    pallas_call x6 -> x5, Pallas kernels: 50.8 us -> 48.6 us  [call(): pl.pallas_call(fn, out_shape=[jax.ShapeDtypeStruct(s, d) for s, d in outs...]
    ppermute x1 -> x2, starting transfers between devices: 3.75 us -> 5.34 us  [swap(): return lax.ppermute(x, 'dp', [(i, i ^ 1) for i in range(DP)])]
    dot_general x1, matrix products: 1.86 us -> 2.92 us  [nt(): lax.dot_general(a, b, (((1,), (1,)), ((), ())), preferred_element_type=F32)]
  transfers between devices with their start and end apart: 5 -> 6, of which waited for: 3 -> 3; matrix products, arithmetic and copies ran while one was open for 2% -> 3% of each run, Pallas kernels for 29% -> 46%
where the time goes in v3:
time: 102 us; the launch traced here: 101 us
  Pallas kernels  48.6 us (48%)
  starting transfers between devices  32.7 us (32%)
  waiting for transfers between devices  15.6 us (15%)
  matrix products  2.92 us (3%)
    pallas_call x5, Pallas kernels, call(): pl.pallas_call(fn, out_shape=[jax.ShapeDtypeStruct(s, d) for s, d in outs...  48.6 us
    all_to_all x3, starting transfers between devices, exchange(): return lax.all_to_all(x.reshape(SEQ, POS, D), 'seq', 0, 0, tiled=True)  17.9 us
    all_to_all x3, waiting for transfers between devices, exchange(): return lax.all_to_all(x.reshape(SEQ, POS, D), 'seq', 0, 0, tiled=True)  10.4 us
    all_to_all x1, starting transfers between devices, per_device(): lax.all_to_all(chunks, ('dp', 'seq'), 0, 0, axis_index_groups=owners, til...  9.37 us
    ppermute x2, starting transfers between devices, swap(): return lax.ppermute(x, 'dp', [(i, i ^ 1) for i in range(DP)])  5.34 us
    all_to_all x1, waiting for transfers between devices, per_device(): lax.all_to_all(chunks, ('dp', 'seq'), 0, 0, axis_index_groups=owners, til...  5.14 us
    dot_general x1, matrix products, nt(): lax.dot_general(a, b, (((1,), (1,)), ((), ())), preferred_element_type=F32)  2.92 us
  transfers between devices with their start and end apart: 6, of which 3 were waited for; matrix products, arithmetic and copies ran while one was open for 3% of the time, Pallas kernels for 46%

profile of v3, /device:TPU:1, one launch (start us, length us, event | category | flops | bytes accessed | tf_op | source)
XLA Modules:
  0.0 101.3 jit_solution(8949879039425786004)
XLA Ops:
  0.6 0.0 copy-start
  0.6 7.7 %all-to-all-start.1 = ((bf16[8,32,1152]{2,1,0:T(8,128)(2,1)}), bf16[8,32,1152]{2,1,0:T(8,128)(2,1)}, u32[]{:S(2)}, u32[]{:S(2)}) async-start(bf16[8,32,1152]{2,1,0:T(8,128)(2,1)} %bitcast.15), calls=%async_computation.1 | async-start | bytes 1179648 | tf_op jit(solution)/shard_map/all_to_all | solution.py:437
  8.4 12.0 %shard_map.95 = (bf16[256,1152]{1,0:T(8,128)(2,1)}, f32[256,1152]{1,0:T(8,128)}, bf16[256,3456]{1,0:T(8,128)(2,1)}, bf16[16,256,256]{2,1,0:T(8,128)(2,1)}) custom-call(bf16[256,1152]{1,0:T(8,128)(2,1)} %bitcast.18, f32[1152]{0:T(1024)} %gs.3, f32[1152]{0:T(1024)} %gt.3, bf16[1152,3456]{1,0:T(8,128)(2,1)} %wq_hbm.5, bf16[1152,1152]{1,0:T(8,128)(2,1)} %wo_hbm.3), custom_call_target="tpu_custom_call" | custom-call | flops 3397386240 | bytes 16851968 | tf_op jit(solution)/shard_map/pallas_call | solution.py:343
  20.4 0.0 all-to-all-done.1
  20.4 6.7 %all-to-all-start = ((bf16[8,32,1152]{2,1,0:T(8,128)(2,1)}), bf16[8,32,1152]{2,1,0:T(8,128)(2,1)S(1)}, u32[]{:S(2)}, u32[]{:S(2)}) async-start(bf16[8,32,1152]{2,1,0:T(8,128)(2,1)} %bitcast.21), calls=%async_computation | async-start | bytes 1179648 | tf_op jit(solution)/shard_map/all_to_all | solution.py:437
  27.0 1.5 %collective-permute-start.1 = (bf16[8,32,1152]{2,1,0:T(8,128)(2,1)}, bf16[8,32,1152]{2,1,0:T(8,128)(2,1)}, u32[]{:S(2)}, u32[]{:S(2)}) collective-permute-start(bf16[8,32,1152]{2,1,0:T(8,128)(2,1)} %all-to-all-done.1), channel_id=1, source_target_pairs={{0,8},{8,0},{16,24},{24,16},{32,40},{40,32},{48,56},{56,48},{64,72... | collective-permute-start | bytes 1769480 | tf_op jit(solution)/shard_map/ppermute | solution.py:440
  28.6 0.0 copy-done
  28.6 2.9 %convolution_convert_fusion = bf16[256,1152]{1,0:T(8,128)(2,1)} fusion(bf16[256,1152]{1,0:T(8,128)(2,1)} %bitcast.4.og, bf16[1152,1152]{1,0:T(8,128)(2,1)S(1)} %copy-done), kind=kOutput, calls=%fused_computation | convolution fusion | flops 679772160 | bytes 3833856 | tf_op jit(solution)/shard_map/dot_general | solution.py:39
  31.5 4.6 %all-to-all-done.hid_in = bf16[8,32,1152]{2,1,0:T(8,128)(2,1)S(1)} async-done(((bf16[8,32,1152]{2,1,0:T(8,128)(2,1)}), bf16[8,32,1152]{2,1,0:T(8,128)(2,1)S(1)}, u32[]{:S(2)}, u32[]{:S(2)}) %all-to-all-start) | async-done | bytes 589856 | tf_op jit(solution)/shard_map/all_to_all | solution.py:437
  36.0 0.0 copy-start.2
  36.0 0.8 copy-done.2
  36.9 14.2 %shard_map.96 = (bf16[8,32,1152]{2,1,0:T(8,128)(2,1)}, bf16[8,32,1152]{2,1,0:T(8,128)(2,1)}) custom-call(bf16[8,32,1152]{2,1,0:T(8,128)(2,1)} %copy-done.2, bf16[8,32,1152]{2,1,0:T(8,128)(2,1)} %bitcast.23, bf16[1152,3456]{1,0:T(8,128)(2,1)} %wq_hbm.4), custom_call_target="tpu_custom_call" | custom-call | flops 5435817984 | bytes 10321920 | tf_op jit(solution)/shard_map/pallas_call | solution.py:343
  51.1 3.8 %collective-permute-start = (bf16[8,32,1152]{2,1,0:T(8,128)(2,1)}, bf16[8,32,1152]{2,1,0:T(8,128)(2,1)}, u32[]{:S(2)}, u32[]{:S(2)}) collective-permute-start(bf16[8,32,1152]{2,1,0:T(8,128)(2,1)} %get-tuple-element.11), channel_id=1, source_target_pairs={{0,8},{8,0},{16,24},{24,16},{32,40},{40,32},{48,56},{56,48},{64,72... | collective-permute-start | bytes 1769480 | tf_op jit(solution)/shard_map/ppermute | solution.py:440
  54.9 3.5 %all-to-all-start.2 = ((bf16[8,32,1152]{2,1,0:T(8,128)(2,1)}), bf16[8,32,1152]{2,1,0:T(8,128)(2,1)S(1)}, u32[]{:S(2)}, u32[]{:S(2)}) async-start(bf16[8,32,1152]{2,1,0:T(8,128)(2,1)} %get-tuple-element.12), calls=%async_computation.2 | async-start | bytes 1179648 | tf_op jit(solution)/shard_map/all_to_all | solution.py:437
  58.4 0.0 collective-permute-done.1
  58.4 0.0 collective-permute-done
  58.5 4.8 %shard_map.97 = bf16[64,88,128]{2,1,0:T(8,128)(2,1)} custom-call(s32[1]{0:T(128)} %bitcast.core, bf16[256,1152]{1,0:T(8,128)(2,1)} %bitcast.22, bf16[256,1152]{1,0:T(8,128)(2,1)} %bitcast.7.other_mixed, bf16[256,1152]{1,0:T(8,128)(2,1)} %bitcast.4.og, bf16[256,1152]{1,0:T(8,128)(2,1)} %bitcast.8.other_og), custom_call_target="tpu_custom_call" | custom-call | flops 1358954496 | bytes 3801092 | tf_op jit(solution)/shard_map/pallas_call | solution.py:343
  63.3 5.8 %all-to-all-done.2 = bf16[8,32,1152]{2,1,0:T(8,128)(2,1)S(1)} async-done(((bf16[8,32,1152]{2,1,0:T(8,128)(2,1)}), bf16[8,32,1152]{2,1,0:T(8,128)(2,1)S(1)}, u32[]{:S(2)}, u32[]{:S(2)}) %all-to-all-start.2) | async-done | bytes 589856 | tf_op jit(solution)/shard_map/all_to_all | solution.py:437
  69.1 0.0 copy-start.1
  69.1 9.4 %all-to-all-start.3 = ((bf16[64,88,128]{2,1,0:T(8,128)(2,1)}), bf16[64,88,128]{2,1,0:T(8,128)(2,1)}, u32[]{:S(2)}, u32[]{:S(2)}) async-start(bf16[64,88,128]{2,1,0:T(8,128)(2,1)} %shard_map.97), calls=%async_computation.3 | async-start | bytes 2883584 | tf_op jit(solution)/shard_map/all_to_all | solution.py:461
  78.5 0.0 copy-done.1
  78.5 15.3 %shard_map.98 = bf16[256,1152]{1,0:T(8,128)(2,1)} custom-call(bf16[256,1152]{1,0:T(8,128)(2,1)} %bitcast.17, f32[256,1152]{1,0:T(8,128)} %get-tuple-element.14.stream_hbm, f32[1152]{0:T(1024)} %gt.3, bf16[256,1152]{1,0:T(8,128)(2,1)} %bitcast.16, bf16[256,3456]{1,0:T(8,128)(2,1)} %get-tuple-element.15.qkv_hbm, ...), custom_call_target="tpu_custom_call" | custom-call | flops 4756340736 | bytes 18031616 | tf_op jit(solution)/shard_map/pallas_call | solution.py:343
  93.9 5.1 %all-to-all-done.3.got_ref = bf16[64,88,128]{2,1,0:T(8,128)(2,1)} async-done(((bf16[64,88,128]{2,1,0:T(8,128)(2,1)}), bf16[64,88,128]{2,1,0:T(8,128)(2,1)}, u32[]{:S(2)}, u32[]{:S(2)}) %all-to-all-start.3) | async-done | bytes 1441824 | tf_op jit(solution)/shard_map/all_to_all | solution.py:461
  99.0 2.3 %shard_map.99 = f32[9,1152]{1,0:T(8,128)} custom-call(s32[1]{0:T(128)} %bitcast.12.owner_ref, bf16[64,88,128]{2,1,0:T(8,128)(2,1)} %all-to-all-done.3.got_ref), custom_call_target="tpu_custom_call" | custom-call | flops 1000 | bytes 1483268 | tf_op jit(solution)/shard_map/pallas_call | solution.py:343
Async XLA Ops:
  0.6 27.9 %copy-start = (bf16[1152,1152]{1,0:T(8,128)(2,1)S(1)}, bf16[1152,1152]{1,0:T(8,128)(2,1)}, u32[]{:S(2)}) copy-start(bf16[1152,1152]{1,0:T(8,128)(2,1)} %param.15) | copy-start | bytes 7962628
  0.6 19.7 %all-to-all-start.1 = ((bf16[8,32,1152]{2,1,0:T(8,128)(2,1)}), bf16[8,32,1152]{2,1,0:T(8,128)(2,1)}, u32[]{:S(2)}, u32[]{:S(2)}) async-start(bf16[8,32,1152]{2,1,0:T(8,128)(2,1)} %bitcast.15), calls=%async_computation.1 | async-start | bytes 1179648 | tf_op jit(solution)/shard_map/all_to_all | solution.py:437
  20.4 15.7 %all-to-all-start = ((bf16[8,32,1152]{2,1,0:T(8,128)(2,1)}), bf16[8,32,1152]{2,1,0:T(8,128)(2,1)S(1)}, u32[]{:S(2)}, u32[]{:S(2)}) async-start(bf16[8,32,1152]{2,1,0:T(8,128)(2,1)} %bitcast.21), calls=%async_computation | async-start | bytes 1179648 | tf_op jit(solution)/shard_map/all_to_all | solution.py:437
  27.0 31.4 %collective-permute-start.1 = (bf16[8,32,1152]{2,1,0:T(8,128)(2,1)}, bf16[8,32,1152]{2,1,0:T(8,128)(2,1)}, u32[]{:S(2)}, u32[]{:S(2)}) collective-permute-start(bf16[8,32,1152]{2,1,0:T(8,128)(2,1)} %all-to-all-done.1), channel_id=1, source_target_pairs={{0,8},{8,0},{16,24},{24,16},{32,40},{40,32},{48,56},{56,48},{64,72... | collective-permute-start | bytes 1769480 | tf_op jit(solution)/shard_map/ppermute | solution.py:440
  36.0 0.8 copy-start.2
  51.1 7.4 %collective-permute-start = (bf16[8,32,1152]{2,1,0:T(8,128)(2,1)}, bf16[8,32,1152]{2,1,0:T(8,128)(2,1)}, u32[]{:S(2)}, u32[]{:S(2)}) collective-permute-start(bf16[8,32,1152]{2,1,0:T(8,128)(2,1)} %get-tuple-element.11), channel_id=1, source_target_pairs={{0,8},{8,0},{16,24},{24,16},{32,40},{40,32},{48,56},{56,48},{64,72... | collective-permute-start | bytes 1769480 | tf_op jit(solution)/shard_map/ppermute | solution.py:440
  54.9 14.3 %all-to-all-start.2 = ((bf16[8,32,1152]{2,1,0:T(8,128)(2,1)}), bf16[8,32,1152]{2,1,0:T(8,128)(2,1)S(1)}, u32[]{:S(2)}, u32[]{:S(2)}) async-start(bf16[8,32,1152]{2,1,0:T(8,128)(2,1)} %get-tuple-element.12), calls=%async_computation.2 | async-start | bytes 1179648 | tf_op jit(solution)/shard_map/all_to_all | solution.py:437
  69.1 9.4 %copy-start.1 = (bf16[8,32,1152]{2,1,0:T(8,128)(2,1)}, bf16[8,32,1152]{2,1,0:T(8,128)(2,1)S(1)}, u32[]{:S(2)}) copy-start(bf16[8,32,1152]{2,1,0:T(8,128)(2,1)S(1)} %all-to-all-done.2) | copy-start | bytes 1769476
  69.1 29.9 %all-to-all-start.3 = ((bf16[64,88,128]{2,1,0:T(8,128)(2,1)}), bf16[64,88,128]{2,1,0:T(8,128)(2,1)}, u32[]{:S(2)}, u32[]{:S(2)}) async-start(bf16[64,88,128]{2,1,0:T(8,128)(2,1)} %shard_map.97), calls=%async_computation.3 | async-start | bytes 2883584 | tf_op jit(solution)/shard_map/all_to_all | solution.py:461

commit v4 on v3

--- a/solution.py
+++ b/solution.py
@@ -55,7 +55,7 @@
         fn(pl.ds(pl.multiple_of(i * ROWS, ROWS), ROWS))
         return carry
 
-    lax.fori_loop(0, T // ROWS, body, 0)
+    lax.fori_loop(0, T // ROWS, body, 0, unroll=4)
 
 
 def norm_back(x, g, dy):
@@ -116,6 +116,16 @@
         dst[:, base + t * LANES : base + (t + 1) * LANES] = total
 
 
+def project_back(slots, grad, weight):
+    total = None
+    for i, section in enumerate(slots):
+        merge(section, grad, i * D)
+        cols = slice(i * D, (i + 1) * D)
+        part = nt(grad[:, cols], weight[:, cols])
+        total = part if total is None else total + part
+    return total
+
+
 def fetch(src, dst, sem):
     copy = pltpu.make_async_copy(src, dst, sem)
     copy.start()
@@ -178,7 +188,7 @@
 
 
 def temporal(hid_in, dmix_in, wq_hbm, mixed_out, dhid_out,
-             wq, hid, dmix, qkv, mix, dqkv, o_slots, q_slots, k_slots, v_slots, sems):
+             wq, hid, dmix, qkv, mix, dqkv, dh, o_slots, q_slots, k_slots, v_slots, sems):
     wq_copies = fetch_columns(wq_hbm, wq, sems)
     for b in range(2):
         part = slice(b * HALF, (b + 1) * HALF)
@@ -219,9 +229,7 @@
 
     heads_loop(head, rest)
     merge(o_slots, mix)
-    for i, slots in enumerate((q_slots, k_slots, v_slots)):
-        merge(slots, dqkv, i * D)
-    dh = nt(dqkv[...], wq[...]).astype(BF)
+    dh[...] = project_back((q_slots, k_slots, v_slots), dqkv, wq).astype(BF)
     for b in range(2):
         part = slice(b * HALF, (b + 1) * HALF)
         rows = slice(b * BLK, (b + 1) * BLK)
@@ -269,10 +277,8 @@
         q_slots[h] = tn(ds, k).astype(BF)
 
     heads_loop(head, rest)
-    for i, slots in enumerate((q_slots, k_slots, v_slots)):
-        merge(slots, dqkv, i * D)
     copies[6].wait()
-    dh[...] = nt(dqkv[...], wq[...]).astype(BF)
+    dh[...] = project_back((q_slots, k_slots, v_slots), dqkv, wq).astype(BF)
     copies[7].wait()
 
     def video_grad(rows):
@@ -374,7 +380,7 @@
         temporal,
         [((SEQ, POS, D), BF), ((SEQ, POS, D), BF)],
         (hid, dmix, wq),
-        [WIDE, TOK, TOK, TOK3, TOK, TOK3, SLOTS, SLOTS, SLOTS, SLOTS, DMA((4,))],
+        [WIDE, TOK, TOK, TOK3, TOK, TOK3, TOK, SLOTS, SLOTS, SLOTS, SLOTS, DMA((4,))],
         8 * UNIT,
         [VMEM, VMEM, ANY],
     )

time: 102 us -> 102 us (level)
  Pallas kernels: 48.6 us -> 44.5 us
  waiting for transfers between devices: 15.6 us -> 18.8 us
    pallas_call x5, Pallas kernels: 48.6 us -> 44.5 us  [call(): pl.pallas_call(fn, out_shape=[jax.ShapeDtypeStruct(s, d) for s, d in outs...]
    all_to_all x1, waiting for transfers between devices: 5.14 us -> 8.38 us  [per_device(): lax.all_to_all(chunks, ('dp', 'seq'), 0, 0, axis_index_groups=owners, til...]
  transfers between devices with their start and end apart: 6 -> 6, of which waited for: 3 -> 3; matrix products, arithmetic and copies ran while one was open for 3% -> 3% of each run, Pallas kernels for 46% -> 42%
where the time goes in v4:
time: 102 us; the launch traced here: 100 us
  Pallas kernels  44.5 us (44%)
  starting transfers between devices  32.7 us (32%)
  waiting for transfers between devices  18.8 us (18%)
  matrix products  2.93 us (3%)
    pallas_call x5, Pallas kernels, call(): pl.pallas_call(fn, out_shape=[jax.ShapeDtypeStruct(s, d) for s, d in outs...  44.5 us
    all_to_all x3, starting transfers between devices, exchange(): return lax.all_to_all(x.reshape(SEQ, POS, D), 'seq', 0, 0, tiled=True)  17.9 us
    all_to_all x3, waiting for transfers between devices, exchange(): return lax.all_to_all(x.reshape(SEQ, POS, D), 'seq', 0, 0, tiled=True)  10.4 us
    all_to_all x1, starting transfers between devices, per_device(): lax.all_to_all(chunks, ('dp', 'seq'), 0, 0, axis_index_groups=owners, til...  9.37 us
    all_to_all x1, waiting for transfers between devices, per_device(): lax.all_to_all(chunks, ('dp', 'seq'), 0, 0, axis_index_groups=owners, til...  8.38 us
    ppermute x2, starting transfers between devices, swap(): return lax.ppermute(x, 'dp', [(i, i ^ 1) for i in range(DP)])  5.34 us
    dot_general x1, matrix products, nt(): lax.dot_general(a, b, (((1,), (1,)), ((), ())), preferred_element_type=F32)  2.93 us
  transfers between devices with their start and end apart: 6, of which 3 were waited for; matrix products, arithmetic and copies ran while one was open for 3% of the time, Pallas kernels for 42%

profile of v4, /device:TPU:1, one launch (start us, length us, event | category | flops | bytes accessed | tf_op | source)
XLA Modules:
  0.0 100.5 jit_solution(13215262470123905054)
XLA Ops:
  0.6 0.0 copy-start
  0.6 7.7 %all-to-all-start.1 = ((bf16[8,32,1152]{2,1,0:T(8,128)(2,1)}), bf16[8,32,1152]{2,1,0:T(8,128)(2,1)}, u32[]{:S(2)}, u32[]{:S(2)}) async-start(bf16[8,32,1152]{2,1,0:T(8,128)(2,1)} %bitcast.15), calls=%async_computation.1 | async-start | bytes 1179648 | tf_op jit(solution)/shard_map/all_to_all | solution.py:443
  8.4 11.3 %shard_map.95 = (bf16[256,1152]{1,0:T(8,128)(2,1)}, f32[256,1152]{1,0:T(8,128)}, bf16[256,3456]{1,0:T(8,128)(2,1)}, bf16[16,256,256]{2,1,0:T(8,128)(2,1)}) custom-call(bf16[256,1152]{1,0:T(8,128)(2,1)} %bitcast.18, f32[1152]{0:T(1024)} %gs.3, f32[1152]{0:T(1024)} %gt.3, bf16[1152,3456]{1,0:T(8,128)(2,1)} %wq_hbm.5, bf16[1152,1152]{1,0:T(8,128)(2,1)} %wo_hbm.3), custom_call_target="tpu_custom_call" | custom-call | flops 3397386240 | bytes 16851968 | tf_op jit(solution)/shard_map/pallas_call | solution.py:349
  19.7 0.0 all-to-all-done.1
  19.7 6.7 %all-to-all-start = ((bf16[8,32,1152]{2,1,0:T(8,128)(2,1)}), bf16[8,32,1152]{2,1,0:T(8,128)(2,1)S(1)}, u32[]{:S(2)}, u32[]{:S(2)}) async-start(bf16[8,32,1152]{2,1,0:T(8,128)(2,1)} %bitcast.21), calls=%async_computation | async-start | bytes 1179648 | tf_op jit(solution)/shard_map/all_to_all | solution.py:443
  26.4 1.5 %collective-permute-start.1 = (bf16[8,32,1152]{2,1,0:T(8,128)(2,1)}, bf16[8,32,1152]{2,1,0:T(8,128)(2,1)}, u32[]{:S(2)}, u32[]{:S(2)}) collective-permute-start(bf16[8,32,1152]{2,1,0:T(8,128)(2,1)} %all-to-all-done.1), channel_id=1, source_target_pairs={{0,8},{8,0},{16,24},{24,16},{32,40},{40,32},{48,56},{56,48},{64,72... | collective-permute-start | bytes 1769480 | tf_op jit(solution)/shard_map/ppermute | solution.py:446
  27.9 0.0 copy-done
  27.9 2.9 %convolution_convert_fusion = bf16[256,1152]{1,0:T(8,128)(2,1)} fusion(bf16[256,1152]{1,0:T(8,128)(2,1)} %bitcast.4.og, bf16[1152,1152]{1,0:T(8,128)(2,1)S(1)} %copy-done), kind=kOutput, calls=%fused_computation | convolution fusion | flops 679772160 | bytes 3833856 | tf_op jit(solution)/shard_map/dot_general | solution.py:39
  30.8 4.6 %all-to-all-done.hid_in = bf16[8,32,1152]{2,1,0:T(8,128)(2,1)S(1)} async-done(((bf16[8,32,1152]{2,1,0:T(8,128)(2,1)}), bf16[8,32,1152]{2,1,0:T(8,128)(2,1)S(1)}, u32[]{:S(2)}, u32[]{:S(2)}) %all-to-all-start) | async-done | bytes 589856 | tf_op jit(solution)/shard_map/all_to_all | solution.py:443
  35.4 0.0 copy-start.2
  35.4 0.8 copy-done.2
  36.2 14.0 %shard_map.96 = (bf16[8,32,1152]{2,1,0:T(8,128)(2,1)}, bf16[8,32,1152]{2,1,0:T(8,128)(2,1)}) custom-call(bf16[8,32,1152]{2,1,0:T(8,128)(2,1)} %copy-done.2, bf16[8,32,1152]{2,1,0:T(8,128)(2,1)} %bitcast.23, bf16[1152,3456]{1,0:T(8,128)(2,1)} %wq_hbm.4), custom_call_target="tpu_custom_call" | custom-call | flops 5435817984 | bytes 10321920 | tf_op jit(solution)/shard_map/pallas_call | solution.py:349
  50.2 3.8 %collective-permute-start = (bf16[8,32,1152]{2,1,0:T(8,128)(2,1)}, bf16[8,32,1152]{2,1,0:T(8,128)(2,1)}, u32[]{:S(2)}, u32[]{:S(2)}) collective-permute-start(bf16[8,32,1152]{2,1,0:T(8,128)(2,1)} %get-tuple-element.11), channel_id=1, source_target_pairs={{0,8},{8,0},{16,24},{24,16},{32,40},{40,32},{48,56},{56,48},{64,72... | collective-permute-start | bytes 1769480 | tf_op jit(solution)/shard_map/ppermute | solution.py:446
  54.0 3.5 %all-to-all-start.2 = ((bf16[8,32,1152]{2,1,0:T(8,128)(2,1)}), bf16[8,32,1152]{2,1,0:T(8,128)(2,1)S(1)}, u32[]{:S(2)}, u32[]{:S(2)}) async-start(bf16[8,32,1152]{2,1,0:T(8,128)(2,1)} %get-tuple-element.12), calls=%async_computation.2 | async-start | bytes 1179648 | tf_op jit(solution)/shard_map/all_to_all | solution.py:443
  57.6 0.0 collective-permute-done.1
  57.6 0.0 collective-permute-done
  57.6 4.8 %shard_map.97 = bf16[64,88,128]{2,1,0:T(8,128)(2,1)} custom-call(s32[1]{0:T(128)} %bitcast.core, bf16[256,1152]{1,0:T(8,128)(2,1)} %bitcast.22, bf16[256,1152]{1,0:T(8,128)(2,1)} %bitcast.7.other_mixed, bf16[256,1152]{1,0:T(8,128)(2,1)} %bitcast.4.og, bf16[256,1152]{1,0:T(8,128)(2,1)} %bitcast.8.other_og), custom_call_target="tpu_custom_call" | custom-call | flops 1358954496 | bytes 3801092 | tf_op jit(solution)/shard_map/pallas_call | solution.py:349
  62.5 5.8 %all-to-all-done.2 = bf16[8,32,1152]{2,1,0:T(8,128)(2,1)S(1)} async-done(((bf16[8,32,1152]{2,1,0:T(8,128)(2,1)}), bf16[8,32,1152]{2,1,0:T(8,128)(2,1)S(1)}, u32[]{:S(2)}, u32[]{:S(2)}) %all-to-all-start.2) | async-done | bytes 589856 | tf_op jit(solution)/shard_map/all_to_all | solution.py:443
  68.3 0.0 copy-start.1
  68.3 9.4 %all-to-all-start.3 = ((bf16[64,88,128]{2,1,0:T(8,128)(2,1)}), bf16[64,88,128]{2,1,0:T(8,128)(2,1)}, u32[]{:S(2)}, u32[]{:S(2)}) async-start(bf16[64,88,128]{2,1,0:T(8,128)(2,1)} %shard_map.97), calls=%async_computation.3 | async-start | bytes 2883584 | tf_op jit(solution)/shard_map/all_to_all | solution.py:467
  77.7 0.0 copy-done.1
  77.7 12.1 %shard_map.98 = bf16[256,1152]{1,0:T(8,128)(2,1)} custom-call(bf16[256,1152]{1,0:T(8,128)(2,1)} %bitcast.17, f32[256,1152]{1,0:T(8,128)} %get-tuple-element.14.stream_hbm, f32[1152]{0:T(1024)} %gt.3, bf16[256,1152]{1,0:T(8,128)(2,1)} %bitcast.16, bf16[256,3456]{1,0:T(8,128)(2,1)} %get-tuple-element.15.qkv_hbm, ...), custom_call_target="tpu_custom_call" | custom-call | flops 4756340736 | bytes 18031616 | tf_op jit(solution)/shard_map/pallas_call | solution.py:349
  89.8 8.4 %all-to-all-done.3.got_ref = bf16[64,88,128]{2,1,0:T(8,128)(2,1)} async-done(((bf16[64,88,128]{2,1,0:T(8,128)(2,1)}), bf16[64,88,128]{2,1,0:T(8,128)(2,1)}, u32[]{:S(2)}, u32[]{:S(2)}) %all-to-all-start.3) | async-done | bytes 1441824 | tf_op jit(solution)/shard_map/all_to_all | solution.py:467
  98.2 2.3 %shard_map.99 = f32[9,1152]{1,0:T(8,128)} custom-call(s32[1]{0:T(128)} %bitcast.12.owner_ref, bf16[64,88,128]{2,1,0:T(8,128)(2,1)} %all-to-all-done.3.got_ref), custom_call_target="tpu_custom_call" | custom-call | flops 1000 | bytes 1483268 | tf_op jit(solution)/shard_map/pallas_call | solution.py:349
Async XLA Ops:
  0.6 27.3 %copy-start = (bf16[1152,1152]{1,0:T(8,128)(2,1)S(1)}, bf16[1152,1152]{1,0:T(8,128)(2,1)}, u32[]{:S(2)}) copy-start(bf16[1152,1152]{1,0:T(8,128)(2,1)} %param.15) | copy-start | bytes 7962628
  0.6 19.0 %all-to-all-start.1 = ((bf16[8,32,1152]{2,1,0:T(8,128)(2,1)}), bf16[8,32,1152]{2,1,0:T(8,128)(2,1)}, u32[]{:S(2)}, u32[]{:S(2)}) async-start(bf16[8,32,1152]{2,1,0:T(8,128)(2,1)} %bitcast.15), calls=%async_computation.1 | async-start | bytes 1179648 | tf_op jit(solution)/shard_map/all_to_all | solution.py:443
  19.7 15.7 %all-to-all-start = ((bf16[8,32,1152]{2,1,0:T(8,128)(2,1)}), bf16[8,32,1152]{2,1,0:T(8,128)(2,1)S(1)}, u32[]{:S(2)}, u32[]{:S(2)}) async-start(bf16[8,32,1152]{2,1,0:T(8,128)(2,1)} %bitcast.21), calls=%async_computation | async-start | bytes 1179648 | tf_op jit(solution)/shard_map/all_to_all | solution.py:443
  26.4 31.2 %collective-permute-start.1 = (bf16[8,32,1152]{2,1,0:T(8,128)(2,1)}, bf16[8,32,1152]{2,1,0:T(8,128)(2,1)}, u32[]{:S(2)}, u32[]{:S(2)}) collective-permute-start(bf16[8,32,1152]{2,1,0:T(8,128)(2,1)} %all-to-all-done.1), channel_id=1, source_target_pairs={{0,8},{8,0},{16,24},{24,16},{32,40},{40,32},{48,56},{56,48},{64,72... | collective-permute-start | bytes 1769480 | tf_op jit(solution)/shard_map/ppermute | solution.py:446
  35.4 0.8 copy-start.2
  50.2 7.4 %collective-permute-start = (bf16[8,32,1152]{2,1,0:T(8,128)(2,1)}, bf16[8,32,1152]{2,1,0:T(8,128)(2,1)}, u32[]{:S(2)}, u32[]{:S(2)}) collective-permute-start(bf16[8,32,1152]{2,1,0:T(8,128)(2,1)} %get-tuple-element.11), channel_id=1, source_target_pairs={{0,8},{8,0},{16,24},{24,16},{32,40},{40,32},{48,56},{56,48},{64,72... | collective-permute-start | bytes 1769480 | tf_op jit(solution)/shard_map/ppermute | solution.py:446
  54.0 14.3 %all-to-all-start.2 = ((bf16[8,32,1152]{2,1,0:T(8,128)(2,1)}), bf16[8,32,1152]{2,1,0:T(8,128)(2,1)S(1)}, u32[]{:S(2)}, u32[]{:S(2)}) async-start(bf16[8,32,1152]{2,1,0:T(8,128)(2,1)} %get-tuple-element.12), calls=%async_computation.2 | async-start | bytes 1179648 | tf_op jit(solution)/shard_map/all_to_all | solution.py:443
  68.3 9.4 %copy-start.1 = (bf16[8,32,1152]{2,1,0:T(8,128)(2,1)}, bf16[8,32,1152]{2,1,0:T(8,128)(2,1)S(1)}, u32[]{:S(2)}) copy-start(bf16[8,32,1152]{2,1,0:T(8,128)(2,1)S(1)} %all-to-all-done.2) | copy-start | bytes 1769476
  68.3 29.9 %all-to-all-start.3 = ((bf16[64,88,128]{2,1,0:T(8,128)(2,1)}), bf16[64,88,128]{2,1,0:T(8,128)(2,1)}, u32[]{:S(2)}, u32[]{:S(2)}) async-start(bf16[64,88,128]{2,1,0:T(8,128)(2,1)} %shard_map.97), calls=%async_computation.3 | async-start | bytes 2883584 | tf_op jit(solution)/shard_map/all_to_all | solution.py:467

commit v5 on v4

--- a/solution.py
+++ b/solution.py
@@ -68,12 +68,12 @@
 
 
 def window(h):
-    tile = jnp.minimum(lax.div(h * HD, LANES), TILES - 2)
-    low = pl.multiple_of(tile * LANES, LANES)
+    low = h * HD // LANES * LANES
+    width = -(-(h * HD + HD - low) // LANES) * LANES
     start = h * HD - low
-    lane = lax.broadcasted_iota(jnp.int32, (1, WIN), 1)
+    lane = lax.broadcasted_iota(jnp.int32, (1, width), 1)
     inside = jnp.where((lane >= start) & (lane < start + HD), 1.0, 0.0)
-    return low, inside.astype(BF)
+    return low, width, inside.astype(BF)
 
 
 def softmax_keys(scores):
@@ -88,29 +88,22 @@
     return ((t - prob * delta) * SCALE).astype(BF)
 
 
-def heads_loop(first, second, unroll=8, ahead=1):
-    def body(i, carry):
-        waiting = []
-        for u in range(unroll):
-            h = i * unroll + u
-            waiting.append((h, first(h)))
-            if len(waiting) > ahead:
-                h, values = waiting.pop(0)
-                second(h, *values)
-        for h, values in waiting:
-            second(h, *values)
-        return carry
-
-    lax.fori_loop(0, HEADS // unroll, body, 0)
+def all_heads(first, second):
+    waiting = None
+    for h in range(HEADS):
+        values = first(h)
+        if waiting is not None:
+            second(h - 1, *waiting)
+        waiting = values
+    second(HEADS - 1, *waiting)
 
 
 def merge(slots, dst, base=0):
     for t in range(TILES):
         total = None
         for h in range(HEADS):
-            first = min(h * HD // LANES, TILES - 2)
             if h * HD < (t + 1) * LANES and (h + 1) * HD > t * LANES:
-                at = (t - first) * LANES
+                at = (t - h * HD // LANES) * LANES
                 piece = slots[h, :, at : at + LANES]
                 total = piece if total is None else total + piece
         dst[:, base + t * LANES : base + (t + 1) * LANES] = total
@@ -140,7 +133,7 @@
     return [fetch(src.at[:, p], dst.at[:, p], sems.at[i]) for i, p in enumerate(PIECES)]
 
 
-def spatial_forward(video, gs, gt, wq_hbm, wo_hbm, hid_out, stream_hbm, qkv_hbm, prob_hbm,
+def spatial_forward(video, gs, gt, wq_hbm, wo_hbm, hid_out, mix_hbm, qkv_hbm, prob_hbm,
                     wq, wo, hid, mix, stream, qkv, prob, slots, sems, out_sems):
     wq_copies = fetch_columns(wq_hbm, wq, sems)
     wo_copy = fetch(wo_hbm, wo, sems.at[4])
@@ -156,30 +149,30 @@
     qkv_copy = fetch(qkv, qkv_hbm, out_sems.at[0])
 
     def head(h):
-        low, inside = window(h)
-        q = qkv[:, pl.ds(low, WIN)] * inside
-        k = qkv[:, pl.ds(D + low, WIN)]
-        v = qkv[:, pl.ds(2 * D + low, WIN)] * inside
+        low, width, inside = window(h)
+        q = qkv[:, pl.ds(low, width)] * inside
+        k = qkv[:, pl.ds(D + low, width)]
+        v = qkv[:, pl.ds(2 * D + low, width)] * inside
         return nt(k, q), v
 
     def rest(h, scores, v):
         p = softmax_keys(scores).astype(BF)
         prob[h] = p
-        slots[h] = tn(p, v).astype(BF)
-
-    heads_loop(head, rest)
+        slots[h, :, : v.shape[1]] = tn(p, v).astype(BF)
+
+    all_heads(head, rest)
     prob_copy = fetch(prob, prob_hbm, out_sems.at[1])
     merge(slots, mix)
+    mix_copy = fetch(mix, mix_hbm, out_sems.at[2])
     wo_copy.wait()
     stream[...] = video[...].astype(F32) + nn(mix[...], wo[...])
-    stream_copy = fetch(stream, stream_hbm, out_sems.at[2])
 
     def second_norm(rows):
         centered, inv = row_stats(stream[rows, :])
         hid_out[rows, :] = (centered * inv * gt[...].reshape(1, D)).astype(BF)
 
     row_blocks(second_norm)
-    for copy in (qkv_copy, prob_copy, stream_copy):
+    for copy in (qkv_copy, prob_copy, mix_copy):
         copy.wait()
 
 
@@ -204,11 +197,11 @@
     same = key_pos == query_pos
 
     def head(h):
-        low, inside = window(h)
+        low, width, inside = window(h)
         values = []
         for b in range(2):
             rows = slice(b * BLK, (b + 1) * BLK)
-            qs, ks, vs = pl.ds(low, WIN), pl.ds(D + low, WIN), pl.ds(2 * D + low, WIN)
+            qs, ks, vs = pl.ds(low, width), pl.ds(D + low, width), pl.ds(2 * D + low, width)
             q = qkv[rows, qs] * inside
             k = qkv[rows, ks] * inside
             v = qkv[rows, vs] * inside
@@ -222,12 +215,12 @@
             p = softmax_keys(jnp.where(same, scores, -1e30))
             pb = p.astype(BF)
             ds = score_grad(p, prob_grad)
-            o_slots[h, rows, :] = tn(pb, v).astype(BF)
-            v_slots[h, rows, :] = nn(pb, do).astype(BF)
-            k_slots[h, rows, :] = nn(ds, q).astype(BF)
-            q_slots[h, rows, :] = tn(ds, k).astype(BF)
-
-    heads_loop(head, rest)
+            o_slots[h, rows, : q.shape[1]] = tn(pb, v).astype(BF)
+            v_slots[h, rows, : q.shape[1]] = nn(pb, do).astype(BF)
+            k_slots[h, rows, : q.shape[1]] = nn(ds, q).astype(BF)
+            q_slots[h, rows, : q.shape[1]] = tn(ds, k).astype(BF)
+
+    all_heads(head, rest)
     merge(o_slots, mix)
     dh[...] = project_back((q_slots, k_slots, v_slots), dqkv, wq).astype(BF)
     for b in range(2):
@@ -237,15 +230,18 @@
         dhid_out[:, part, :] = dh[rows, :].reshape(SEQ, HALF, D)
 
 
-def spatial_backward(dhid_hbm, stream_hbm, gt, og_hbm, qkv_hbm, prob_hbm, video_hbm, gs,
-                     wo_hbm, wq_hbm, out, dhid, stream, og, qkv, prob, video, wo, wq,
+def spatial_backward(dhid_hbm, mix_hbm, gt, og_hbm, qkv_hbm, prob_hbm, video_hbm, gs,
+                     wo_hbm, wq_hbm, out, dhid, mix, stream, og, qkv, prob, video, wo, wq,
                      sg, sgb, dmix, dqkv, dh, q_slots, k_slots, v_slots, sems):
     pairs = (
-        (dhid_hbm, dhid), (stream_hbm, stream), (og_hbm, og), (wo_hbm, wo), (qkv_hbm, qkv),
-        (prob_hbm, prob), (wq_hbm, wq), (video_hbm, video),
+        (wo_hbm, wo), (mix_hbm, mix), (video_hbm, video), (dhid_hbm, dhid), (og_hbm, og),
+        (qkv_hbm, qkv), (prob_hbm, prob), (wq_hbm, wq),
     )
     copies = [fetch(src, dst, sems.at[i]) for i, (src, dst) in enumerate(pairs)]
     for copy in copies[:3]:
+        copy.wait()
+    stream[...] = video[...].astype(F32) + nn(mix[...], wo[...])
+    for copy in copies[3:5]:
         copy.wait()
 
     def stream_grad(rows):
@@ -255,14 +251,13 @@
         sgb[rows, :] = total.astype(BF)
 
     row_blocks(stream_grad)
-    copies[3].wait()
     dmix[...] = nt(sgb[...], wo[...]).astype(BF)
-    copies[4].wait()
     copies[5].wait()
+    copies[6].wait()
 
     def head(h):
-        low, inside = window(h)
-        qs, ks, vs = pl.ds(low, WIN), pl.ds(D + low, WIN), pl.ds(2 * D + low, WIN)
+        low, width, inside = window(h)
+        qs, ks, vs = pl.ds(low, width), pl.ds(D + low, width), pl.ds(2 * D + low, width)
         q = qkv[:, qs] * inside
         k = qkv[:, ks] * inside
         v = qkv[:, vs]
@@ -272,14 +267,13 @@
     def rest(h, prob_grad, q, k, do):
         pb = prob[h]
         ds = score_grad(pb.astype(F32), prob_grad)
-        v_slots[h] = nn(pb, do).astype(BF)
-        k_slots[h] = nn(ds, q).astype(BF)
-        q_slots[h] = tn(ds, k).astype(BF)
-
-    heads_loop(head, rest)
-    copies[6].wait()
+        v_slots[h, :, : q.shape[1]] = nn(pb, do).astype(BF)
+        k_slots[h, :, : q.shape[1]] = nn(ds, q).astype(BF)
+        q_slots[h, :, : q.shape[1]] = tn(ds, k).astype(BF)
+
+    all_heads(head, rest)
+    copies[7].wait()
     dh[...] = project_back((q_slots, k_slots, v_slots), dqkv, wq).astype(BF)
-    copies[7].wait()
 
     def video_grad(rows):
         dx = norm_back(video[rows, :].astype(F32), gs[...].reshape(1, D), dh[rows, :].astype(F32))
@@ -366,7 +360,7 @@
 def run_spatial_forward(clip, gs, gt, wq, wo):
     return call(
         spatial_forward,
-        [((T, D), BF), ((T, D), F32), ((T, 3 * D), BF), ((HEADS, T, T), BF)],
+        [((T, D), BF), ((T, D), BF), ((T, 3 * D), BF), ((HEADS, T, T), BF)],
         (clip, gs, gt, wq, wo),
         [WIDE, SQUARE, TOK, TOK, TOKF, TOK3, PROB, SLOTS, DMA((5,)), DMA((3,))],
         5 * UNIT,
@@ -386,12 +380,12 @@
     )
 
 
-def run_spatial_backward(dhid, stream, gt, og, qkv, prob, clip, gs, wo, wq):
+def run_spatial_backward(dhid, mix, gt, og, qkv, prob, clip, gs, wo, wq):
     return call(
         spatial_backward,
         [((T, D), BF)],
-        (dhid, stream, gt, og, qkv, prob, clip, gs, wo, wq),
-        [TOK, TOKF, TOK, TOK3, PROB, TOK, SQUARE, WIDE, TOKF, TOK, TOK, TOK3, TOK,
+        (dhid, mix, gt, og, qkv, prob, clip, gs, wo, wq),
+        [TOK, TOK, TOKF, TOK, TOK3, PROB, TOK, SQUARE, WIDE, TOKF, TOK, TOK, TOK3, TOK,
          SLOTS, SLOTS, SLOTS, DMA((8,))],
         7 * UNIT,
         [ANY, ANY, VMEM, ANY, ANY, ANY, ANY, VMEM, ANY, ANY],
@@ -447,7 +441,7 @@
 
     og_pos = exchange(og)
     other_og = swap(og_pos)
-    hid, stream, qkv, prob = run_spatial_forward(
+    hid, mix, qkv, prob = run_spatial_forward(
         clip, gain_spatial, gain_temporal, w_spatial_qkv, w_spatial_out
     )
     hid_pos = exchange(hid)
@@ -468,7 +462,7 @@
         chunks, ("dp", "seq"), 0, 0, axis_index_groups=owners, tiled=True
     )
     video_grad = run_spatial_backward(
-        dhid, stream, gain_temporal, og, qkv, prob, clip, gain_spatial,
+        dhid, mix, gain_temporal, og, qkv, prob, clip, gain_spatial,
         w_spatial_out, w_spatial_qkv,
     )
     owner = lax.axis_index("seq").reshape(1)

time: 102 us -> 99.8 us (0.978)
  matrix products: 2.93 us -> 1.86 us
    all_to_all x3, waiting for transfers between devices: 10.4 us -> 11.6 us  [exchange(): return lax.all_to_all(x.reshape(SEQ, POS, D), 'seq', 0, 0, tiled=True)]
    all_to_all x1, waiting for transfers between devices: 8.38 us -> 7.28 us  [per_device(): lax.all_to_all(chunks, ('dp', 'seq'), 0, 0, axis_index_groups=owners, til...]
    dot_general x1, matrix products: 2.93 us -> 1.86 us  [nt(): lax.dot_general(a, b, (((1,), (1,)), ((), ())), preferred_element_type=F32)]
  transfers between devices with their start and end apart: 6 -> 6, of which waited for: 3 -> 3; matrix products, arithmetic and copies ran while one was open for 3% -> 2% of each run, Pallas kernels for 42% -> 42%
where the time goes in v5:
time: 99.8 us; the launch traced here: 98.7 us
  Pallas kernels  43.8 us (44%)
  starting transfers between devices  33.3 us (33%)
  waiting for transfers between devices  18.9 us (19%)
  matrix products  1.86 us (2%)
    pallas_call x5, Pallas kernels, call(): pl.pallas_call(fn, out_shape=[jax.ShapeDtypeStruct(s, d) for s, d in outs...  43.8 us
    all_to_all x3, starting transfers between devices, exchange(): return lax.all_to_all(x.reshape(SEQ, POS, D), 'seq', 0, 0, tiled=True)  18.6 us
    all_to_all x3, waiting for transfers between devices, exchange(): return lax.all_to_all(x.reshape(SEQ, POS, D), 'seq', 0, 0, tiled=True)  11.6 us
    all_to_all x1, starting transfers between devices, per_device(): lax.all_to_all(chunks, ('dp', 'seq'), 0, 0, axis_index_groups=owners, til...  9.38 us
    all_to_all x1, waiting for transfers between devices, per_device(): lax.all_to_all(chunks, ('dp', 'seq'), 0, 0, axis_index_groups=owners, til...  7.28 us
    ppermute x2, starting transfers between devices, swap(): return lax.ppermute(x, 'dp', [(i, i ^ 1) for i in range(DP)])  5.35 us
  transfers between devices with their start and end apart: 6, of which 3 were waited for; matrix products, arithmetic and copies ran while one was open for 2% of the time, Pallas kernels for 42%

profile of v5, /device:TPU:1, one launch (start us, length us, event | category | flops | bytes accessed | tf_op | source)
XLA Modules:
  0.0 98.7 jit_solution(976653385084941953)
XLA Ops:
  0.6 0.0 copy-start
  0.6 7.7 %all-to-all-start.1 = ((bf16[8,32,1152]{2,1,0:T(8,128)(2,1)}), bf16[8,32,1152]{2,1,0:T(8,128)(2,1)S(1)}, u32[]{:S(2)}, u32[]{:S(2)}) async-start(bf16[8,32,1152]{2,1,0:T(8,128)(2,1)} %bitcast.15), calls=%async_computation.1 | async-start | bytes 1179648 | tf_op jit(solution)/shard_map/all_to_all | solution.py:437
  8.4 10.2 %shard_map.95 = (bf16[256,1152]{1,0:T(8,128)(2,1)}, bf16[256,1152]{1,0:T(8,128)(2,1)}, bf16[256,3456]{1,0:T(8,128)(2,1)}, bf16[16,256,256]{2,1,0:T(8,128)(2,1)}) custom-call(bf16[256,1152]{1,0:T(8,128)(2,1)} %bitcast.20, f32[1152]{0:T(1024)} %gs.3, f32[1152]{0:T(1024)} %gt.3, bf16[1152,3456]{1,0:T(8,128)(2,1)} %wq_hbm.5, bf16[1152,1152]{1,0:T(8,128)(2,1)} %wo_hbm.3), custom_call_target="tpu_custom_call" | custom-call | flops 3397386240 | bytes 16262144 | tf_op jit(solution)/shard_map/pallas_call | solution.py:343
  18.6 0.0 all-to-all-done.1
  18.6 0.0 copy-start.1
  18.6 6.7 %all-to-all-start = ((bf16[8,32,1152]{2,1,0:T(8,128)(2,1)}), bf16[8,32,1152]{2,1,0:T(8,128)(2,1)}, u32[]{:S(2)}, u32[]{:S(2)}) async-start(bf16[8,32,1152]{2,1,0:T(8,128)(2,1)} %bitcast.19), calls=%async_computation | async-start | bytes 1179648 | tf_op jit(solution)/shard_map/all_to_all | solution.py:437
  25.3 1.5 %collective-permute-start.1 = (bf16[8,32,1152]{2,1,0:T(8,128)(2,1)S(1)}, bf16[8,32,1152]{2,1,0:T(8,128)(2,1)}, u32[]{:S(2)}, u32[]{:S(2)}) collective-permute-start(bf16[8,32,1152]{2,1,0:T(8,128)(2,1)S(1)} %all-to-all-done.1), channel_id=1, source_target_pairs={{0,8},{8,0},{16,24},{24,16},{32,40},{40,32},{48,56},{56,48},{64,72... | collective-permute-start | bytes 1769480 | tf_op jit(solution)/shard_map/ppermute | solution.py:440
  26.8 0.0 copy-done
  26.8 1.9 %convolution_convert_fusion = bf16[256,1152]{1,0:T(8,128)(2,1)} fusion(bf16[256,1152]{1,0:T(8,128)(2,1)S(1)} %bitcast.17, bf16[1152,1152]{1,0:T(8,128)(2,1)S(1)} %copy-done), kind=kOutput, calls=%fused_computation | convolution fusion | flops 679772160 | bytes 3833856 | tf_op jit(solution)/shard_map/dot_general | solution.py:39
  28.7 0.0 copy-done.1
  28.7 5.7 %all-to-all-done.hid_in = bf16[8,32,1152]{2,1,0:T(8,128)(2,1)} async-done(((bf16[8,32,1152]{2,1,0:T(8,128)(2,1)}), bf16[8,32,1152]{2,1,0:T(8,128)(2,1)}, u32[]{:S(2)}, u32[]{:S(2)}) %all-to-all-start) | async-done | bytes 589856 | tf_op jit(solution)/shard_map/all_to_all | solution.py:437
  34.4 13.3 %shard_map.96 = (bf16[8,32,1152]{2,1,0:T(8,128)(2,1)}, bf16[8,32,1152]{2,1,0:T(8,128)(2,1)}) custom-call(bf16[8,32,1152]{2,1,0:T(8,128)(2,1)} %all-to-all-done.hid_in, bf16[8,32,1152]{2,1,0:T(8,128)(2,1)} %bitcast.24, bf16[1152,3456]{1,0:T(8,128)(2,1)} %wq_hbm.4), custom_call_target="tpu_custom_call" | custom-call | flops 5435817984 | bytes 10321920 | tf_op jit(solution)/shard_map/pallas_call | solution.py:343
  47.7 3.8 %collective-permute-start = (bf16[8,32,1152]{2,1,0:T(8,128)(2,1)}, bf16[8,32,1152]{2,1,0:T(8,128)(2,1)}, u32[]{:S(2)}, u32[]{:S(2)}) collective-permute-start(bf16[8,32,1152]{2,1,0:T(8,128)(2,1)} %get-tuple-element.11), channel_id=1, source_target_pairs={{0,8},{8,0},{16,24},{24,16},{32,40},{40,32},{48,56},{56,48},{64,72... | collective-permute-start | bytes 1769480 | tf_op jit(solution)/shard_map/ppermute | solution.py:440
  51.5 4.2 %all-to-all-start.2 = ((bf16[8,32,1152]{2,1,0:T(8,128)(2,1)}), bf16[8,32,1152]{2,1,0:T(8,128)(2,1)}, u32[]{:S(2)}, u32[]{:S(2)}) async-start(bf16[8,32,1152]{2,1,0:T(8,128)(2,1)} %get-tuple-element.12), calls=%async_computation.2 | async-start | bytes 1179648 | tf_op jit(solution)/shard_map/all_to_all | solution.py:437
  55.7 0.0 collective-permute-done.1
  55.8 0.0 collective-permute-done
  55.8 4.8 %shard_map.97 = bf16[64,88,128]{2,1,0:T(8,128)(2,1)} custom-call(s32[1]{0:T(128)} %bitcast.core, bf16[256,1152]{1,0:T(8,128)(2,1)} %bitcast.22, bf16[256,1152]{1,0:T(8,128)(2,1)} %bitcast.7.other_mixed, bf16[256,1152]{1,0:T(8,128)(2,1)} %bitcast.18, bf16[256,1152]{1,0:T(8,128)(2,1)} %bitcast.8.other_og), custom_call_target="tpu_custom_call" | custom-call | flops 1358954496 | bytes 3801092 | tf_op jit(solution)/shard_map/pallas_call | solution.py:343
  60.6 5.9 %all-to-all-done.2 = bf16[8,32,1152]{2,1,0:T(8,128)(2,1)} async-done(((bf16[8,32,1152]{2,1,0:T(8,128)(2,1)}), bf16[8,32,1152]{2,1,0:T(8,128)(2,1)}, u32[]{:S(2)}, u32[]{:S(2)}) %all-to-all-start.2) | async-done | bytes 589856 | tf_op jit(solution)/shard_map/all_to_all | solution.py:437
  66.5 9.4 %all-to-all-start.3 = ((bf16[64,88,128]{2,1,0:T(8,128)(2,1)}), bf16[64,88,128]{2,1,0:T(8,128)(2,1)}, u32[]{:S(2)}, u32[]{:S(2)}) async-start(bf16[64,88,128]{2,1,0:T(8,128)(2,1)} %shard_map.97), calls=%async_computation.3 | async-start | bytes 2883584 | tf_op jit(solution)/shard_map/all_to_all | solution.py:461
  75.9 13.2 %shard_map.98 = bf16[256,1152]{1,0:T(8,128)(2,1)} custom-call(bf16[256,1152]{1,0:T(8,128)(2,1)} %bitcast.9.dhid_hbm, bf16[256,1152]{1,0:T(8,128)(2,1)} %get-tuple-element.14.mix_hbm, f32[1152]{0:T(1024)} %gt.3, bf16[256,1152]{1,0:T(8,128)(2,1)} %bitcast.16, bf16[256,3456]{1,0:T(8,128)(2,1)} %get-tuple-element.15.qkv_hbm, ...), custom_call_target="tpu_custom_call" | custom-call | flops 4756340736 | bytes 17441792 | tf_op jit(solution)/shard_map/pallas_call | solution.py:343
  89.1 7.3 %all-to-all-done.3.got_ref = bf16[64,88,128]{2,1,0:T(8,128)(2,1)} async-done(((bf16[64,88,128]{2,1,0:T(8,128)(2,1)}), bf16[64,88,128]{2,1,0:T(8,128)(2,1)}, u32[]{:S(2)}, u32[]{:S(2)}) %all-to-all-start.3) | async-done | bytes 1441824 | tf_op jit(solution)/shard_map/all_to_all | solution.py:461
  96.4 2.3 %shard_map.99 = f32[9,1152]{1,0:T(8,128)} custom-call(s32[1]{0:T(128)} %bitcast.12.owner_ref, bf16[64,88,128]{2,1,0:T(8,128)(2,1)} %all-to-all-done.3.got_ref), custom_call_target="tpu_custom_call" | custom-call | flops 1000 | bytes 1483268 | tf_op jit(solution)/shard_map/pallas_call | solution.py:343
Async XLA Ops:
  0.6 26.2 %copy-start = (bf16[1152,1152]{1,0:T(8,128)(2,1)S(1)}, bf16[1152,1152]{1,0:T(8,128)(2,1)}, u32[]{:S(2)}) copy-start(bf16[1152,1152]{1,0:T(8,128)(2,1)} %param.15) | copy-start | bytes 7962628
  0.6 18.0 %all-to-all-start.1 = ((bf16[8,32,1152]{2,1,0:T(8,128)(2,1)}), bf16[8,32,1152]{2,1,0:T(8,128)(2,1)S(1)}, u32[]{:S(2)}, u32[]{:S(2)}) async-start(bf16[8,32,1152]{2,1,0:T(8,128)(2,1)} %bitcast.15), calls=%async_computation.1 | async-start | bytes 1179648 | tf_op jit(solution)/shard_map/all_to_all | solution.py:437
  18.6 10.1 %copy-start.1 = (bf16[8,32,1152]{2,1,0:T(8,128)(2,1)}, bf16[8,32,1152]{2,1,0:T(8,128)(2,1)S(1)}, u32[]{:S(2)}) copy-start(bf16[8,32,1152]{2,1,0:T(8,128)(2,1)S(1)} %all-to-all-done.1) | copy-start | bytes 1769476
  18.6 15.8 %all-to-all-start = ((bf16[8,32,1152]{2,1,0:T(8,128)(2,1)}), bf16[8,32,1152]{2,1,0:T(8,128)(2,1)}, u32[]{:S(2)}, u32[]{:S(2)}) async-start(bf16[8,32,1152]{2,1,0:T(8,128)(2,1)} %bitcast.19), calls=%async_computation | async-start | bytes 1179648 | tf_op jit(solution)/shard_map/all_to_all | solution.py:437
  25.3 30.4 %collective-permute-start.1 = (bf16[8,32,1152]{2,1,0:T(8,128)(2,1)S(1)}, bf16[8,32,1152]{2,1,0:T(8,128)(2,1)}, u32[]{:S(2)}, u32[]{:S(2)}) collective-permute-start(bf16[8,32,1152]{2,1,0:T(8,128)(2,1)S(1)} %all-to-all-done.1), channel_id=1, source_target_pairs={{0,8},{8,0},{16,24},{24,16},{32,40},{40,32},{48,56},{56,48},{64,72... | collective-permute-start | bytes 1769480 | tf_op jit(solution)/shard_map/ppermute | solution.py:440
  47.7 8.0 %collective-permute-start = (bf16[8,32,1152]{2,1,0:T(8,128)(2,1)}, bf16[8,32,1152]{2,1,0:T(8,128)(2,1)}, u32[]{:S(2)}, u32[]{:S(2)}) collective-permute-start(bf16[8,32,1152]{2,1,0:T(8,128)(2,1)} %get-tuple-element.11), channel_id=1, source_target_pairs={{0,8},{8,0},{16,24},{24,16},{32,40},{40,32},{48,56},{56,48},{64,72... | collective-permute-start | bytes 1769480 | tf_op jit(solution)/shard_map/ppermute | solution.py:440
  51.5 15.0 %all-to-all-start.2 = ((bf16[8,32,1152]{2,1,0:T(8,128)(2,1)}), bf16[8,32,1152]{2,1,0:T(8,128)(2,1)}, u32[]{:S(2)}, u32[]{:S(2)}) async-start(bf16[8,32,1152]{2,1,0:T(8,128)(2,1)} %get-tuple-element.12), calls=%async_computation.2 | async-start | bytes 1179648 | tf_op jit(solution)/shard_map/all_to_all | solution.py:437
  66.5 29.9 %all-to-all-start.3 = ((bf16[64,88,128]{2,1,0:T(8,128)(2,1)}), bf16[64,88,128]{2,1,0:T(8,128)(2,1)}, u32[]{:S(2)}, u32[]{:S(2)}) async-start(bf16[64,88,128]{2,1,0:T(8,128)(2,1)} %shard_map.97), calls=%async_computation.3 | async-start | bytes 2883584 | tf_op jit(solution)/shard_map/all_to_all | solution.py:461

commit v6 on v5

--- a/solution.py
+++ b/solution.py
@@ -50,12 +50,12 @@
     return centered, lax.rsqrt(spread + EPS)
 
 
-def row_blocks(fn):
+def row_blocks(fn, first=0, last=T // ROWS):
     def body(i, carry):
         fn(pl.ds(pl.multiple_of(i * ROWS, ROWS), ROWS))
         return carry
 
-    lax.fori_loop(0, T // ROWS, body, 0, unroll=4)
+    lax.fori_loop(first, last, body, 0, unroll=4)
 
 
 def norm_back(x, g, dy):
@@ -133,7 +133,7 @@
     return [fetch(src.at[:, p], dst.at[:, p], sems.at[i]) for i, p in enumerate(PIECES)]
 
 
-def spatial_forward(video, gs, gt, wq_hbm, wo_hbm, hid_out, mix_hbm, qkv_hbm, prob_hbm,
+def spatial_forward(video, gs, gt, wq_hbm, wo_hbm, hid_hbm, mix_hbm, qkv_hbm, prob_hbm,
                     wq, wo, hid, mix, stream, qkv, prob, slots, sems, out_sems):
     wq_copies = fetch_columns(wq_hbm, wq, sems)
     wo_copy = fetch(wo_hbm, wo, sems.at[4])
@@ -169,10 +169,14 @@
 
     def second_norm(rows):
         centered, inv = row_stats(stream[rows, :])
-        hid_out[rows, :] = (centered * inv * gt[...].reshape(1, D)).astype(BF)
-
-    row_blocks(second_norm)
-    for copy in (qkv_copy, prob_copy, mix_copy):
+        hid[rows, :] = (centered * inv * gt[...].reshape(1, D)).astype(BF)
+
+    copies = [qkv_copy, prob_copy, mix_copy]
+    for i in range(2):
+        row_blocks(second_norm, i * T // ROWS // 2, (i + 1) * T // ROWS // 2)
+        rows = slice(i * T // 2, (i + 1) * T // 2)
+        copies.append(fetch(hid.at[rows, :], hid_hbm.at[rows, :], out_sems.at[3 + i]))
+    for copy in copies:
         copy.wait()
 
 
@@ -180,17 +184,36 @@
 BLK = SEQ * HALF
 
 
-def temporal(hid_in, dmix_in, wq_hbm, mixed_out, dhid_out,
-             wq, hid, dmix, qkv, mix, dqkv, dh, o_slots, q_slots, k_slots, v_slots, sems):
+def block_of(ref, b):
+    return ref.at[b * BLK : (b + 1) * BLK, :].reshape(SEQ, HALF, D)
+
+
+def fetch_blocks(src, dst, sems, first):
+    return [
+        fetch(src.at[:, b * HALF : (b + 1) * HALF, :], block_of(dst, b), sems.at[first + b])
+        for b in range(2)
+    ]
+
+
+def store_blocks(src, dst, sems, first):
+    return [
+        fetch(block_of(src, b), dst.at[:, b * HALF : (b + 1) * HALF, :], sems.at[first + b])
+        for b in range(2)
+    ]
+
+
+def temporal(hid_hbm, dmix_hbm, wq_hbm, mixed_hbm, dhid_hbm,
+             wq, hid, dmix, qkv, mix, dqkv, dh, o_slots, q_slots, k_slots, v_slots, sems, io_sems):
+    hid_copies = fetch_blocks(hid_hbm, hid, io_sems, 0)
     wq_copies = fetch_columns(wq_hbm, wq, sems)
-    for b in range(2):
-        part = slice(b * HALF, (b + 1) * HALF)
-        rows = slice(b * BLK, (b + 1) * BLK)
-        hid[rows, :] = hid_in[:, part, :].reshape(BLK, D)
-        dmix[rows, :] = dmix_in[:, part, :].reshape(BLK, D)
+    dmix_copies = fetch_blocks(dmix_hbm, dmix, io_sems, 2)
+    for copy in hid_copies:
+        copy.wait()
     for copy, p in zip(wq_copies, PIECES):
         copy.wait()
         qkv[:, p] = nn(hid[...], wq[:, p]).astype(BF)
+    for copy in dmix_copies:
+        copy.wait()
 
     key_pos = lax.rem(lax.broadcasted_iota(jnp.int32, (BLK, BLK), 0), HALF)
     query_pos = lax.rem(lax.broadcasted_iota(jnp.int32, (BLK, BLK), 1), HALF)
@@ -222,12 +245,11 @@
 
     all_heads(head, rest)
     merge(o_slots, mix)
+    out_copies = store_blocks(mix, mixed_hbm, io_sems, 4)
     dh[...] = project_back((q_slots, k_slots, v_slots), dqkv, wq).astype(BF)
-    for b in range(2):
-        part = slice(b * HALF, (b + 1) * HALF)
-        rows = slice(b * BLK, (b + 1) * BLK)
-        mixed_out[:, part, :] = mix[rows, :].reshape(SEQ, HALF, D)
-        dhid_out[:, part, :] = dh[rows, :].reshape(SEQ, HALF, D)
+    out_copies += store_blocks(dh, dhid_hbm, io_sems, 6)
+    for copy in out_copies:
+        copy.wait()
 
 
 def spatial_backward(dhid_hbm, mix_hbm, gt, og_hbm, qkv_hbm, prob_hbm, video_hbm, gs,
@@ -324,8 +346,15 @@
     lax.fori_loop(0, GROUPS, body, 0)
 
 
-def sum_chunks(owner, got, out, total, *, scale):
-    total[...] = jnp.sum(got[...].astype(F32), axis=0) * scale
+def sum_chunks(owner, got_hbm, out, got, total, sems, *, scale):
+    step = GROUPS * SEQ // 4
+    pieces = [slice(i * step, (i + 1) * step) for i in range(4)]
+    copies = [fetch(got_hbm.at[p], got.at[p], sems.at[i]) for i, p in enumerate(pieces)]
+    for i, (copy, p) in enumerate(zip(copies, pieces)):
+        copy.wait()
+        part = jnp.sum(got[p].astype(F32), axis=0)
+        total[...] = part if i == 0 else total[...] + part
+    total[...] *= scale
     back = lax.rem(SUB - owner[0], SUB)
     for t in range(TILES):
         lanes = slice(t * LANES, (t + 1) * LANES)
@@ -362,10 +391,10 @@
         spatial_forward,
         [((T, D), BF), ((T, D), BF), ((T, 3 * D), BF), ((HEADS, T, T), BF)],
         (clip, gs, gt, wq, wo),
-        [WIDE, SQUARE, TOK, TOK, TOKF, TOK3, PROB, SLOTS, DMA((5,)), DMA((3,))],
+        [WIDE, SQUARE, TOK, TOK, TOKF, TOK3, PROB, SLOTS, DMA((5,)), DMA((5,))],
         5 * UNIT,
         [VMEM, VMEM, VMEM, ANY, ANY],
-        [VMEM, ANY, ANY, ANY],
+        [ANY, ANY, ANY, ANY],
     )
 
 
@@ -374,9 +403,11 @@
         temporal,
         [((SEQ, POS, D), BF), ((SEQ, POS, D), BF)],
         (hid, dmix, wq),
-        [WIDE, TOK, TOK, TOK3, TOK, TOK3, TOK, SLOTS, SLOTS, SLOTS, SLOTS, DMA((4,))],
+        [WIDE, TOK, TOK, TOK3, TOK, TOK3, TOK, SLOTS, SLOTS, SLOTS, SLOTS, DMA((4,)),
+         DMA((8,))],
         8 * UNIT,
-        [VMEM, VMEM, ANY],
+        [ANY, ANY, ANY],
+        [ANY, ANY],
     )
 
 
@@ -405,16 +436,16 @@
 
 
 def run_sum_chunks(owner, parts, scale):
-    def finish(owner_ref, got_ref, out_ref, total_ref):
-        sum_chunks(owner_ref, got_ref, out_ref, total_ref, scale=scale)
+    def finish(*refs):
+        sum_chunks(*refs, scale=scale)
 
     return call(
         finish,
         [((OWN, D), F32)],
         (owner, parts),
-        [VMEM((CHUNK, LANES), F32)],
+        [VMEM((GROUPS * SEQ, CHUNK, LANES), BF), VMEM((CHUNK, LANES), F32), DMA((4,))],
         1000,
-        [pltpu.SMEM, VMEM],
+        [pltpu.SMEM, ANY],
     )[0]
 
 

time: 99.8 us -> 98.7 us (0.989)
  Pallas kernels: 43.8 us -> 42.6 us
    pallas_call x5, Pallas kernels: 43.8 us -> 42.6 us  [call(): pl.pallas_call(fn, out_shape=[jax.ShapeDtypeStruct(s, d) for s, d in outs...]
where the time goes in v6:
time: 98.7 us; the launch traced here: 97.6 us
  Pallas kernels  42.6 us (43%)
  starting transfers between devices  33.3 us (34%)
  waiting for transfers between devices  18.9 us (19%)
  matrix products  1.86 us (2%)
    pallas_call x5, Pallas kernels, call(): pl.pallas_call(fn, out_shape=[jax.ShapeDtypeStruct(s, d) for s, d in outs...  42.6 us
    all_to_all x3, starting transfers between devices, exchange(): return lax.all_to_all(x.reshape(SEQ, POS, D), 'seq', 0, 0, tiled=True)  18.6 us
    all_to_all x3, waiting for transfers between devices, exchange(): return lax.all_to_all(x.reshape(SEQ, POS, D), 'seq', 0, 0, tiled=True)  11.7 us
    all_to_all x1, starting transfers between devices, per_device(): lax.all_to_all(chunks, ('dp', 'seq'), 0, 0, axis_index_groups=owners, til...  9.38 us
    all_to_all x1, waiting for transfers between devices, per_device(): lax.all_to_all(chunks, ('dp', 'seq'), 0, 0, axis_index_groups=owners, til...  7.28 us
    ppermute x2, starting transfers between devices, swap(): return lax.ppermute(x, 'dp', [(i, i ^ 1) for i in range(DP)])  5.35 us
  transfers between devices with their start and end apart: 6, of which 3 were waited for; matrix products, arithmetic and copies ran while one was open for 2% of the time, Pallas kernels for 42%

profile of v6, /device:TPU:1, one launch (start us, length us, event | category | flops | bytes accessed | tf_op | source)
XLA Modules:
  0.0 97.6 jit_solution(14310103037666976373)
XLA Ops:
  0.6 0.0 copy-start
  0.6 7.7 %all-to-all-start.1 = ((bf16[8,32,1152]{2,1,0:T(8,128)(2,1)}), bf16[8,32,1152]{2,1,0:T(8,128)(2,1)S(1)}, u32[]{:S(2)}, u32[]{:S(2)}) async-start(bf16[8,32,1152]{2,1,0:T(8,128)(2,1)} %bitcast.15), calls=%async_computation.1 | async-start | bytes 1179648 | tf_op jit(solution)/shard_map/all_to_all | solution.py:468
  8.4 10.0 %shard_map.95 = (bf16[256,1152]{1,0:T(8,128)(2,1)}, bf16[256,1152]{1,0:T(8,128)(2,1)}, bf16[256,3456]{1,0:T(8,128)(2,1)}, bf16[16,256,256]{2,1,0:T(8,128)(2,1)}) custom-call(bf16[256,1152]{1,0:T(8,128)(2,1)} %bitcast.20, f32[1152]{0:T(1024)} %gs.3, f32[1152]{0:T(1024)} %gt.3, bf16[1152,3456]{1,0:T(8,128)(2,1)} %wq_hbm.5, bf16[1152,1152]{1,0:T(8,128)(2,1)} %wo_hbm.3), custom_call_target="tpu_custom_call" | custom-call | flops 3397386240 | bytes 16262144 | tf_op jit(solution)/shard_map/pallas_call | solution.py:372
  18.4 0.0 all-to-all-done.1
  18.4 0.0 copy-start.1
  18.4 6.7 %all-to-all-start = ((bf16[8,32,1152]{2,1,0:T(8,128)(2,1)}), bf16[8,32,1152]{2,1,0:T(8,128)(2,1)}, u32[]{:S(2)}, u32[]{:S(2)}) async-start(bf16[8,32,1152]{2,1,0:T(8,128)(2,1)} %bitcast.19), calls=%async_computation | async-start | bytes 1179648 | tf_op jit(solution)/shard_map/all_to_all | solution.py:468
  25.1 1.5 %collective-permute-start.1 = (bf16[8,32,1152]{2,1,0:T(8,128)(2,1)S(1)}, bf16[8,32,1152]{2,1,0:T(8,128)(2,1)}, u32[]{:S(2)}, u32[]{:S(2)}) collective-permute-start(bf16[8,32,1152]{2,1,0:T(8,128)(2,1)S(1)} %all-to-all-done.1), channel_id=1, source_target_pairs={{0,8},{8,0},{16,24},{24,16},{32,40},{40,32},{48,56},{56,48},{64,72... | collective-permute-start | bytes 1769480 | tf_op jit(solution)/shard_map/ppermute | solution.py:471
  26.6 0.0 copy-done
  26.6 1.9 %convolution_convert_fusion = bf16[256,1152]{1,0:T(8,128)(2,1)} fusion(bf16[256,1152]{1,0:T(8,128)(2,1)S(1)} %bitcast.17, bf16[1152,1152]{1,0:T(8,128)(2,1)S(1)} %copy-done), kind=kOutput, calls=%fused_computation | convolution fusion | flops 679772160 | bytes 3833856 | tf_op jit(solution)/shard_map/dot_general | solution.py:39
  28.5 0.0 copy-done.1
  28.5 5.7 %all-to-all-done.hid_hbm = bf16[8,32,1152]{2,1,0:T(8,128)(2,1)} async-done(((bf16[8,32,1152]{2,1,0:T(8,128)(2,1)}), bf16[8,32,1152]{2,1,0:T(8,128)(2,1)}, u32[]{:S(2)}, u32[]{:S(2)}) %all-to-all-start) | async-done | bytes 589856 | tf_op jit(solution)/shard_map/all_to_all | solution.py:468
  34.2 12.5 %shard_map.96 = (bf16[8,32,1152]{2,1,0:T(8,128)(2,1)}, bf16[8,32,1152]{2,1,0:T(8,128)(2,1)}) custom-call(bf16[8,32,1152]{2,1,0:T(8,128)(2,1)} %all-to-all-done.hid_hbm, bf16[8,32,1152]{2,1,0:T(8,128)(2,1)} %bitcast.24, bf16[1152,3456]{1,0:T(8,128)(2,1)} %wq_hbm.4), custom_call_target="tpu_custom_call" | custom-call | flops 5435817984 | bytes 10321920 | tf_op jit(solution)/shard_map/pallas_call | solution.py:372
  46.7 3.8 %collective-permute-start = (bf16[8,32,1152]{2,1,0:T(8,128)(2,1)}, bf16[8,32,1152]{2,1,0:T(8,128)(2,1)}, u32[]{:S(2)}, u32[]{:S(2)}) collective-permute-start(bf16[8,32,1152]{2,1,0:T(8,128)(2,1)} %get-tuple-element.11), channel_id=1, source_target_pairs={{0,8},{8,0},{16,24},{24,16},{32,40},{40,32},{48,56},{56,48},{64,72... | collective-permute-start | bytes 1769480 | tf_op jit(solution)/shard_map/ppermute | solution.py:471
  50.5 4.2 %all-to-all-start.2 = ((bf16[8,32,1152]{2,1,0:T(8,128)(2,1)}), bf16[8,32,1152]{2,1,0:T(8,128)(2,1)}, u32[]{:S(2)}, u32[]{:S(2)}) async-start(bf16[8,32,1152]{2,1,0:T(8,128)(2,1)} %get-tuple-element.12), calls=%async_computation.2 | async-start | bytes 1179648 | tf_op jit(solution)/shard_map/all_to_all | solution.py:468
  54.7 0.0 collective-permute-done.1
  54.7 0.0 collective-permute-done
  54.7 4.8 %shard_map.97 = bf16[64,88,128]{2,1,0:T(8,128)(2,1)} custom-call(s32[1]{0:T(128)} %bitcast.core, bf16[256,1152]{1,0:T(8,128)(2,1)} %bitcast.22, bf16[256,1152]{1,0:T(8,128)(2,1)} %bitcast.7.other_mixed, bf16[256,1152]{1,0:T(8,128)(2,1)} %bitcast.18, bf16[256,1152]{1,0:T(8,128)(2,1)} %bitcast.8.other_og), custom_call_target="tpu_custom_call" | custom-call | flops 1358954496 | bytes 3801092 | tf_op jit(solution)/shard_map/pallas_call | solution.py:372
  59.6 5.9 %all-to-all-done.2 = bf16[8,32,1152]{2,1,0:T(8,128)(2,1)} async-done(((bf16[8,32,1152]{2,1,0:T(8,128)(2,1)}), bf16[8,32,1152]{2,1,0:T(8,128)(2,1)}, u32[]{:S(2)}, u32[]{:S(2)}) %all-to-all-start.2) | async-done | bytes 589856 | tf_op jit(solution)/shard_map/all_to_all | solution.py:468
  65.5 9.4 %all-to-all-start.3 = ((bf16[64,88,128]{2,1,0:T(8,128)(2,1)}), bf16[64,88,128]{2,1,0:T(8,128)(2,1)}, u32[]{:S(2)}, u32[]{:S(2)}) async-start(bf16[64,88,128]{2,1,0:T(8,128)(2,1)} %shard_map.97), calls=%async_computation.3 | async-start | bytes 2883584 | tf_op jit(solution)/shard_map/all_to_all | solution.py:492
  74.9 13.2 %shard_map.98 = bf16[256,1152]{1,0:T(8,128)(2,1)} custom-call(bf16[256,1152]{1,0:T(8,128)(2,1)} %bitcast.9.dhid_hbm, bf16[256,1152]{1,0:T(8,128)(2,1)} %get-tuple-element.14.mix_hbm, f32[1152]{0:T(1024)} %gt.3, bf16[256,1152]{1,0:T(8,128)(2,1)} %bitcast.16, bf16[256,3456]{1,0:T(8,128)(2,1)} %get-tuple-element.15.qkv_hbm, ...), custom_call_target="tpu_custom_call" | custom-call | flops 4756340736 | bytes 17441792 | tf_op jit(solution)/shard_map/pallas_call | solution.py:372
  88.1 7.3 %all-to-all-done.3.refs_1_ = bf16[64,88,128]{2,1,0:T(8,128)(2,1)} async-done(((bf16[64,88,128]{2,1,0:T(8,128)(2,1)}), bf16[64,88,128]{2,1,0:T(8,128)(2,1)}, u32[]{:S(2)}, u32[]{:S(2)}) %all-to-all-start.3) | async-done | bytes 1441824 | tf_op jit(solution)/shard_map/all_to_all | solution.py:492
  95.4 2.0 %shard_map.99 = f32[9,1152]{1,0:T(8,128)} custom-call(s32[1]{0:T(128)} %bitcast.12.refs_0_, bf16[64,88,128]{2,1,0:T(8,128)(2,1)} %all-to-all-done.3.refs_1_), custom_call_target="tpu_custom_call" | custom-call | flops 1000 | bytes 1483268 | tf_op jit(solution)/shard_map/pallas_call | solution.py:372
Async XLA Ops:
  0.6 26.0 %copy-start = (bf16[1152,1152]{1,0:T(8,128)(2,1)S(1)}, bf16[1152,1152]{1,0:T(8,128)(2,1)}, u32[]{:S(2)}) copy-start(bf16[1152,1152]{1,0:T(8,128)(2,1)} %param.15) | copy-start | bytes 7962628
  0.6 17.8 %all-to-all-start.1 = ((bf16[8,32,1152]{2,1,0:T(8,128)(2,1)}), bf16[8,32,1152]{2,1,0:T(8,128)(2,1)S(1)}, u32[]{:S(2)}, u32[]{:S(2)}) async-start(bf16[8,32,1152]{2,1,0:T(8,128)(2,1)} %bitcast.15), calls=%async_computation.1 | async-start | bytes 1179648 | tf_op jit(solution)/shard_map/all_to_all | solution.py:468
  18.4 10.1 %copy-start.1 = (bf16[8,32,1152]{2,1,0:T(8,128)(2,1)}, bf16[8,32,1152]{2,1,0:T(8,128)(2,1)S(1)}, u32[]{:S(2)}) copy-start(bf16[8,32,1152]{2,1,0:T(8,128)(2,1)S(1)} %all-to-all-done.1) | copy-start | bytes 1769476
  18.4 15.8 %all-to-all-start = ((bf16[8,32,1152]{2,1,0:T(8,128)(2,1)}), bf16[8,32,1152]{2,1,0:T(8,128)(2,1)}, u32[]{:S(2)}, u32[]{:S(2)}) async-start(bf16[8,32,1152]{2,1,0:T(8,128)(2,1)} %bitcast.19), calls=%async_computation | async-start | bytes 1179648 | tf_op jit(solution)/shard_map/all_to_all | solution.py:468
  25.1 29.6 %collective-permute-start.1 = (bf16[8,32,1152]{2,1,0:T(8,128)(2,1)S(1)}, bf16[8,32,1152]{2,1,0:T(8,128)(2,1)}, u32[]{:S(2)}, u32[]{:S(2)}) collective-permute-start(bf16[8,32,1152]{2,1,0:T(8,128)(2,1)S(1)} %all-to-all-done.1), channel_id=1, source_target_pairs={{0,8},{8,0},{16,24},{24,16},{32,40},{40,32},{48,56},{56,48},{64,72... | collective-permute-start | bytes 1769480 | tf_op jit(solution)/shard_map/ppermute | solution.py:471
  46.7 8.0 %collective-permute-start = (bf16[8,32,1152]{2,1,0:T(8,128)(2,1)}, bf16[8,32,1152]{2,1,0:T(8,128)(2,1)}, u32[]{:S(2)}, u32[]{:S(2)}) collective-permute-start(bf16[8,32,1152]{2,1,0:T(8,128)(2,1)} %get-tuple-element.11), channel_id=1, source_target_pairs={{0,8},{8,0},{16,24},{24,16},{32,40},{40,32},{48,56},{56,48},{64,72... | collective-permute-start | bytes 1769480 | tf_op jit(solution)/shard_map/ppermute | solution.py:471
  50.5 15.0 %all-to-all-start.2 = ((bf16[8,32,1152]{2,1,0:T(8,128)(2,1)}), bf16[8,32,1152]{2,1,0:T(8,128)(2,1)}, u32[]{:S(2)}, u32[]{:S(2)}) async-start(bf16[8,32,1152]{2,1,0:T(8,128)(2,1)} %get-tuple-element.12), calls=%async_computation.2 | async-start | bytes 1179648 | tf_op jit(solution)/shard_map/all_to_all | solution.py:468
  65.5 29.9 %all-to-all-start.3 = ((bf16[64,88,128]{2,1,0:T(8,128)(2,1)}), bf16[64,88,128]{2,1,0:T(8,128)(2,1)}, u32[]{:S(2)}, u32[]{:S(2)}) async-start(bf16[64,88,128]{2,1,0:T(8,128)(2,1)} %shard_map.97), calls=%async_computation.3 | async-start | bytes 2883584 | tf_op jit(solution)/shard_map/all_to_all | solution.py:492

commit v7 on v6

--- a/solution.py
+++ b/solution.py
@@ -89,13 +89,14 @@
 
 
 def all_heads(first, second):
-    waiting = None
+    waiting = []
     for h in range(HEADS):
-        values = first(h)
-        if waiting is not None:
-            second(h - 1, *waiting)
-        waiting = values
-    second(HEADS - 1, *waiting)
+        waiting.append((h, first(h)))
+        if len(waiting) > 2:
+            at, values = waiting.pop(0)
+            second(at, *values)
+    for at, values in waiting:
+        second(at, *values)
 
 
 def merge(slots, dst, base=0):
@@ -133,8 +134,8 @@
     return [fetch(src.at[:, p], dst.at[:, p], sems.at[i]) for i, p in enumerate(PIECES)]
 
 
-def spatial_forward(video, gs, gt, wq_hbm, wo_hbm, hid_hbm, mix_hbm, qkv_hbm, prob_hbm,
-                    wq, wo, hid, mix, stream, qkv, prob, slots, sems, out_sems):
+def spatial_forward(video, gs, gt, wq_hbm, wo_hbm, hid_hbm, mix_hbm, qkv_hbm,
+                    wq, wo, hid, mix, stream, qkv, slots, sems, out_sems):
     wq_copies = fetch_columns(wq_hbm, wq, sems)
     wo_copy = fetch(wo_hbm, wo, sems.at[4])
 
@@ -157,11 +158,9 @@
 
     def rest(h, scores, v):
         p = softmax_keys(scores).astype(BF)
-        prob[h] = p
         slots[h, :, : v.shape[1]] = tn(p, v).astype(BF)
 
     all_heads(head, rest)
-    prob_copy = fetch(prob, prob_hbm, out_sems.at[1])
     merge(slots, mix)
     mix_copy = fetch(mix, mix_hbm, out_sems.at[2])
     wo_copy.wait()
@@ -171,7 +170,7 @@
         centered, inv = row_stats(stream[rows, :])
         hid[rows, :] = (centered * inv * gt[...].reshape(1, D)).astype(BF)
 
-    copies = [qkv_copy, prob_copy, mix_copy]
+    copies = [qkv_copy, mix_copy]
     for i in range(2):
         row_blocks(second_norm, i * T // ROWS // 2, (i + 1) * T // ROWS // 2)
         rows = slice(i * T // 2, (i + 1) * T // 2)
@@ -252,12 +251,12 @@
         copy.wait()
 
 
-def spatial_backward(dhid_hbm, mix_hbm, gt, og_hbm, qkv_hbm, prob_hbm, video_hbm, gs,
-                     wo_hbm, wq_hbm, out, dhid, mix, stream, og, qkv, prob, video, wo, wq,
+def spatial_backward(dhid_hbm, mix_hbm, gt, og_hbm, qkv_hbm, video_hbm, gs,
+                     wo_hbm, wq_hbm, out, dhid, mix, stream, og, qkv, video, wo, wq,
                      sg, sgb, dmix, dqkv, dh, q_slots, k_slots, v_slots, sems):
     pairs = (
         (wo_hbm, wo), (mix_hbm, mix), (video_hbm, video), (dhid_hbm, dhid), (og_hbm, og),
-        (qkv_hbm, qkv), (prob_hbm, prob), (wq_hbm, wq),
+        (qkv_hbm, qkv), (wq_hbm, wq),
     )
     copies = [fetch(src, dst, sems.at[i]) for i, (src, dst) in enumerate(pairs)]
     for copy in copies[:3]:
@@ -275,7 +274,6 @@
     row_blocks(stream_grad)
     dmix[...] = nt(sgb[...], wo[...]).astype(BF)
     copies[5].wait()
-    copies[6].wait()
 
     def head(h):
         low, width, inside = window(h)
@@ -284,17 +282,18 @@
         k = qkv[:, ks] * inside
         v = qkv[:, vs]
         do = dmix[:, qs] * inside
-        return nt(v, do), q, k, do
-
-    def rest(h, prob_grad, q, k, do):
-        pb = prob[h]
-        ds = score_grad(pb.astype(F32), prob_grad)
+        return nt(k, q), nt(v, do), q, k, do
+
+    def rest(h, scores, prob_grad, q, k, do):
+        p = softmax_keys(scores)
+        pb = p.astype(BF)
+        ds = score_grad(p, prob_grad)
         v_slots[h, :, : q.shape[1]] = nn(pb, do).astype(BF)
         k_slots[h, :, : q.shape[1]] = nn(ds, q).astype(BF)
         q_slots[h, :, : q.shape[1]] = tn(ds, k).astype(BF)
 
     all_heads(head, rest)
-    copies[7].wait()
+    copies[6].wait()
     dh[...] = project_back((q_slots, k_slots, v_slots), dqkv, wq).astype(BF)
 
     def video_grad(rows):
@@ -382,19 +381,19 @@
 UNIT = 2 * T * D * D
 WIDE, SQUARE = VMEM((D, 3 * D), BF), VMEM((D, D), BF)
 TOK, TOK3, TOKF = VMEM((T, D), BF), VMEM((T, 3 * D), BF), VMEM((T, D), F32)
-PROB, SLOTS = VMEM((HEADS, T, T), BF), VMEM((HEADS, T, WIN), BF)
+SLOTS = VMEM((HEADS, T, WIN), BF)
 DMA = pltpu.SemaphoreType.DMA
 
 
 def run_spatial_forward(clip, gs, gt, wq, wo):
     return call(
         spatial_forward,
-        [((T, D), BF), ((T, D), BF), ((T, 3 * D), BF), ((HEADS, T, T), BF)],
+        [((T, D), BF), ((T, D), BF), ((T, 3 * D), BF)],
         (clip, gs, gt, wq, wo),
-        [WIDE, SQUARE, TOK, TOK, TOKF, TOK3, PROB, SLOTS, DMA((5,)), DMA((5,))],
+        [WIDE, SQUARE, TOK, TOK, TOKF, TOK3, SLOTS, DMA((5,)), DMA((5,))],
         5 * UNIT,
         [VMEM, VMEM, VMEM, ANY, ANY],
-        [ANY, ANY, ANY, ANY],
+        [ANY, ANY, ANY],
     )
 
 
@@ -411,15 +410,15 @@
     )
 
 
-def run_spatial_backward(dhid, mix, gt, og, qkv, prob, clip, gs, wo, wq):
+def run_spatial_backward(dhid, mix, gt, og, qkv, clip, gs, wo, wq):
     return call(
         spatial_backward,
         [((T, D), BF)],
-        (dhid, mix, gt, og, qkv, prob, clip, gs, wo, wq),
-        [TOK, TOK, TOKF, TOK, TOK3, PROB, TOK, SQUARE, WIDE, TOKF, TOK, TOK, TOK3, TOK,
-         SLOTS, SLOTS, SLOTS, DMA((8,))],
+        (dhid, mix, gt, og, qkv, clip, gs, wo, wq),
+        [TOK, TOK, TOKF, TOK, TOK3, TOK, SQUARE, WIDE, TOKF, TOK, TOK, TOK3, TOK,
+         SLOTS, SLOTS, SLOTS, DMA((7,))],
         7 * UNIT,
-        [ANY, ANY, VMEM, ANY, ANY, ANY, ANY, VMEM, ANY, ANY],
+        [ANY, ANY, VMEM, ANY, ANY, ANY, VMEM, ANY, ANY],
     )[0]
 
 
@@ -472,7 +471,7 @@
 
     og_pos = exchange(og)
     other_og = swap(og_pos)
-    hid, mix, qkv, prob = run_spatial_forward(
+    hid, mix, qkv = run_spatial_forward(
         clip, gain_spatial, gain_temporal, w_spatial_qkv, w_spatial_out
     )
     hid_pos = exchange(hid)
@@ -493,7 +492,7 @@
         chunks, ("dp", "seq"), 0, 0, axis_index_groups=owners, tiled=True
     )
     video_grad = run_spatial_backward(
-        dhid, mix, gain_temporal, og, qkv, prob, clip, gain_spatial,
+        dhid, mix, gain_temporal, og, qkv, clip, gain_spatial,
         w_spatial_out, w_spatial_qkv,
     )
     owner = lax.axis_index("seq").reshape(1)

time: 98.7 us -> 98.2 us (level)
  waiting for transfers between devices: 18.9 us -> 17.9 us
    all_to_all x1, waiting for transfers between devices: 7.28 us -> 6.12 us  [per_device(): lax.all_to_all(chunks, ('dp', 'seq'), 0, 0, axis_index_groups=owners, til...]
  transfers between devices with their start and end apart: 6 -> 6, of which waited for: 3 -> 4; matrix products, arithmetic and copies ran while one was open for 2% -> 2% of each run, Pallas kernels for 42% -> 42%
where the time goes in v7:
time: 98.2 us; the launch traced here: 97.1 us
  Pallas kernels  43.2 us (44%)
  starting transfers between devices  33.3 us (34%)
  waiting for transfers between devices  17.9 us (18%)
  matrix products  1.85 us (2%)
    pallas_call x5, Pallas kernels, call(): pl.pallas_call(fn, out_shape=[jax.ShapeDtypeStruct(s, d) for s, d in outs...  43.2 us
    all_to_all x3, starting transfers between devices, exchange(): return lax.all_to_all(x.reshape(SEQ, POS, D), 'seq', 0, 0, tiled=True)  18.6 us
    all_to_all x3, waiting for transfers between devices, exchange(): return lax.all_to_all(x.reshape(SEQ, POS, D), 'seq', 0, 0, tiled=True)  11.8 us
    all_to_all x1, starting transfers between devices, per_device(): lax.all_to_all(chunks, ('dp', 'seq'), 0, 0, axis_index_groups=owners, til...  9.38 us
    all_to_all x1, waiting for transfers between devices, per_device(): lax.all_to_all(chunks, ('dp', 'seq'), 0, 0, axis_index_groups=owners, til...  6.12 us
    ppermute x2, starting transfers between devices, swap(): return lax.ppermute(x, 'dp', [(i, i ^ 1) for i in range(DP)])  5.35 us
  transfers between devices with their start and end apart: 6, of which 4 were waited for; matrix products, arithmetic and copies ran while one was open for 2% of the time, Pallas kernels for 42%

profile of v7, /device:TPU:1, one launch (start us, length us, event | category | flops | bytes accessed | tf_op | source)
XLA Modules:
  0.0 97.1 jit_solution(3439359145253314917)
XLA Ops:
  0.6 0.0 copy-start
  0.6 7.7 %all-to-all-start.1 = ((bf16[8,32,1152]{2,1,0:T(8,128)(2,1)}), bf16[8,32,1152]{2,1,0:T(8,128)(2,1)S(1)}, u32[]{:S(2)}, u32[]{:S(2)}) async-start(bf16[8,32,1152]{2,1,0:T(8,128)(2,1)} %bitcast.15), calls=%async_computation.1 | async-start | bytes 1179648 | tf_op jit(solution)/shard_map/all_to_all | solution.py:467
  8.4 9.8 %shard_map.95 = (bf16[256,1152]{1,0:T(8,128)(2,1)}, bf16[256,1152]{1,0:T(8,128)(2,1)}, bf16[256,3456]{1,0:T(8,128)(2,1)}) custom-call(bf16[256,1152]{1,0:T(8,128)(2,1)} %bitcast.20, f32[1152]{0:T(1024)} %gs.3, f32[1152]{0:T(1024)} %gt.3, bf16[1152,3456]{1,0:T(8,128)(2,1)} %wq_hbm.5, bf16[1152,1152]{1,0:T(8,128)(2,1)} %wo_hbm.3), custom_call_target="tpu_custom_call" | custom-call | flops 3397386240 | bytes 14164992 | tf_op jit(solution)/shard_map/pallas_call | solution.py:371
  18.2 0.1 all-to-all-done.1
  18.2 0.0 copy-start.1
  18.2 6.6 %all-to-all-start = ((bf16[8,32,1152]{2,1,0:T(8,128)(2,1)}), bf16[8,32,1152]{2,1,0:T(8,128)(2,1)}, u32[]{:S(2)}, u32[]{:S(2)}) async-start(bf16[8,32,1152]{2,1,0:T(8,128)(2,1)} %bitcast.19), calls=%async_computation | async-start | bytes 1179648 | tf_op jit(solution)/shard_map/all_to_all | solution.py:467
  24.9 1.5 %collective-permute-start.1 = (bf16[8,32,1152]{2,1,0:T(8,128)(2,1)S(1)}, bf16[8,32,1152]{2,1,0:T(8,128)(2,1)}, u32[]{:S(2)}, u32[]{:S(2)}) collective-permute-start(bf16[8,32,1152]{2,1,0:T(8,128)(2,1)S(1)} %all-to-all-done.1), channel_id=1, source_target_pairs={{0,8},{8,0},{16,24},{24,16},{32,40},{40,32},{48,56},{56,48},{64,72... | collective-permute-start | bytes 1769480 | tf_op jit(solution)/shard_map/ppermute | solution.py:470
  26.4 0.0 copy-done
  26.4 1.9 %convolution_convert_fusion = bf16[256,1152]{1,0:T(8,128)(2,1)} fusion(bf16[256,1152]{1,0:T(8,128)(2,1)S(1)} %bitcast.17, bf16[1152,1152]{1,0:T(8,128)(2,1)S(1)} %copy-done), kind=kOutput, calls=%fused_computation | convolution fusion | flops 679772160 | bytes 3833856 | tf_op jit(solution)/shard_map/dot_general | solution.py:39
  28.2 0.0 copy-done.1
  28.2 5.7 %all-to-all-done.hid_hbm = bf16[8,32,1152]{2,1,0:T(8,128)(2,1)} async-done(((bf16[8,32,1152]{2,1,0:T(8,128)(2,1)}), bf16[8,32,1152]{2,1,0:T(8,128)(2,1)}, u32[]{:S(2)}, u32[]{:S(2)}) %all-to-all-start) | async-done | bytes 589856 | tf_op jit(solution)/shard_map/all_to_all | solution.py:467
  34.0 12.2 %shard_map.96 = (bf16[8,32,1152]{2,1,0:T(8,128)(2,1)}, bf16[8,32,1152]{2,1,0:T(8,128)(2,1)}) custom-call(bf16[8,32,1152]{2,1,0:T(8,128)(2,1)} %all-to-all-done.hid_hbm, bf16[8,32,1152]{2,1,0:T(8,128)(2,1)} %bitcast.24, bf16[1152,3456]{1,0:T(8,128)(2,1)} %wq_hbm.4), custom_call_target="tpu_custom_call" | custom-call | flops 5435817984 | bytes 10321920 | tf_op jit(solution)/shard_map/pallas_call | solution.py:371
  46.2 3.8 %collective-permute-start = (bf16[8,32,1152]{2,1,0:T(8,128)(2,1)}, bf16[8,32,1152]{2,1,0:T(8,128)(2,1)}, u32[]{:S(2)}, u32[]{:S(2)}) collective-permute-start(bf16[8,32,1152]{2,1,0:T(8,128)(2,1)} %get-tuple-element.10), channel_id=1, source_target_pairs={{0,8},{8,0},{16,24},{24,16},{32,40},{40,32},{48,56},{56,48},{64,72... | collective-permute-start | bytes 1769480 | tf_op jit(solution)/shard_map/ppermute | solution.py:470
  50.0 4.2 %all-to-all-start.2 = ((bf16[8,32,1152]{2,1,0:T(8,128)(2,1)}), bf16[8,32,1152]{2,1,0:T(8,128)(2,1)}, u32[]{:S(2)}, u32[]{:S(2)}) async-start(bf16[8,32,1152]{2,1,0:T(8,128)(2,1)} %get-tuple-element.11), calls=%async_computation.2 | async-start | bytes 1179648 | tf_op jit(solution)/shard_map/all_to_all | solution.py:467
  54.2 0.0 collective-permute-done.1
  54.2 0.0 collective-permute-done
  54.2 4.8 %shard_map.97 = bf16[64,88,128]{2,1,0:T(8,128)(2,1)} custom-call(s32[1]{0:T(128)} %bitcast.core, bf16[256,1152]{1,0:T(8,128)(2,1)} %bitcast.22, bf16[256,1152]{1,0:T(8,128)(2,1)} %bitcast.7.other_mixed, bf16[256,1152]{1,0:T(8,128)(2,1)} %bitcast.18, bf16[256,1152]{1,0:T(8,128)(2,1)} %bitcast.8.other_og), custom_call_target="tpu_custom_call" | custom-call | flops 1358954496 | bytes 3801092 | tf_op jit(solution)/shard_map/pallas_call | solution.py:371
  59.0 6.0 %all-to-all-done.2 = bf16[8,32,1152]{2,1,0:T(8,128)(2,1)} async-done(((bf16[8,32,1152]{2,1,0:T(8,128)(2,1)}), bf16[8,32,1152]{2,1,0:T(8,128)(2,1)}, u32[]{:S(2)}, u32[]{:S(2)}) %all-to-all-start.2) | async-done | bytes 589856 | tf_op jit(solution)/shard_map/all_to_all | solution.py:467
  65.0 9.4 %all-to-all-start.3 = ((bf16[64,88,128]{2,1,0:T(8,128)(2,1)}), bf16[64,88,128]{2,1,0:T(8,128)(2,1)}, u32[]{:S(2)}, u32[]{:S(2)}) async-start(bf16[64,88,128]{2,1,0:T(8,128)(2,1)} %shard_map.97), calls=%async_computation.3 | async-start | bytes 2883584 | tf_op jit(solution)/shard_map/all_to_all | solution.py:491
  74.4 14.4 %shard_map.98 = bf16[256,1152]{1,0:T(8,128)(2,1)} custom-call(bf16[256,1152]{1,0:T(8,128)(2,1)} %bitcast.9.dhid_hbm, bf16[256,1152]{1,0:T(8,128)(2,1)} %get-tuple-element.13.mix_hbm, f32[1152]{0:T(1024)} %gt.3, bf16[256,1152]{1,0:T(8,128)(2,1)} %bitcast.16, bf16[256,3456]{1,0:T(8,128)(2,1)} %get-tuple-element.14.qkv_hbm, bf16[256,1152]{1,0:T(8,128)(2,1)} %bitcast.21, ...), custom_call_target="tpu_custom_call" | custom-call | flops 4756340736 | bytes 15344640 | tf_op jit(solution)/shard_map/pallas_call | solution.py:371
  88.8 6.1 %all-to-all-done.3.refs_1_ = bf16[64,88,128]{2,1,0:T(8,128)(2,1)} async-done(((bf16[64,88,128]{2,1,0:T(8,128)(2,1)}), bf16[64,88,128]{2,1,0:T(8,128)(2,1)}, u32[]{:S(2)}, u32[]{:S(2)}) %all-to-all-start.3) | async-done | bytes 1441824 | tf_op jit(solution)/shard_map/all_to_all | solution.py:491
  94.9 2.0 %shard_map.99 = f32[9,1152]{1,0:T(8,128)} custom-call(s32[1]{0:T(128)} %bitcast.12.refs_0_, bf16[64,88,128]{2,1,0:T(8,128)(2,1)} %all-to-all-done.3.refs_1_), custom_call_target="tpu_custom_call" | custom-call | flops 1000 | bytes 1483268 | tf_op jit(solution)/shard_map/pallas_call | solution.py:371
Async XLA Ops:
  0.6 25.8 %copy-start = (bf16[1152,1152]{1,0:T(8,128)(2,1)S(1)}, bf16[1152,1152]{1,0:T(8,128)(2,1)}, u32[]{:S(2)}) copy-start(bf16[1152,1152]{1,0:T(8,128)(2,1)} %param.15) | copy-start | bytes 7962628
  0.6 17.6 %all-to-all-start.1 = ((bf16[8,32,1152]{2,1,0:T(8,128)(2,1)}), bf16[8,32,1152]{2,1,0:T(8,128)(2,1)S(1)}, u32[]{:S(2)}, u32[]{:S(2)}) async-start(bf16[8,32,1152]{2,1,0:T(8,128)(2,1)} %bitcast.15), calls=%async_computation.1 | async-start | bytes 1179648 | tf_op jit(solution)/shard_map/all_to_all | solution.py:467
  18.2 10.0 %copy-start.1 = (bf16[8,32,1152]{2,1,0:T(8,128)(2,1)}, bf16[8,32,1152]{2,1,0:T(8,128)(2,1)S(1)}, u32[]{:S(2)}) copy-start(bf16[8,32,1152]{2,1,0:T(8,128)(2,1)S(1)} %all-to-all-done.1) | copy-start | bytes 1769476
  18.2 15.7 %all-to-all-start = ((bf16[8,32,1152]{2,1,0:T(8,128)(2,1)}), bf16[8,32,1152]{2,1,0:T(8,128)(2,1)}, u32[]{:S(2)}, u32[]{:S(2)}) async-start(bf16[8,32,1152]{2,1,0:T(8,128)(2,1)} %bitcast.19), calls=%async_computation | async-start | bytes 1179648 | tf_op jit(solution)/shard_map/all_to_all | solution.py:467
  24.9 29.4 %collective-permute-start.1 = (bf16[8,32,1152]{2,1,0:T(8,128)(2,1)S(1)}, bf16[8,32,1152]{2,1,0:T(8,128)(2,1)}, u32[]{:S(2)}, u32[]{:S(2)}) collective-permute-start(bf16[8,32,1152]{2,1,0:T(8,128)(2,1)S(1)} %all-to-all-done.1), channel_id=1, source_target_pairs={{0,8},{8,0},{16,24},{24,16},{32,40},{40,32},{48,56},{56,48},{64,72... | collective-permute-start | bytes 1769480 | tf_op jit(solution)/shard_map/ppermute | solution.py:470
  46.2 8.1 %collective-permute-start = (bf16[8,32,1152]{2,1,0:T(8,128)(2,1)}, bf16[8,32,1152]{2,1,0:T(8,128)(2,1)}, u32[]{:S(2)}, u32[]{:S(2)}) collective-permute-start(bf16[8,32,1152]{2,1,0:T(8,128)(2,1)} %get-tuple-element.10), channel_id=1, source_target_pairs={{0,8},{8,0},{16,24},{24,16},{32,40},{40,32},{48,56},{56,48},{64,72... | collective-permute-start | bytes 1769480 | tf_op jit(solution)/shard_map/ppermute | solution.py:470
  50.0 15.0 %all-to-all-start.2 = ((bf16[8,32,1152]{2,1,0:T(8,128)(2,1)}), bf16[8,32,1152]{2,1,0:T(8,128)(2,1)}, u32[]{:S(2)}, u32[]{:S(2)}) async-start(bf16[8,32,1152]{2,1,0:T(8,128)(2,1)} %get-tuple-element.11), calls=%async_computation.2 | async-start | bytes 1179648 | tf_op jit(solution)/shard_map/all_to_all | solution.py:467
  65.0 29.9 %all-to-all-start.3 = ((bf16[64,88,128]{2,1,0:T(8,128)(2,1)}), bf16[64,88,128]{2,1,0:T(8,128)(2,1)}, u32[]{:S(2)}, u32[]{:S(2)}) async-start(bf16[64,88,128]{2,1,0:T(8,128)(2,1)} %shard_map.97), calls=%async_computation.3 | async-start | bytes 2883584 | tf_op jit(solution)/shard_map/all_to_all | solution.py:491
